TPU v7x, 128 devices: a whole 4x4x4 slice. The times are simulated.
128 devices in a mesh: calib: 32 (over z_lo, y, x), peak: 4 (over z_hi, core).
Axes of the slice: x: 4, y: 4, z: 4 (z_hi: 2, z_lo: 2; z = z_hi * 2 + z_lo), core: 2. Of those that a mesh axis runs over, the one named last changes fastest.
Arguments:
- raw: int32 [8, 32, 512, 1024], P('peak', None, 'calib'), may hold values from 256 to 8184, as said below
- pedestal: float32 [3, 32, 512, 1024], P(None, None, 'calib'), may hold values from 594 to 1406
- gain: bfloat16 [3, 32, 512, 1024], P(None, None, 'calib'), may hold values from 16 to 64
- good: int32 [32, 512, 1024], P(None, 'calib'), may hold values from 0 to 1, as said below
- bounds: int32 [32, 7], replicated, may hold values from 1 to 1023, as said below
- table: int32 [32], replicated, may hold values from 0 to 31, as said below
Outputs:
- snr: bfloat16 [8, 32, 512, 1024], P(None, 'calib', None, 'peak')
- curvature: bfloat16 [8, 32, 512, 1024], P(None, 'calib', None, 'peak')
Inputs may be any that keep to these rules, and one draw needn't show every extreme that they name: raw // 2048 is the gain code (0, 1 or 3) and raw % 2048 the ADC count, which lies between 256 and 2040. `good`: some module rows are bad in every column. `bounds`: strictly increasing along the last dimension. `table`: each slot is named once.
All inputs are finite; a program needn't handle non-finite values.
Results may differ from a plain program's by a relative error of at most 0.0007.
The roundings to bfloat16 on the way count: a program that leaves them out, or rounds other values in their place, can miss the bound.
Values may be sent and summed in bfloat16 or wider, within the bound.
A program may use at most 128 MiB of HBM per device.

v0:
```python
import jax
import jax.numpy as jnp
from jax import lax
from jax.sharding import PartitionSpec as P
from jax.experimental import pallas as pl
from jax.experimental.pallas import tpu as pltpu

COLS = 1024
BANDS = 8
SLOT_C = 4
CYCLES = 32
CYCLE_W = 64


precise_variant = lax.Precision.HIGHEST


def padded_2(block, sides, width):
    for axis, dim in sides:
        count = lax.axis_size(axis)
        forward = [(i, i + 1) for i in range(count - 1)]
        backward = [(target, source) for source, target in forward]
        low = lax.ppermute(
            lax.slice_in_dim(block, block.shape[dim] - width, None, axis=dim), axis, forward
        )
        high = lax.ppermute(lax.slice_in_dim(block, 0, width, axis=dim), axis, backward)
        block = jnp.concatenate([low, block, high], axis=dim)
    return block


def cycle_index(dist):
    levels = jnp.arange(1, CYCLES, dtype=jnp.int32)
    lows = (2 * CYCLE_W * levels) ** 2
    return jnp.sum((dist[..., None] >= lows).astype(jnp.int32), axis=-1)


def cycle_onehot(slot, row_pos, col_pos, mrows, slot_rows):
    ypos = slot // SLOT_C * mrows + row_pos
    xpos = slot % SLOT_C * COLS + col_pos
    dy_two = 2 * ypos + 1 - slot_rows * mrows
    dx_two = 2 * xpos + 1 - SLOT_C * COLS
    dist = dy_two[:, None] * dy_two[:, None] + dx_two[None, :] * dx_two[None, :]
    levels = jnp.arange(CYCLES, dtype=jnp.int32)
    lows = (2 * CYCLE_W * levels) ** 2
    cycle = jnp.sum((dist[None] >= lows[:, None, None]).astype(jnp.int32), axis=0) - 1
    hits = (cycle[None] == levels[:, None, None]).astype(jnp.float32)
    return hits.reshape(CYCLES, -1)


def calibrate(raw, pedestal, gain, good, bounds):
    code = raw // 2048
    counts_adc = (raw % 2048).astype(jnp.float32)
    base = jnp.where(code == 0, pedestal[0], jnp.where(code == 1, pedestal[1], pedestal[2]))
    gain_factor = gain.astype(jnp.float32)
    scale = jnp.where(
        code == 0, gain_factor[0], jnp.where(code == 1, gain_factor[1], gain_factor[2])
    )
    weight_factor = good.astype(jnp.float32)
    energy = weight_factor * (counts_adc - base) / scale
    columns = jnp.arange(raw.shape[-1], dtype=jnp.int32)
    band = jnp.sum((columns[None, :, None] >= bounds[:, None, :]).astype(jnp.int32), axis=2)
    member_entry = (band[:, :, None] == jnp.arange(BANDS, dtype=jnp.int32)[None, None, :]).astype(
        jnp.float32
    )
    totals = jnp.einsum("fmrc,mcb->fmrb", energy, member_entry, precision=precise_variant)
    present_flag = jnp.einsum(
        "tlg,tgd->tld", weight_factor, member_entry, precision=precise_variant
    )
    level = totals / jnp.maximum(present_flag, 1.0)
    spread = jnp.einsum("fmrb,mcb->fmrc", level, member_entry, precision=precise_variant)
    return (weight_factor * (energy - spread)).astype(jnp.bfloat16)


def calibrate_kernel(table_ref, bounds_ref, raw_ref, ped_ref, gain_ref, good_ref, out_ref):
    module = pl.program_id(0)
    raw = raw_ref[...]
    code = raw // 2048
    counts_adc = (raw % 2048).astype(jnp.float32)
    base = jnp.where(code == 0, ped_ref[0], jnp.where(code == 1, ped_ref[1], ped_ref[2]))
    scale = jnp.where(
        code == 0,
        gain_ref[0].astype(jnp.float32),
        jnp.where(code == 1, gain_ref[1].astype(jnp.float32), gain_ref[2].astype(jnp.float32)),
    )
    weight_factor = good_ref[...].astype(jnp.float32)
    energy = weight_factor * (counts_adc - base) / scale
    cols = raw.shape[-1]
    columns = lax.broadcasted_iota(jnp.int32, (1, cols), 1)
    band = jnp.zeros((1, cols), jnp.int32)
    for j in range(BANDS - 1):
        band = band + (columns >= bounds_ref[module * (BANDS - 1) + j]).astype(jnp.int32)
    spread = jnp.zeros(energy.shape, jnp.float32)
    for b in range(BANDS):
        member = band == b
        totals = jnp.sum(jnp.where(member, energy, 0.0), axis=-1, keepdims=True)
        present = jnp.sum(jnp.where(member, weight_factor, 0.0), axis=-1, keepdims=True)
        spread = jnp.where(member, totals / jnp.maximum(present, 1.0), spread)
    corrected = (weight_factor * (energy - spread)).astype(jnp.bfloat16)
    quarters = out_ref.shape[0]
    width = cols // quarters
    for q in range(quarters):
        out_ref[q] = corrected[:, :, q * width : (q + 1) * width]


def calibrate_send(raw, pedestal, gain, good, bounds, table, n_peak):
    frame_dev, mods, row_dev, cols = raw.shape
    width = cols // n_peak
    grid_spec = pltpu.PrefetchScalarGridSpec(
        num_scalar_prefetch=2,
        grid=(mods,),
        in_specs=[
            pl.BlockSpec((frame_dev, None, row_dev, cols), lambda m, t, b: (0, m, 0, 0)),
            pl.BlockSpec((3, None, row_dev, cols), lambda m, t, b: (0, m, 0, 0)),
            pl.BlockSpec((3, None, row_dev, cols), lambda m, t, b: (0, m, 0, 0)),
            pl.BlockSpec((None, row_dev, cols), lambda m, t, b: (m, 0, 0)),
        ],
        out_specs=pl.BlockSpec(
            (None, n_peak, frame_dev, row_dev, width), lambda m, t, b: (t[m], 0, 0, 0, 0)
        ),
    )
    return pl.pallas_call(
        calibrate_kernel,
        grid_spec=grid_spec,
        out_shape=jax.ShapeDtypeStruct((mods, n_peak, frame_dev, row_dev, width), jnp.bfloat16),
    )(table, bounds.reshape(-1), raw, pedestal, gain, good)


def laplace(padded):
    center = padded[..., 1:-1, 1:-1]
    return (
        4.0 * center
        - padded[..., :-2, 1:-1]
        - padded[..., 2:, 1:-1]
        - padded[..., 1:-1, :-2]
        - padded[..., 1:-1, 2:]
    )


def local_present(good, table, row_src, mrows, slot_rows):
    n_peak = lax.axis_size("peak")
    width = good.shape[2] // n_peak
    start = lax.axis_index("peak") * width
    part = lax.dynamic_slice_in_dim(good, start, width, axis=2)
    col = start + jnp.arange(width, dtype=jnp.int32)
    ypos = (table // SLOT_C)[:, None] * mrows + row_src[None, :]
    xpos = (table % SLOT_C)[:, None] * COLS + col[None, :]
    dy_two = 2 * ypos + 1 - slot_rows * mrows
    dx_two = 2 * xpos + 1 - SLOT_C * COLS
    dist = dy_two[:, :, None] * dy_two[:, :, None] + dx_two[:, None, :] * dx_two[:, None, :]
    cycle = cycle_index(dist)
    levels = jnp.arange(CYCLES, dtype=jnp.int32)
    hit = jnp.where(cycle[..., None] == levels, part[..., None], 0)
    return jnp.sum(hit, axis=(0, 1, 2)).astype(jnp.float32)


def gather_sum_kernel(n_calib, n_peak, x_ref, o_ref, buf, send_sem, recv_sem):
    total = n_calib * n_peak
    me = lax.axis_index("calib") * n_peak + lax.axis_index("peak")
    buf[total - 1] = x_ref[...]
    barrier = pltpu.get_barrier_semaphore()

    def peer_of(step):
        peer = lax.rem(me + step, total)
        return (peer // n_peak, peer % n_peak)

    def greet(step, carry):
        pl.semaphore_signal(
            barrier, inc=1, device_id=peer_of(step), device_id_type=pl.DeviceIdType.MESH
        )
        return carry

    lax.fori_loop(1, total, greet, 0)
    pl.semaphore_wait(barrier, total - 1)

    def send(step, carry):
        pltpu.make_async_remote_copy(
            src_ref=x_ref,
            dst_ref=buf.at[total - 1 - step],
            send_sem=send_sem,
            recv_sem=recv_sem,
            device_id=peer_of(step),
            device_id_type=pl.DeviceIdType.MESH,
        ).start()
        return carry

    lax.fori_loop(1, total, send, 0)
    every = pltpu.make_async_remote_copy(
        src_ref=buf.at[pl.ds(0, total - 1)],
        dst_ref=buf.at[pl.ds(0, total - 1)],
        send_sem=send_sem,
        recv_sem=recv_sem,
        device_id=peer_of(1),
        device_id_type=pl.DeviceIdType.MESH,
    )
    every.wait_send()
    every.wait_recv()

    def add(source, acc):
        return acc + buf[lax.rem(source - me - 1 + 2 * total, total)]

    o_ref[...] = lax.fori_loop(0, total, add, jnp.zeros(x_ref.shape, x_ref.dtype))


def gather_sum(x):
    n_calib = lax.axis_size("calib")
    n_peak = lax.axis_size("peak")
    return pl.pallas_call(
        lambda *refs: gather_sum_kernel(n_calib, n_peak, *refs),
        out_shape=jax.ShapeDtypeStruct(x.shape, x.dtype),
        in_specs=[pl.BlockSpec(memory_space=pltpu.VMEM)],
        out_specs=pl.BlockSpec(memory_space=pltpu.VMEM),
        scratch_shapes=[
            pltpu.VMEM((n_calib * n_peak,) + x.shape, x.dtype),
            pltpu.SemaphoreType.DMA,
            pltpu.SemaphoreType.DMA,
        ],
        compiler_params=pltpu.CompilerParams(collective_id=0, has_side_effects=True),
    )(x)


def cycle_stats(first, second, present_flag):
    cycle_average = first / present_flag[None, :]
    cycle_rms = jnp.sqrt(second / present_flag[None, :] + 1e-06)
    return (cycle_average, cycle_rms)


def body(raw, pedestal, gain, good, bounds, table):
    frame_dev, mods, row_dev, cols = raw.shape
    n_calib = lax.axis_size("calib")
    n_peak = lax.axis_size("peak")
    mrows = row_dev * n_calib
    slot_rows = mods // SLOT_C
    width_here = cols // n_peak
    frames_all = frame_dev * n_peak
    row_src = lax.axis_index("calib") * row_dev + jnp.arange(row_dev, dtype=jnp.int32)
    send = calibrate_send(raw, pedestal, gain, good, bounds, table, n_peak)
    send = send.reshape(mods * n_peak, frame_dev, row_dev, width_here)
    present_part = local_present(good, table, row_src, mrows, slot_rows)
    got = lax.all_to_all(send, ("calib", "peak"), 0, 0, tiled=True)
    got = got.reshape(n_calib, n_peak, frame_dev, row_dev, width_here)
    frame = jnp.transpose(got, (1, 2, 0, 3, 4)).reshape(frames_all, mrows, width_here)
    slot = lax.axis_index("calib")
    col_dst = lax.axis_index("peak") * width_here + jnp.arange(width_here, dtype=jnp.int32)
    hits = cycle_onehot(slot, jnp.arange(mrows, dtype=jnp.int32), col_dst, mrows, slot_rows)
    hits = hits.astype(jnp.bfloat16)
    pixels = frame.reshape(frames_all, -1)
    values = pixels.astype(jnp.float32)
    square = values * values
    square_top = lax.reduce_precision(square, exponent_bits=8, mantissa_bits=7)
    square_hi = square_top.astype(jnp.bfloat16)
    square_lo = (square - square_top).astype(jnp.bfloat16)
    stacked = jnp.concatenate([pixels, square_hi, square_lo], axis=0)
    sums = jnp.einsum("fp,kp->fk", stacked, hits, preferred_element_type=jnp.float32)
    first = sums[:frames_all]
    second = sums[frames_all : 2 * frames_all] + sums[2 * frames_all :]
    lanes = 128
    packed = jnp.concatenate(
        [
            first,
            second,
            jnp.zeros((frames_all, CYCLES), jnp.float32).at[0].set(present_part),
            jnp.zeros((frames_all, lanes - 3 * CYCLES), jnp.float32),
        ],
        axis=1,
    )
    summed = gather_sum(packed)
    first = summed[:, :CYCLES]
    second = summed[:, CYCLES : 2 * CYCLES]
    present_flag = summed[0, 2 * CYCLES : 3 * CYCLES]
    cycle_average, cycle_rms = cycle_stats(first, second, present_flag)
    table_f32 = jnp.concatenate([cycle_average, cycle_rms], axis=0)
    top_1 = lax.reduce_precision(table_f32, exponent_bits=8, mantissa_bits=7)
    rest = table_f32 - top_1
    top_2 = lax.reduce_precision(rest, exponent_bits=8, mantissa_bits=7)
    piece_1 = top_1.astype(jnp.bfloat16)
    piece_2 = top_2.astype(jnp.bfloat16)
    piece_3 = (rest - top_2).astype(jnp.bfloat16)
    pieces = jnp.concatenate([piece_1, piece_2, piece_3], axis=1)
    hits_3 = jnp.concatenate([hits, hits, hits], axis=0)
    lookup = jnp.einsum("fk,kp->fp", pieces, hits_3, preferred_element_type=jnp.float32)
    pixel_mean = lookup[:frames_all]
    pixel_rms = lookup[frames_all:]
    score = ((values - pixel_mean) / pixel_rms).reshape(frames_all, mrows, width_here)
    padded = padded_2(score, (("peak", 2),), 1)
    padded = jnp.pad(padded, ((0, 0), (1, 1), (0, 0)))
    bent = laplace(padded)
    return (score.astype(jnp.bfloat16)[:, None], bent.astype(jnp.bfloat16)[:, None])


def solution(mesh):
    in_specs = (
        P("peak", None, "calib", None),
        P(None, None, "calib", None),
        P(None, None, "calib", None),
        P(None, "calib", None),
        P(),
        P(),
    )
    out_specs = (P(None, "calib", None, "peak"), P(None, "calib", None, "peak"))
    return jax.shard_map(body, mesh=mesh, in_specs=in_specs, out_specs=out_specs, check_vma=False)
```

profile of v0, /device:TPU:1, one launch (start us, length us, event | category | flops | bytes accessed | tf_op | source)
XLA Modules:
  0.0 148.7 jit_solution(2514231226214089231)
XLA Ops:
  0.6 0.8 copy.51
  1.4 0.7 reshape.193.bounds_ref
  2.1 25.9 %shard_map.77 = bf16[32,4,2,16,256]{4,3,2,1,0:T(8,128)(2,1)} custom-call(s32[32]{0:T(128)} %table_ref.1, s32[224]{0:T(256)} %reshape.193.bounds_ref, s32[2,32,16,1024]{3,2,1,0:T(8,128)} %raw_ref.1, f32[3,32,16,1024]{3,2,1,0:T(8,128)} %ped_ref.1, bf16[3,32,16,1024]{3,2,1,0:T(8,128)(2,1)} %gain_ref.1, s32[32,16,1024]{2,1,0:T(8,128)} %good_ref.1), custom_call_target="tpu_custom_call" | custom-call | tf_op jit(solution)/shard_map/pallas_call | solution.py:121
  28.0 11.5 %all-to-all-start = ((bf16[128,2,16,256]{3,2,1,0:T(8,128)(2,1)}), bf16[128,2,16,256]{3,2,1,0:T(8,128)(2,1)S(1)}, u32[]{:S(2)}, u32[]{:S(2)}) async-start(bf16[128,2,16,256]{3,2,1,0:T(8,128)(2,1)} %bitcast.22), calls=%async_computation | async-start | bytes 4194304 | tf_op jit(solution)/shard_map/all_to_all | solution.py:239
  39.7 1.7 %convert_reduce_fusion = s32[512,256]{1,0:T(8,128)S(1)} fusion(s32[512,256]{1,0:T(8,128)S(1)} %broadcast_add_fusion.1, s32[32]{0:T(128)S(1)} %multiply_multiply_fusion.1), kind=kLoop, calls=%fused_computation.10 | loop fusion | flops 12451840 | bytes 1048704 | tf_op jit(solution)/shard_map/reduce_sum | solution.py:45
  41.5 0.3 copy.67
  41.8 4.6 %convert_convert_fusion = bf16[32,131072]{1,0:T(8,128)(2,1)} fusion(s32[131072]{0:T(1024)S(1)} %bitcast.24), kind=kLoop, calls=%fused_computation.8 | loop fusion | flops 12582912 | bytes 8912896 | tf_op jit(solution)/shard_map/convert_element_type | solution.py:245
  46.6 1.1 constant_dynamic-slice_fusion
  47.9 1.7 %convert_reduce_fusion.1 = s32[32,16,256]{2,1,0:T(8,128)S(1)} fusion(s32[32,16,256]{2,1,0:T(8,128)S(1)} %broadcast_add_fusion, s32[31]{0:T(128)S(1)} %multiply_multiply_fusion), kind=kLoop, calls=%fused_computation.11 | loop fusion | flops 12058624 | bytes 1048700 | tf_op jit(solution)/shard_map/reduce_sum | solution.py:34
  49.6 2.5 %select_reduce_fusion = s32[32]{0:T(128)S(1)} fusion(s32[32,16,256]{2,1,0:T(8,128)S(1)} %constant_dynamic-slice_fusion, s32[32,16,256]{2,1,0:T(8,128)S(1)} %convert_reduce_fusion.1), kind=kLoop, calls=%fused_computation.6 | loop fusion | flops 12582880 | bytes 1048704 | tf_op jit(solution)/shard_map/reduce_sum | solution.py:153
  52.1 17.5 %all-to-all-done = bf16[128,2,16,256]{3,2,1,0:T(8,128)(2,1)S(1)} async-done(((bf16[128,2,16,256]{3,2,1,0:T(8,128)(2,1)}), bf16[128,2,16,256]{3,2,1,0:T(8,128)(2,1)S(1)}, u32[]{:S(2)}, u32[]{:S(2)}) %all-to-all-start) | async-done | bytes 2097184 | tf_op jit(solution)/shard_map/all_to_all | solution.py:239
  69.6 1.5 %copy.69 = bf16[32,4,2,16,256]{4,3,0,2,1:T(8,128)(2,1)} copy(bf16[32,4,2,16,256]{4,3,2,1,0:T(8,128)(2,1)S(1)} %bitcast.20) | data formatting | bytes 4194304 | tf_op jit(solution)/shard_map/reshape | solution.py:240
  71.1 2.5 %reshape_reshape.3 = bf16[8,131072]{1,0:T(8,128)(2,1)S(1)} reshape(bf16[4,2,32,16,256]{4,3,2,1,0:T(8,128)(2,1)} %bitcast.21) | data formatting | bytes 4194304 | tf_op jit(solution)/shard_map/reshape;reshape | solution.py:246
  73.7 0.7 reduce-precision_convert_fusion
  74.3 2.7 %fusion.7 = f32[24,32]{1,0:T(8,128)S(1)} fusion(bf16[8,131072]{1,0:T(8,128)(2,1)S(1)} %get-tuple-element.29, bf16[8,131072]{1,0:T(8,128)(2,1)S(1)} %get-tuple-element.28, bf16[8,131072]{1,0:T(8,128)(2,1)S(1)} %reshape_reshape.3, s32[131072]{0:T(1024)S(1)} %bitcast.25), kind=kOutput, calls=%fused_computation.17 | convolution fusion | flops 232783872 | bytes 6818816 | tf_op jit(solution)/shard_map/fp,kp->fk/dot_general | solution.py:253
  77.1 0.7 fusion.20.refs_0_
  77.8 17.5 %shard_map.78 = f32[8,128]{1,0:T(8,128)} custom-call(f32[8,128]{1,0:T(8,128)} %fusion.20.refs_0_), custom_call_target="tpu_custom_call" | custom-call | tf_op jit(solution)/shard_map/pallas_call | solution.py:207
  95.3 0.7 slice_bitcast_fusion
  96.1 0.8 slice_divide_fusion
  96.9 13.3 %fusion = f32[16,131072]{1,0:T(8,128)} fusion(bf16[32,131072]{1,0:T(8,128)(2,1)} %convert_convert_fusion, bf16[16,32]{1,0:T(8,128)(2,1)S(1)} %get-tuple-element.34, bf16[16,32]{1,0:T(8,128)(2,1)S(1)} %get-tuple-element.33, bf16[16,32]{1,0:T(8,128)(2,1)S(1)} %get-tuple-element.32), kind=kOutput, calls=%fused_computation | convolution fusion | flops 478159872 | bytes 16780288 | tf_op jit(solution)/shard_map/fk,kp->fp/dot_general | solution.py:280
  110.2 5.4 %fusion.31 = (bf16[8,131072]{1,0:T(8,128)(2,1)}, f32[8,131072]{1,0:T(8,128)S(1)}) fusion(f32[16,131072]{1,0:T(8,128)} %fusion, bf16[8,131072]{1,0:T(8,128)(2,1)S(1)} %reshape_reshape.3), kind=kLoop, calls=%fused_computation.80 | loop fusion | flops 4194304 | bytes 16777216 | tf_op jit(solution)/shard_map/convert_element_type | solution.py:287
  115.6 2.4 %fusion.33 = (f32[8,512,1]{2,0,1:T(8,128)}, f32[8,512,1]{2,0,1:T(8,128)S(1)}) fusion(f32[8,512,256]{2,0,1:T(8,128)S(1)} %bitcast.18), kind=kLoop, calls=%fused_computation.81 | loop fusion | bytes 65536 | tf_op jit(solution)/shard_map/slice | solution.py:24
  118.1 2.2 %copy.65 = f32[8,512,1]{1,0,2:T(8,128)S(1)} copy(f32[8,512,1]{2,0,1:T(8,128)} %get-tuple-element.26) | data formatting | bytes 32768
  120.3 3.4 %collective-permute-start = (f32[8,512,1]{1,0,2:T(8,128)S(1)}, f32[8,512,1]{1,0,2:T(8,128)S(1)}, u32[]{:S(2)}, u32[]{:S(2)}) collective-permute-start(f32[8,512,1]{1,0,2:T(8,128)S(1)} %copy.65), channel_id=1, source_target_pairs={{0,1},{1,2},{2,3},{4,5},{5,6},{6,7},{8,9},{9,10},{10,11},{12,13},{... | collective-permute-start | bytes 49160 | tf_op jit(solution)/shard_map/ppermute | solution.py:23
  123.8 0.7 copy.66
  124.5 2.1 %collective-permute-start.1 = (f32[8,512,1]{1,0,2:T(8,128)S(1)}, f32[8,512,1]{1,0,2:T(8,128)S(1)}, u32[]{:S(2)}, u32[]{:S(2)}) collective-permute-start(f32[8,512,1]{1,0,2:T(8,128)S(1)} %copy.66), channel_id=1, source_target_pairs={{1,0},{2,1},{3,2},{5,4},{6,5},{7,6},{9,8},{10,9},{11,10},{13,12},{... | collective-permute-start | bytes 49160 | tf_op jit(solution)/shard_map/ppermute | solution.py:26
  126.6 5.5 %copy.54 = f32[8,512,256]{2,1,0:T(8,128)} copy(f32[8,512,256]{2,0,1:T(8,128)} %bitcast.19) | data formatting | bytes 8388608 | tf_op jit(solution)/shard_map/reshape | solution.py:283
  132.1 1.7 %copy.64 = bf16[8,1,512,256]{3,2,1,0:T(8,128)(2,1)} copy(bf16[8,1,512,256]{3,0,2,1:T(8,128)(2,1)S(1)} %bitcast.23) | data formatting | bytes 4194304
  133.8 0.6 copy.57
  134.5 2.0 %copy.59 = f32[8,512,1]{2,1,0:T(8,128)} copy(f32[8,512,1]{1,0,2:T(8,128)S(1)} %collective-permute-done.1) | data formatting | bytes 32768 | tf_op jit(solution)/shard_map/ppermute | solution.py:26
  136.4 5.6 %select_maximum_fusion = f32[8,514,258]{2,1,0:T(8,128)S(1)} fusion(f32[8,512,1]{2,1,0:T(8,128)} %copy.59, f32[8,512,256]{2,1,0:T(8,128)} %copy.54, f32[8,512,1]{2,1,0:T(8,128)S(1)} %copy.57), kind=kLoop, calls=%fused_computation.14 | loop fusion | flops 8487168 | bytes 8470656 | tf_op jit(solution)/shard_map/concatenate | solution.py:27
  142.0 6.7 %fusion.18 = bf16[8,1,512,256]{3,2,1,0:T(8,128)(2,1)} fusion(f32[8,512,1]{2,1,0:T(8,128)S(1)} %copy-done.2, f32[8,512,256]{2,1,0:T(8,128)S(1)} %copy-done, f32[8,512,1]{2,1,0:T(8,128)S(1)} %copy.57, f32[8,514,258]{2,1,0:T(8,128)S(1)} %select_maximum_fusion), kind=kLoop, calls=%fused_computation.37 | loop fusion | flops 8388608 | bytes 14712832 | tf_op jit(solution)/shard_map/broadcast_in_dim | solution.py:287
  (29 shorter events, 0.8 us)
Async XLA Ops:
  28.0 11.5 %copy-start.4 = (s32[32]{0:T(128)S(1)}, s32[32]{0:T(128)}, u32[]{:S(2)}) copy-start(s32[32]{0:T(128)} %table_ref.1) | copy-start | bytes 388
  28.0 41.6 %all-to-all-start = ((bf16[128,2,16,256]{3,2,1,0:T(8,128)(2,1)}), bf16[128,2,16,256]{3,2,1,0:T(8,128)(2,1)S(1)}, u32[]{:S(2)}, u32[]{:S(2)}) async-start(bf16[128,2,16,256]{3,2,1,0:T(8,128)(2,1)} %bitcast.22), calls=%async_computation | async-start | bytes 4194304 | tf_op jit(solution)/shard_map/all_to_all | solution.py:239
  115.5 2.6 %copy-start.1 = (f32[8,131072]{1,0:T(8,128)}, f32[8,131072]{1,0:T(8,128)S(1)}, u32[]{:S(2)}) copy-start(f32[8,131072]{1,0:T(8,128)S(1)} %get-tuple-element.25) | copy-start | bytes 12582916
  120.3 13.5 %collective-permute-start = (f32[8,512,1]{1,0,2:T(8,128)S(1)}, f32[8,512,1]{1,0,2:T(8,128)S(1)}, u32[]{:S(2)}, u32[]{:S(2)}) collective-permute-start(f32[8,512,1]{1,0,2:T(8,128)S(1)} %copy.65), channel_id=1, source_target_pairs={{0,1},{1,2},{2,3},{4,5},{5,6},{6,7},{8,9},{9,10},{10,11},{12,13},{... | collective-permute-start | bytes 49160 | tf_op jit(solution)/shard_map/ppermute | solution.py:23
  124.5 7.6 %copy-start.3 = (bf16[8,131072]{1,0:T(8,128)(2,1)S(1)}, bf16[8,131072]{1,0:T(8,128)(2,1)}, u32[]{:S(2)}) copy-start(bf16[8,131072]{1,0:T(8,128)(2,1)} %get-tuple-element.24) | copy-start | bytes 6291460
  124.5 10.0 %collective-permute-start.1 = (f32[8,512,1]{1,0,2:T(8,128)S(1)}, f32[8,512,1]{1,0,2:T(8,128)S(1)}, u32[]{:S(2)}, u32[]{:S(2)}) collective-permute-start(f32[8,512,1]{1,0,2:T(8,128)S(1)} %copy.66), channel_id=1, source_target_pairs={{1,0},{2,1},{3,2},{5,4},{6,5},{7,6},{9,8},{10,9},{11,10},{13,12},{... | collective-permute-start | bytes 49160 | tf_op jit(solution)/shard_map/ppermute | solution.py:26
  136.4 5.6 %copy-start = (f32[8,512,256]{2,1,0:T(8,128)S(1)}, f32[8,512,256]{2,1,0:T(8,128)}, u32[]{:S(2)}) copy-start(f32[8,512,256]{2,1,0:T(8,128)} %copy.54) | copy-start | bytes 12582916
  136.4 5.6 %copy-start.2 = (f32[8,512,1]{2,1,0:T(8,128)S(1)}, f32[8,512,1]{2,1,0:T(8,128)}, u32[]{:S(2)}) copy-start(f32[8,512,1]{2,1,0:T(8,128)} %copy.59) | copy-start | bytes 49156
where the time goes:
time: 150 us; the launch traced here: 149 us
  Pallas kernels  43.5 us (29%)
  other arithmetic  30.8 us (21%)
  local copies, waits for them, and re-layouts  23.1 us (15%)
  waiting for transfers between devices  17.5 us (12%)
  starting transfers between devices  17 us (11%)
  matrix products  16 us (11%)
    pallas_call x1, Pallas kernels, calibrate_send(): pl.pallas_call(calibrate_kernel, grid_spec=grid_spec, out_shape=jax.Shape...  25.9 us
    pallas_call x1, Pallas kernels, gather_sum(): pl.pallas_call(lambda *refs: gather_sum_kernel(n_calib, n_peak, *refs), o...  17.5 us
    all_to_all x1, waiting for transfers between devices, body(): got = lax.all_to_all(send, ('calib', 'peak'), 0, 0, tiled=True)  17.5 us
    dot_general x1, matrix products, body(): jnp.einsum('fk,kp->fp', pieces, hits_3, preferred_element_type=jnp.float32)  13.3 us
    all_to_all x1, starting transfers between devices, body(): got = lax.all_to_all(send, ('calib', 'peak'), 0, 0, tiled=True)  11.5 us
    broadcast_in_dim x1, other arithmetic, body(): bent.astype(jnp.bfloat16)[:, None]  6.68 us
    unnamed x15, local copies, waits for them, and re-layouts  5.86 us
    concatenate x1, other arithmetic, padded_2(): block = jnp.concatenate([low, block, high], axis=dim)  5.56 us
  transfers between devices with their start and end apart: 3, of which 1 were waited for; matrix products, arithmetic and copies ran while one was open for 14% of the time, Pallas kernels for 0%

commit v1 on v0

--- a/solution.py
+++ b/solution.py
@@ -240,6 +240,13 @@
     got = got.reshape(n_calib, n_peak, frame_dev, row_dev, width_here)
     frame = jnp.transpose(got, (1, 2, 0, 3, 4)).reshape(frames_all, mrows, width_here)
     slot = lax.axis_index("calib")
+    fwd = [(i, i + 1) for i in range(n_peak - 1)]
+    bwd = [(i + 1, i) for i in range(n_peak - 1)]
+    from_left = lax.ppermute(frame[:, :, width_here - 1 :], "peak", fwd)
+    from_right = lax.ppermute(frame[:, :, :1], "peak", bwd)
+    edge_values = jnp.concatenate([from_left, from_right], axis=2).astype(jnp.float32)
+    peak_start = lax.axis_index("peak") * width_here
+    edge_cols = jnp.stack([peak_start - 1, peak_start + width_here])
     col_dst = lax.axis_index("peak") * width_here + jnp.arange(width_here, dtype=jnp.int32)
     hits = cycle_onehot(slot, jnp.arange(mrows, dtype=jnp.int32), col_dst, mrows, slot_rows)
     hits = hits.astype(jnp.bfloat16)
@@ -281,9 +288,20 @@
     pixel_mean = lookup[:frames_all]
     pixel_rms = lookup[frames_all:]
     score = ((values - pixel_mean) / pixel_rms).reshape(frames_all, mrows, width_here)
-    padded = padded_2(score, (("peak", 2),), 1)
-    padded = jnp.pad(padded, ((0, 0), (1, 1), (0, 0)))
-    bent = laplace(padded)
+    edge_hits = cycle_onehot(slot, jnp.arange(mrows, dtype=jnp.int32), edge_cols, mrows, slot_rows)
+    edge_hits = jnp.concatenate([edge_hits] * 3, axis=0).astype(jnp.bfloat16)
+    edge_lookup = jnp.einsum("fk,kp->fp", pieces, edge_hits, preferred_element_type=jnp.float32)
+    edge_lookup = edge_lookup.reshape(2 * frames_all, mrows, 2)
+    edge_score = (edge_values - edge_lookup[:frames_all]) / edge_lookup[frames_all:]
+    peak_pos = lax.axis_index("peak")
+    left = jnp.where(peak_pos == 0, 0.0, edge_score[:, :, :1])
+    right = jnp.where(peak_pos == n_peak - 1, 0.0, edge_score[:, :, 1:])
+    zero_row = jnp.zeros((frames_all, 1, width_here), jnp.float32)
+    up = jnp.concatenate([zero_row, score[:, :-1]], axis=1)
+    down = jnp.concatenate([score[:, 1:], zero_row], axis=1)
+    left_nb = jnp.concatenate([left, score[:, :, :-1]], axis=2)
+    right_nb = jnp.concatenate([score[:, :, 1:], right], axis=2)
+    bent = 4.0 * score - up - down - left_nb - right_nb
     return (score.astype(jnp.bfloat16)[:, None], bent.astype(jnp.bfloat16)[:, None])
 
 

time: 150 us -> 174 us (1.16)
  local copies, waits for them, and re-layouts: 23.1 us -> 46.5 us
    unnamed x15 -> x25, local copies, waits for them, and re-layouts: 5.86 us -> 19.5 us
    slice x1 -> x8, local copies, waits for them, and re-layouts: 2.45 us -> 12.2 us  [the longest x1 4.57 us: body(): left_nb = jnp.concatenate([left, score[:, :, :-1]], axis=2)]
    select_n x0 -> x2, local copies, waits for them, and re-layouts: none -> 7.63 us  [the longest x1 4.18 us: body(): left = jnp.where(peak_pos == 0, 0.0, edge_score[:, :, :1])]
    reshape x2 -> x0, local copies, waits for them, and re-layouts: 7.04 us -> none  [the longest x1 5.52 us: body(): ((values - pixel_mean) / pixel_rms).reshape(frames_all, mrows, width_here)]
    concatenate x1 -> x0, other arithmetic: 5.56 us -> none  [padded_2(): block = jnp.concatenate([low, block, high], axis=dim)]
    broadcast_in_dim x1, other arithmetic: 6.68 us -> 10.7 us  [body(): bent.astype(jnp.bfloat16)[:, None]]
    ppermute x2 -> x0, local copies, waits for them, and re-layouts: 2.6 us -> none  [the longest x1 1.97 us: padded_2(): lax.ppermute(lax.slice_in_dim(block, 0, width, axis=dim), axis, backward)]
    transpose x0 -> x1, local copies, waits for them, and re-layouts: none -> 1.78 us  [body(): jnp.transpose(got, (1, 2, 0, 3, 4)).reshape(frames_all, mrows, width_here)]
  transfers between devices with their start and end apart: 3 -> 3, of which waited for: 1 -> 1; matrix products, arithmetic and copies ran while one was open for 14% -> 18% of each run, Pallas kernels for 0% -> 0%
where the time goes in v1:
time: 174 us; the launch traced here: 173 us
  local copies, waits for them, and re-layouts  46.5 us (27%)
  Pallas kernels  43.5 us (25%)
  other arithmetic  31.9 us (18%)
  waiting for transfers between devices  16.9 us (10%)
  starting transfers between devices  16.8 us (10%)
  matrix products  16.3 us (9%)
    pallas_call x1, Pallas kernels, calibrate_send(): pl.pallas_call(calibrate_kernel, grid_spec=grid_spec, out_shape=jax.Shape...  25.9 us
    unnamed x25, local copies, waits for them, and re-layouts  19.5 us
    pallas_call x1, Pallas kernels, gather_sum(): pl.pallas_call(lambda *refs: gather_sum_kernel(n_calib, n_peak, *refs), o...  17.5 us
    all_to_all x1, waiting for transfers between devices, body(): got = lax.all_to_all(send, ('calib', 'peak'), 0, 0, tiled=True)  16.9 us
    dot_general x1, matrix products, body(): jnp.einsum('fk,kp->fp', pieces, hits_3, preferred_element_type=jnp.float32)  13.4 us
    all_to_all x1, starting transfers between devices, body(): got = lax.all_to_all(send, ('calib', 'peak'), 0, 0, tiled=True)  11.5 us
    broadcast_in_dim x1, other arithmetic, body(): bent.astype(jnp.bfloat16)[:, None]  10.7 us
    convert_element_type x1, other arithmetic, body(): score.astype(jnp.bfloat16)[:, None]  5.53 us
  transfers between devices with their start and end apart: 3, of which 1 were waited for; matrix products, arithmetic and copies ran while one was open for 18% of the time, Pallas kernels for 0%

profile of v1, /device:TPU:1, one launch (start us, length us, event | category | flops | bytes accessed | tf_op | source)
XLA Modules:
  0.0 172.8 jit_solution(17621458149695505701)
XLA Ops:
  0.6 0.8 copy.85
  2.1 25.9 %shard_map.77 = bf16[32,4,2,16,256]{4,3,2,1,0:T(8,128)(2,1)} custom-call(s32[32]{0:T(128)} %table_ref.1, s32[224]{0:T(256)} %reshape.256.bounds_ref, s32[2,32,16,1024]{3,2,1,0:T(8,128)} %raw_ref.1, f32[3,32,16,1024]{3,2,1,0:T(8,128)} %ped_ref.1, bf16[3,32,16,1024]{3,2,1,0:T(8,128)(2,1)} %gain_ref.1, s32[32,16,1024]{2,1,0:T(8,128)} %good_ref.1), custom_call_target="tpu_custom_call" | custom-call | tf_op jit(solution)/shard_map/pallas_call | solution.py:121
  28.0 11.5 %all-to-all-start = ((bf16[128,2,16,256]{3,2,1,0:T(8,128)(2,1)}), bf16[128,2,16,256]{3,2,1,0:T(8,128)(2,1)S(1)}, u32[]{:S(2)}, u32[]{:S(2)}) async-start(bf16[128,2,16,256]{3,2,1,0:T(8,128)(2,1)} %bitcast.31), calls=%async_computation | async-start | bytes 4194304 | tf_op jit(solution)/shard_map/all_to_all | solution.py:239
  39.7 1.7 convert_reduce_fusion
  41.8 4.6 %convert_convert_fusion = bf16[32,131072]{1,0:T(8,128)(2,1)} fusion(s32[131072]{0:T(1024)S(1)} %bitcast.33), kind=kLoop, calls=%fused_computation.8 | loop fusion | flops 12582912 | bytes 8912896 | tf_op jit(solution)/shard_map/convert_element_type | solution.py:252
  47.2 1.1 constant_dynamic-slice_fusion
  48.5 1.7 convert_reduce_fusion.1
  50.2 2.5 %select_reduce_fusion = s32[32]{0:T(128)S(1)} fusion(s32[32,16,256]{2,1,0:T(8,128)S(1)} %constant_dynamic-slice_fusion, s32[32,16,256]{2,1,0:T(8,128)S(1)} %convert_reduce_fusion.1), kind=kLoop, calls=%fused_computation.6 | loop fusion | flops 12582880 | bytes 1048704 | tf_op jit(solution)/shard_map/reduce_sum | solution.py:153
  52.7 16.9 %all-to-all-done = bf16[128,2,16,256]{3,2,1,0:T(8,128)(2,1)S(1)} async-done(((bf16[128,2,16,256]{3,2,1,0:T(8,128)(2,1)}), bf16[128,2,16,256]{3,2,1,0:T(8,128)(2,1)S(1)}, u32[]{:S(2)}, u32[]{:S(2)}) %all-to-all-start) | async-done | bytes 2097184 | tf_op jit(solution)/shard_map/all_to_all | solution.py:239
  69.6 1.3 copy-done.6
  70.9 1.8 %copy.86 = bf16[4,2,32,16,256]{4,3,2,1,0:T(8,128)(2,1)S(1)} copy(bf16[4,2,32,16,256]{4,3,1,0,2:T(8,128)(2,1)} %bitcast.30) | data formatting | bytes 4194304 | tf_op jit(solution)/shard_map/transpose | solution.py:241
  72.7 2.3 %reshape_reshape.3 = bf16[8,131072]{1,0:T(8,128)(2,1)} reshape(bf16[4,2,32,16,256]{4,3,2,1,0:T(8,128)(2,1)S(1)} %copy.86) | data formatting | bytes 4194304 | tf_op jit(solution)/shard_map/reshape;reshape | solution.py:253
  75.0 2.4 %reduce-precision_convert_fusion = (bf16[8,131072]{1,0:T(8,128)(2,1)S(1)}, bf16[8,131072]{1,0:T(8,128)(2,1)S(1)}) fusion(bf16[8,131072]{1,0:T(8,128)(2,1)} %reshape_reshape.3), kind=kLoop, calls=%fused_computation.19 | loop fusion | flops 6291456 | bytes 6291456 | tf_op jit(solution)/shard_map/convert_element_type | solution.py:257
  77.4 2.7 %fusion.6 = f32[24,32]{1,0:T(8,128)S(1)} fusion(bf16[8,131072]{1,0:T(8,128)(2,1)S(1)} %get-tuple-element.37, bf16[8,131072]{1,0:T(8,128)(2,1)S(1)} %get-tuple-element.36, bf16[8,131072]{1,0:T(8,128)(2,1)S(1)} %copy-done.1, s32[131072]{0:T(1024)S(1)} %bitcast.34), kind=kOutput, calls=%fused_computation.12 | convolution fusion | flops 232783872 | bytes 6818816 | tf_op jit(solution)/shard_map/fp,kp->fk/dot_general | solution.py:260
  80.8 17.5 %shard_map.78 = f32[8,128]{1,0:T(8,128)} custom-call(f32[8,128]{1,0:T(8,128)} %fusion.19.refs_0_), custom_call_target="tpu_custom_call" | custom-call | tf_op jit(solution)/shard_map/pallas_call | solution.py:207
  99.1 0.8 slice_divide_fusion
  100.0 13.4 %fusion = f32[16,131072]{1,0:T(8,128)} fusion(bf16[32,131072]{1,0:T(8,128)(2,1)} %convert_convert_fusion, bf16[16,32]{1,0:T(8,128)(2,1)S(1)} %get-tuple-element.46, bf16[16,32]{1,0:T(8,128)(2,1)S(1)} %get-tuple-element.45, bf16[16,32]{1,0:T(8,128)(2,1)S(1)} %get-tuple-element.44), kind=kOutput, calls=%fused_computation | convolution fusion | flops 478159872 | bytes 16780288 | tf_op jit(solution)/shard_map/fk,kp->fp/dot_general | solution.py:287
  113.4 5.5 %fusion.27 = (bf16[8,131072]{1,0:T(8,128)(2,1)}, f32[8,131072]{1,0:T(8,128)S(1)}) fusion(f32[16,131072]{1,0:T(8,128)} %fusion, bf16[8,131072]{1,0:T(8,128)(2,1)S(1)} %copy-done.2), kind=kLoop, calls=%fused_computation.80 | loop fusion | flops 4194304 | bytes 16777216 | tf_op jit(solution)/shard_map/convert_element_type | solution.py:305
  118.9 4.6 %fusion.30 = (f32[8,512,255]{2,0,1:T(8,128)}, f32[8,512,255]{2,0,1:T(8,128)}) fusion(f32[8,512,256]{2,0,1:T(8,128)S(1)} %bitcast.26), kind=kLoop, calls=%fused_computation.82 | loop fusion | bytes 16711680 | tf_op jit(solution)/shard_map/slice | solution.py:302
  123.5 3.7 %fusion.29 = (f32[8,511,256]{2,0,1:T(8,128)}, f32[8,511,256]{2,0,1:T(8,128)}) fusion(f32[8,512,256]{2,0,1:T(8,128)S(1)} %bitcast.27), kind=kLoop, calls=%fused_computation.81 | loop fusion | bytes 16744448 | tf_op jit(solution)/shard_map/slice | solution.py:300
  127.4 1.5 fusion.31
  128.9 1.6 copy.92
  130.5 3.4 %collective-permute-start = (bf16[8,512,1]{1,0,2:T(8,128)(2,1)S(1)}, bf16[8,512,1]{1,0,2:T(8,128)(2,1)S(1)}, u32[]{:S(2)}, u32[]{:S(2)}) collective-permute-start(bf16[8,512,1]{1,0,2:T(8,128)(2,1)S(1)} %copy.92), channel_id=1, source_target_pairs={{0,1},{1,2},{2,3},{4,5},{5,6},{6,7},{8,9},{9,10},{10,11},{12,13},{... | collective-permute-start | bytes 24584 | tf_op jit(solution)/shard_map/ppermute | solution.py:245
  134.3 1.9 %collective-permute-start.1 = (bf16[8,512,1]{1,0,2:T(8,128)(2,1)S(1)}, bf16[8,512,1]{1,0,2:T(8,128)(2,1)S(1)}, u32[]{:S(2)}, u32[]{:S(2)}) collective-permute-start(bf16[8,512,1]{1,0,2:T(8,128)(2,1)S(1)} %copy.93), channel_id=1, source_target_pairs={{1,0},{2,1},{3,2},{5,4},{6,5},{7,6},{9,8},{10,9},{11,10},{13,12},{... | collective-permute-start | bytes 24584 | tf_op jit(solution)/shard_map/ppermute | solution.py:246
  136.2 5.7 %copy.105 = f32[8,512,255]{2,1,0:T(8,128)} copy(f32[8,512,255]{2,0,1:T(8,128)} %get-tuple-element.33) | data formatting | bytes 8355840
  141.9 3.3 %copy.106 = f32[8,512,255]{2,1,0:T(8,128)} copy(f32[8,512,255]{2,0,1:T(8,128)S(1)} %copy-done.3) | data formatting | bytes 8355840
  145.1 3.2 %copy.107 = f32[8,511,256]{2,1,0:T(8,128)} copy(f32[8,511,256]{2,0,1:T(8,128)S(1)} %copy-done.5) | data formatting | bytes 8372224
  148.3 3.2 %copy.108 = f32[8,511,256]{2,1,0:T(8,128)} copy(f32[8,511,256]{2,0,1:T(8,128)S(1)} %copy-done.4) | data formatting | bytes 8372224
  152.0 1.7 %copy.102 = bf16[8,1,512,256]{3,2,1,0:T(8,128)(2,1)} copy(bf16[8,1,512,256]{3,0,2,1:T(8,128)(2,1)S(1)} %bitcast.32) | data formatting | bytes 4194304
  154.5 3.4 %copy.101 = f32[8,512,1]{2,1,0:T(8,128)S(1)} copy(f32[8,512,1]{0,2,1:T(1,128)S(1)} %get-tuple-element.39) | data formatting | bytes 32768 | tf_op jit(solution)/shard_map/jit(_where)/select_n | solution.py:298
  158.0 4.2 %copy.99 = f32[8,512,1]{2,1,0:T(8,128)} copy(f32[8,512,1]{0,2,1:T(1,128)S(1)} %get-tuple-element.38) | data formatting | bytes 32768 | tf_op jit(solution)/shard_map/jit(_where)/select_n | solution.py:297
  162.2 10.7 %fusion.16 = bf16[8,1,512,256]{3,2,1,0:T(8,128)(2,1)} fusion(f32[8,512,1]{2,1,0:T(8,128)S(1)} %copy.101, f32[8,512,255]{2,1,0:T(8,128)} %copy.105, f32[8,512,255]{2,1,0:T(8,128)} %copy.106, f32[8,512,1]{2,1,0:T(8,128)} %copy.99, f32[8,511,256]{2,1,0:T(8,128)} %copy.107, f32[8,511,256]{2,1,0:T(8,128)} %copy.108, f32[8,512,256]{2,0,1:T(8,128)} %bitcast.28), kind=kLoop, calls=%fused_computation.27 | loop fusion | flops 8388608 | bytes 23052288 | tf_op jit(solution)/shard_map/broadcast_in_dim | solution.py:305
  (56 shorter events, 5.4 us)
Async XLA Ops:
  28.0 11.5 %copy-start.8 = (s32[32]{0:T(128)S(1)}, s32[32]{0:T(128)}, u32[]{:S(2)}) copy-start(s32[32]{0:T(128)} %table_ref.1) | copy-start | bytes 388
  28.0 41.6 %all-to-all-start = ((bf16[128,2,16,256]{3,2,1,0:T(8,128)(2,1)}), bf16[128,2,16,256]{3,2,1,0:T(8,128)(2,1)S(1)}, u32[]{:S(2)}, u32[]{:S(2)}) async-start(bf16[128,2,16,256]{3,2,1,0:T(8,128)(2,1)} %bitcast.31), calls=%async_computation | async-start | bytes 4194304 | tf_op jit(solution)/shard_map/all_to_all | solution.py:239
  69.6 1.3 copy-start.6
  75.0 2.4 %copy-start.1 = (bf16[8,131072]{1,0:T(8,128)(2,1)S(1)}, bf16[8,131072]{1,0:T(8,128)(2,1)}, u32[]{:S(2)}) copy-start(bf16[8,131072]{1,0:T(8,128)(2,1)} %reshape_reshape.3) | copy-start | bytes 6291460
  100.0 13.4 %copy-start.2 = (bf16[8,131072]{1,0:T(8,128)(2,1)S(1)}, bf16[8,131072]{1,0:T(8,128)(2,1)}, u32[]{:S(2)}) copy-start(bf16[8,131072]{1,0:T(8,128)(2,1)} %reshape_reshape.3) | copy-start | bytes 6291460
  118.9 4.6 %copy-start = (f32[8,131072]{1,0:T(8,128)}, f32[8,131072]{1,0:T(8,128)S(1)}, u32[]{:S(2)}) copy-start(f32[8,131072]{1,0:T(8,128)S(1)} %get-tuple-element.29) | copy-start | bytes 12582916
  130.5 23.2 %collective-permute-start = (bf16[8,512,1]{1,0,2:T(8,128)(2,1)S(1)}, bf16[8,512,1]{1,0,2:T(8,128)(2,1)S(1)}, u32[]{:S(2)}, u32[]{:S(2)}) collective-permute-start(bf16[8,512,1]{1,0,2:T(8,128)(2,1)S(1)} %copy.92), channel_id=1, source_target_pairs={{0,1},{1,2},{2,3},{4,5},{5,6},{6,7},{8,9},{9,10},{10,11},{12,13},{... | collective-permute-start | bytes 24584 | tf_op jit(solution)/shard_map/ppermute | solution.py:245
  134.3 19.5 %collective-permute-start.1 = (bf16[8,512,1]{1,0,2:T(8,128)(2,1)S(1)}, bf16[8,512,1]{1,0,2:T(8,128)(2,1)S(1)}, u32[]{:S(2)}, u32[]{:S(2)}) collective-permute-start(bf16[8,512,1]{1,0,2:T(8,128)(2,1)S(1)} %copy.93), channel_id=1, source_target_pairs={{1,0},{2,1},{3,2},{5,4},{6,5},{7,6},{9,8},{10,9},{11,10},{13,12},{... | collective-permute-start | bytes 24584 | tf_op jit(solution)/shard_map/ppermute | solution.py:246
  136.2 5.7 %copy-start.3 = (f32[8,512,255]{2,0,1:T(8,128)S(1)}, f32[8,512,255]{2,0,1:T(8,128)}, u32[]{:S(2)}) copy-start(f32[8,512,255]{2,0,1:T(8,128)} %get-tuple-element.32) | copy-start | bytes 12533764
  141.9 3.3 %copy-start.5 = (f32[8,511,256]{2,0,1:T(8,128)S(1)}, f32[8,511,256]{2,0,1:T(8,128)}, u32[]{:S(2)}) copy-start(f32[8,511,256]{2,0,1:T(8,128)} %get-tuple-element.31) | copy-start | bytes 12558340
  145.1 3.2 %copy-start.4 = (f32[8,511,256]{2,0,1:T(8,128)S(1)}, f32[8,511,256]{2,0,1:T(8,128)}, u32[]{:S(2)}) copy-start(f32[8,511,256]{2,0,1:T(8,128)} %get-tuple-element.30) | copy-start | bytes 12558340
  148.3 3.6 %copy-start.7 = (bf16[8,131072]{1,0:T(8,128)(2,1)S(1)}, bf16[8,131072]{1,0:T(8,128)(2,1)}, u32[]{:S(2)}) copy-start(bf16[8,131072]{1,0:T(8,128)(2,1)} %get-tuple-element.28) | copy-start | bytes 6291460

commit v2 on v0

--- a/solution.py
+++ b/solution.py
@@ -123,6 +123,41 @@
         grid_spec=grid_spec,
         out_shape=jax.ShapeDtypeStruct((mods, n_peak, frame_dev, row_dev, width), jnp.bfloat16),
     )(table, bounds.reshape(-1), raw, pedestal, gain, good)
+
+
+def laplace_kernel(n_peak, score_ref, left_ref, right_ref, snr_ref, bent_ref):
+    score = score_ref[...]
+    rows, cols = score.shape
+    peak_pos = lax.axis_index("peak")
+    row_ids = lax.broadcasted_iota(jnp.int32, (rows, cols), 0)
+    col_ids = lax.broadcasted_iota(jnp.int32, (rows, cols), 1)
+    left_col = jnp.where(peak_pos == 0, 0.0, left_ref[...])
+    right_col = jnp.where(peak_pos == n_peak - 1, 0.0, right_ref[...])
+    total = 4.0 * score
+    for shift in (1, rows - 1):
+        moved = pltpu.roll(score, shift, 0)
+        source = pltpu.roll(row_ids, shift, 0)
+        total = total - jnp.where(jnp.abs(source - row_ids) == 1, moved, 0.0)
+    for shift in (1, cols - 1):
+        moved = pltpu.roll(score, shift, 1)
+        source = pltpu.roll(col_ids, shift, 1)
+        near = jnp.where(source == cols - 1, left_col, right_col)
+        total = total - jnp.where(jnp.abs(source - col_ids) == 1, moved, near)
+    snr_ref[...] = score.astype(snr_ref.dtype)
+    bent_ref[...] = total.astype(bent_ref.dtype)
+
+
+def score_outputs(score, left, right, n_peak):
+    frames, rows, cols = score.shape
+    block = pl.BlockSpec((None, rows, cols), lambda f: (f, 0, 0))
+    edge = pl.BlockSpec((None, rows, 1), lambda f: (f, 0, 0))
+    return pl.pallas_call(
+        lambda *refs: laplace_kernel(n_peak, *refs),
+        grid=(frames,),
+        in_specs=[block, edge, edge],
+        out_specs=[block, block],
+        out_shape=[jax.ShapeDtypeStruct(score.shape, jnp.bfloat16)] * 2,
+    )(score, left, right)
 
 
 def laplace(padded):
@@ -281,10 +316,12 @@
     pixel_mean = lookup[:frames_all]
     pixel_rms = lookup[frames_all:]
     score = ((values - pixel_mean) / pixel_rms).reshape(frames_all, mrows, width_here)
-    padded = padded_2(score, (("peak", 2),), 1)
-    padded = jnp.pad(padded, ((0, 0), (1, 1), (0, 0)))
-    bent = laplace(padded)
-    return (score.astype(jnp.bfloat16)[:, None], bent.astype(jnp.bfloat16)[:, None])
+    fwd = [(i, i + 1) for i in range(n_peak - 1)]
+    bwd = [(i + 1, i) for i in range(n_peak - 1)]
+    left = lax.ppermute(score[:, :, width_here - 1 :], "peak", fwd)
+    right = lax.ppermute(score[:, :, :1], "peak", bwd)
+    snr, bent = score_outputs(score, left, right, n_peak)
+    return (snr[:, None], bent[:, None])
 
 
 def solution(mesh):

time: 150 us -> 144 us (0.960)
  other arithmetic: 30.8 us -> 17.2 us
  Pallas kernels: 43.5 us -> 53.1 us
  local copies, waits for them, and re-layouts: 23.1 us -> 19.8 us
  starting transfers between devices: 17 us -> 18.6 us
    pallas_call x0 -> x1, Pallas kernels: none -> 9.48 us  [score_outputs(): pl.pallas_call(lambda *refs: laplace_kernel(n_peak, *refs), grid=(frames,...]
    broadcast_in_dim x1 -> x0, other arithmetic: 6.68 us -> none  [body(): bent.astype(jnp.bfloat16)[:, None]]
    concatenate x1 -> x0, other arithmetic: 5.56 us -> none  [padded_2(): block = jnp.concatenate([low, block, high], axis=dim)]
    reshape x1 -> x0, local copies, waits for them, and re-layouts: 5.52 us -> none  [body(): ((values - pixel_mean) / pixel_rms).reshape(frames_all, mrows, width_here)]
    convert_element_type x1 -> x0, other arithmetic: 5.4 us -> none  [body(): score.astype(jnp.bfloat16)[:, None]]
    div x0 -> x1, other arithmetic: none -> 4.01 us  [body(): (values - pixel_mean) / pixel_rms]
    slice x1 -> x3, local copies, waits for them, and re-layouts: 2.45 us -> 4.83 us  [the longest x2 4.22 us: body(): right = lax.ppermute(score[:, :, :1], 'peak', bwd)]
    ppermute x2, starting transfers between devices: 5.46 us -> 7.07 us  [the longest x1 4.71 us: body(): left = lax.ppermute(score[:, :, width_here - 1:], 'peak', fwd)]
  transfers between devices with their start and end apart: 3 -> 3, of which waited for: 1 -> 1; matrix products, arithmetic and copies ran while one was open for 14% -> 11% of each run, Pallas kernels for 0% -> 0%
where the time goes in v2:
time: 144 us; the launch traced here: 143 us
  Pallas kernels  53.1 us (37%)
  local copies, waits for them, and re-layouts  19.8 us (14%)
  starting transfers between devices  18.6 us (13%)
  waiting for transfers between devices  17.5 us (12%)
  other arithmetic  17.2 us (12%)
  matrix products  16 us (11%)
    pallas_call x1, Pallas kernels, calibrate_send(): pl.pallas_call(calibrate_kernel, grid_spec=grid_spec, out_shape=jax.Shape...  26.1 us
    pallas_call x1, Pallas kernels, gather_sum(): pl.pallas_call(lambda *refs: gather_sum_kernel(n_calib, n_peak, *refs), o...  17.6 us
    all_to_all x1, waiting for transfers between devices, body(): got = lax.all_to_all(send, ('calib', 'peak'), 0, 0, tiled=True)  17.5 us
    dot_general x1, matrix products, body(): jnp.einsum('fk,kp->fp', pieces, hits_3, preferred_element_type=jnp.float32)  13.3 us
    all_to_all x1, starting transfers between devices, body(): got = lax.all_to_all(send, ('calib', 'peak'), 0, 0, tiled=True)  11.5 us
    pallas_call x1, Pallas kernels, score_outputs(): pl.pallas_call(lambda *refs: laplace_kernel(n_peak, *refs), grid=(frames,...  9.48 us
    ppermute x1, starting transfers between devices, body(): left = lax.ppermute(score[:, :, width_here - 1:], 'peak', fwd)  4.71 us
    convert_element_type x1, other arithmetic, body(): hits = hits.astype(jnp.bfloat16)  4.58 us
  transfers between devices with their start and end apart: 3, of which 1 were waited for; matrix products, arithmetic and copies ran while one was open for 11% of the time, Pallas kernels for 0%

profile of v2, /device:TPU:1, one launch (start us, length us, event | category | flops | bytes accessed | tf_op | source)
XLA Modules:
  0.0 143.0 jit_solution(5941691568640244693)
XLA Ops:
  0.6 0.8 copy.31
  1.4 0.7 reshape.182.bounds_ref
  2.1 26.1 %shard_map.77 = bf16[32,4,2,16,256]{4,3,2,1,0:T(8,128)(2,1)} custom-call(s32[32]{0:T(128)} %table_ref.1, s32[224]{0:T(256)} %reshape.182.bounds_ref, s32[2,32,16,1024]{3,2,1,0:T(8,128)} %raw_ref.1, f32[3,32,16,1024]{3,2,1,0:T(8,128)} %ped_ref.1, bf16[3,32,16,1024]{3,2,1,0:T(8,128)(2,1)} %gain_ref.1, s32[32,16,1024]{2,1,0:T(8,128)} %good_ref.1), custom_call_target="tpu_custom_call" | custom-call | tf_op jit(solution)/shard_map/pallas_call | solution.py:121
  28.1 11.5 %all-to-all-start = ((bf16[128,2,16,256]{3,2,1,0:T(8,128)(2,1)}), bf16[128,2,16,256]{3,2,1,0:T(8,128)(2,1)S(1)}, u32[]{:S(2)}, u32[]{:S(2)}) async-start(bf16[128,2,16,256]{3,2,1,0:T(8,128)(2,1)} %bitcast.29), calls=%async_computation | async-start | bytes 4194304 | tf_op jit(solution)/shard_map/all_to_all | solution.py:274
  39.9 1.7 %convert_reduce_fusion = s32[512,256]{1,0:T(8,128)S(1)} fusion(s32[512,256]{1,0:T(8,128)S(1)} %broadcast_add_fusion.1, s32[32]{0:T(128)S(1)} %multiply_multiply_fusion.1), kind=kLoop, calls=%fused_computation.10 | loop fusion | flops 12451840 | bytes 1048704 | tf_op jit(solution)/shard_map/reduce_sum | solution.py:45
  41.6 0.3 copy.40
  41.9 4.6 %convert_convert_fusion = bf16[32,131072]{1,0:T(8,128)(2,1)} fusion(s32[131072]{0:T(1024)S(1)} %bitcast.30), kind=kLoop, calls=%fused_computation.8 | loop fusion | flops 12582912 | bytes 8912896 | tf_op jit(solution)/shard_map/convert_element_type | solution.py:280
  46.7 1.1 constant_dynamic-slice_fusion
  47.9 0.1 broadcast_add_fusion
  48.0 1.7 %convert_reduce_fusion.1 = s32[32,16,256]{2,1,0:T(8,128)S(1)} fusion(s32[32,16,256]{2,1,0:T(8,128)S(1)} %broadcast_add_fusion, s32[31]{0:T(128)S(1)} %multiply_multiply_fusion), kind=kLoop, calls=%fused_computation.11 | loop fusion | flops 12058624 | bytes 1048700 | tf_op jit(solution)/shard_map/reduce_sum | solution.py:34
  49.7 2.5 %select_reduce_fusion = s32[32]{0:T(128)S(1)} fusion(s32[32,16,256]{2,1,0:T(8,128)S(1)} %constant_dynamic-slice_fusion, s32[32,16,256]{2,1,0:T(8,128)S(1)} %convert_reduce_fusion.1), kind=kLoop, calls=%fused_computation.6 | loop fusion | flops 12582880 | bytes 1048704 | tf_op jit(solution)/shard_map/reduce_sum | solution.py:188
  52.2 17.5 %all-to-all-done = bf16[128,2,16,256]{3,2,1,0:T(8,128)(2,1)S(1)} async-done(((bf16[128,2,16,256]{3,2,1,0:T(8,128)(2,1)}), bf16[128,2,16,256]{3,2,1,0:T(8,128)(2,1)S(1)}, u32[]{:S(2)}, u32[]{:S(2)}) %all-to-all-start) | async-done | bytes 2097184 | tf_op jit(solution)/shard_map/all_to_all | solution.py:274
  69.7 1.5 %copy.45 = bf16[32,4,2,16,256]{4,3,0,2,1:T(8,128)(2,1)} copy(bf16[32,4,2,16,256]{4,3,2,1,0:T(8,128)(2,1)S(1)} %bitcast.27) | data formatting | bytes 4194304 | tf_op jit(solution)/shard_map/reshape | solution.py:275
  71.2 2.5 %reshape_reshape.3 = bf16[8,131072]{1,0:T(8,128)(2,1)S(1)} reshape(bf16[4,2,32,16,256]{4,3,2,1,0:T(8,128)(2,1)} %bitcast.28) | data formatting | bytes 4194304 | tf_op jit(solution)/shard_map/reshape;reshape | solution.py:281
  73.8 0.7 reduce-precision_convert_fusion
  74.5 2.7 %fusion.6 = f32[24,32]{1,0:T(8,128)S(1)} fusion(bf16[8,131072]{1,0:T(8,128)(2,1)S(1)} %get-tuple-element.31, bf16[8,131072]{1,0:T(8,128)(2,1)S(1)} %get-tuple-element.30, bf16[8,131072]{1,0:T(8,128)(2,1)S(1)} %reshape_reshape.3, s32[131072]{0:T(1024)S(1)} %bitcast.31), kind=kOutput, calls=%fused_computation.12 | convolution fusion | flops 232783872 | bytes 6818816 | tf_op jit(solution)/shard_map/fp,kp->fk/dot_general | solution.py:288
  77.2 0.7 fusion.15.refs_0_
  77.9 17.6 %shard_map.78 = f32[8,128]{1,0:T(8,128)} custom-call(f32[8,128]{1,0:T(8,128)} %fusion.15.refs_0_), custom_call_target="tpu_custom_call" | custom-call | tf_op jit(solution)/shard_map/pallas_call | solution.py:242
  95.4 0.8 slice_bitcast_fusion
  96.2 0.8 slice_divide_fusion
  97.1 13.3 %fusion = f32[16,131072]{1,0:T(8,128)} fusion(bf16[32,131072]{1,0:T(8,128)(2,1)} %convert_convert_fusion, bf16[16,32]{1,0:T(8,128)(2,1)S(1)} %get-tuple-element.36, bf16[16,32]{1,0:T(8,128)(2,1)S(1)} %get-tuple-element.35, bf16[16,32]{1,0:T(8,128)(2,1)S(1)} %get-tuple-element.34), kind=kOutput, calls=%fused_computation | convolution fusion | flops 478159872 | bytes 16780288 | tf_op jit(solution)/shard_map/fk,kp->fp/dot_general | solution.py:315
  110.3 4.0 %fusion.12 = f32[8,131072]{1,0:T(8,128)S(1)} fusion(bf16[8,131072]{1,0:T(8,128)(2,1)S(1)} %reshape_reshape.3, f32[16,131072]{1,0:T(8,128)} %fusion), kind=kLoop, calls=%fused_computation.22 | loop fusion | flops 3145728 | bytes 14680064 | tf_op jit(solution)/shard_map/div | solution.py:318
  114.4 1.4 copy.44
  115.7 1.9 %copy-done = f32[1,8,512,256]{3,2,1,0:T(8,128)} copy-done((f32[1,8,512,256]{3,2,1,0:T(8,128)}, f32[1,8,512,256]{3,2,1,0:T(8,128)S(1)}, u32[]{:S(2)}) %copy-start) | copy-done | bytes 4194328
  117.6 2.0 %fusion.26 = (f32[8,512,1]{2,1,0:T(8,128)}, f32[8,512,1]{2,1,0:T(8,128)S(1)}) fusion(f32[8,512,256]{2,1,0:T(8,128)S(1)} %bitcast.24), kind=kLoop, calls=%fused_computation.68 | loop fusion | bytes 65536 | tf_op jit(solution)/shard_map/slice | solution.py:322
  119.7 2.2 %copy.35 = f32[8,512,1]{1,0,2:T(8,128)S(1)} copy(f32[8,512,1]{2,1,0:T(8,128)} %get-tuple-element.28) | data formatting | bytes 32768 | tf_op jit(solution)/shard_map/slice | solution.py:322
  121.9 2.4 %collective-permute-start.1 = (f32[8,512,1]{1,0,2:T(8,128)S(1)}, f32[8,512,1]{1,0,2:T(8,128)S(1)}, u32[]{:S(2)}, u32[]{:S(2)}) collective-permute-start(f32[8,512,1]{1,0,2:T(8,128)S(1)} %copy.35), channel_id=1, source_target_pairs={{1,0},{2,1},{3,2},{5,4},{6,5},{7,6},{9,8},{10,9},{11,10},{13,12},{... | collective-permute-start | bytes 49160 | tf_op jit(solution)/shard_map/ppermute | solution.py:322
  124.2 0.6 copy.34
  124.8 4.7 %collective-permute-start = (f32[8,512,1]{1,0,2:T(8,128)S(1)}, f32[8,512,1]{1,0,2:T(8,128)S(1)}, u32[]{:S(2)}, u32[]{:S(2)}) collective-permute-start(f32[8,512,1]{1,0,2:T(8,128)S(1)} %copy.34), channel_id=1, source_target_pairs={{0,1},{1,2},{2,3},{4,5},{5,6},{6,7},{8,9},{9,10},{10,11},{12,13},{... | collective-permute-start | bytes 49160 | tf_op jit(solution)/shard_map/ppermute | solution.py:321
  129.6 2.0 %copy.37.refs_2_ = f32[8,512,1]{2,1,0:T(8,128)} copy(f32[8,512,1]{1,0,2:T(8,128)S(1)} %collective-permute-done.1) | data formatting | bytes 32768 | tf_op jit(solution)/shard_map/ppermute | solution.py:322
  131.6 2.0 %copy.36.refs_1_ = f32[8,512,1]{2,1,0:T(8,128)} copy(f32[8,512,1]{1,0,2:T(8,128)S(1)} %collective-permute-done) | data formatting | bytes 32768 | tf_op jit(solution)/shard_map/ppermute | solution.py:321
  133.5 9.5 %shard_map.79 = (bf16[8,512,256]{2,1,0:T(8,128)(2,1)}, bf16[8,512,256]{2,1,0:T(8,128)(2,1)}) custom-call(f32[8,512,256]{2,1,0:T(8,128)} %bitcast.25, f32[8,512,1]{2,1,0:T(8,128)} %copy.36.refs_1_, f32[8,512,1]{2,1,0:T(8,128)} %copy.37.refs_2_), custom_call_target="tpu_custom_call" | custom-call | tf_op jit(solution)/shard_map/pallas_call | solution.py:154
  (21 shorter events, 0.6 us)
Async XLA Ops:
  2.1 37.6 %copy-start.1 = (s32[32]{0:T(128)S(1)}, s32[32]{0:T(128)}, u32[]{:S(2)}) copy-start(s32[32]{0:T(128)} %table_ref.1) | copy-start | bytes 388
  28.1 41.6 %all-to-all-start = ((bf16[128,2,16,256]{3,2,1,0:T(8,128)(2,1)}), bf16[128,2,16,256]{3,2,1,0:T(8,128)(2,1)S(1)}, u32[]{:S(2)}, u32[]{:S(2)}) async-start(bf16[128,2,16,256]{3,2,1,0:T(8,128)(2,1)} %bitcast.29), calls=%async_computation | async-start | bytes 4194304 | tf_op jit(solution)/shard_map/all_to_all | solution.py:274
  115.7 1.9 %copy-start = (f32[1,8,512,256]{3,2,1,0:T(8,128)}, f32[1,8,512,256]{3,2,1,0:T(8,128)S(1)}, u32[]{:S(2)}) copy-start(f32[1,8,512,256]{3,2,1,0:T(8,128)S(1)} %copy.44) | copy-start | bytes 12582916
  121.9 7.7 %collective-permute-start.1 = (f32[8,512,1]{1,0,2:T(8,128)S(1)}, f32[8,512,1]{1,0,2:T(8,128)S(1)}, u32[]{:S(2)}, u32[]{:S(2)}) collective-permute-start(f32[8,512,1]{1,0,2:T(8,128)S(1)} %copy.35), channel_id=1, source_target_pairs={{1,0},{2,1},{3,2},{5,4},{6,5},{7,6},{9,8},{10,9},{11,10},{13,12},{... | collective-permute-start | bytes 49160 | tf_op jit(solution)/shard_map/ppermute | solution.py:322
  124.8 6.7 %collective-permute-start = (f32[8,512,1]{1,0,2:T(8,128)S(1)}, f32[8,512,1]{1,0,2:T(8,128)S(1)}, u32[]{:S(2)}, u32[]{:S(2)}) collective-permute-start(f32[8,512,1]{1,0,2:T(8,128)S(1)} %copy.34), channel_id=1, source_target_pairs={{0,1},{1,2},{2,3},{4,5},{5,6},{6,7},{8,9},{9,10},{10,11},{12,13},{... | collective-permute-start | bytes 49160 | tf_op jit(solution)/shard_map/ppermute | solution.py:321

commit v3 on v2

--- a/solution.py
+++ b/solution.py
@@ -71,55 +71,65 @@
     return (weight_factor * (energy - spread)).astype(jnp.bfloat16)
 
 
-def calibrate_kernel(table_ref, bounds_ref, raw_ref, ped_ref, gain_ref, good_ref, out_ref):
-    module = pl.program_id(0)
-    raw = raw_ref[...]
-    code = raw // 2048
-    counts_adc = (raw % 2048).astype(jnp.float32)
-    base = jnp.where(code == 0, ped_ref[0], jnp.where(code == 1, ped_ref[1], ped_ref[2]))
-    scale = jnp.where(
-        code == 0,
-        gain_ref[0].astype(jnp.float32),
-        jnp.where(code == 1, gain_ref[1].astype(jnp.float32), gain_ref[2].astype(jnp.float32)),
-    )
-    weight_factor = good_ref[...].astype(jnp.float32)
-    energy = weight_factor * (counts_adc - base) / scale
-    cols = raw.shape[-1]
+def calibrate_kernel(group, table_ref, bounds_ref, raw_ref, ped_ref, gain_ref, good_ref, out_ref):
+    step = pl.program_id(0)
+    cols = raw_ref.shape[-1]
     columns = lax.broadcasted_iota(jnp.int32, (1, cols), 1)
-    band = jnp.zeros((1, cols), jnp.int32)
-    for j in range(BANDS - 1):
-        band = band + (columns >= bounds_ref[module * (BANDS - 1) + j]).astype(jnp.int32)
-    spread = jnp.zeros(energy.shape, jnp.float32)
-    for b in range(BANDS):
-        member = band == b
-        totals = jnp.sum(jnp.where(member, energy, 0.0), axis=-1, keepdims=True)
-        present = jnp.sum(jnp.where(member, weight_factor, 0.0), axis=-1, keepdims=True)
-        spread = jnp.where(member, totals / jnp.maximum(present, 1.0), spread)
-    corrected = (weight_factor * (energy - spread)).astype(jnp.bfloat16)
-    quarters = out_ref.shape[0]
+    quarters = out_ref.shape[1]
     width = cols // quarters
-    for q in range(quarters):
-        out_ref[q] = corrected[:, :, q * width : (q + 1) * width]
+    for inner in range(group):
+        module = step * group + inner
+        raw = raw_ref[:, inner]
+        code = raw // 2048
+        counts_adc = (raw % 2048).astype(jnp.float32)
+        base = jnp.where(
+            code == 0, ped_ref[0, inner], jnp.where(code == 1, ped_ref[1, inner], ped_ref[2, inner])
+        )
+        scale = jnp.where(
+            code == 0,
+            gain_ref[0, inner].astype(jnp.float32),
+            jnp.where(
+                code == 1,
+                gain_ref[1, inner].astype(jnp.float32),
+                gain_ref[2, inner].astype(jnp.float32),
+            ),
+        )
+        weight_factor = good_ref[inner].astype(jnp.float32)
+        energy = weight_factor * (counts_adc - base) / scale
+        band = jnp.zeros((1, cols), jnp.int32)
+        for j in range(BANDS - 1):
+            band = band + (columns >= bounds_ref[module * (BANDS - 1) + j]).astype(jnp.int32)
+        spread = jnp.zeros(energy.shape, jnp.float32)
+        for b in range(BANDS):
+            member = band == b
+            totals = jnp.sum(jnp.where(member, energy, 0.0), axis=-1, keepdims=True)
+            present = jnp.sum(jnp.where(member, weight_factor, 0.0), axis=-1, keepdims=True)
+            spread = jnp.where(member, totals / jnp.maximum(present, 1.0), spread)
+        corrected = (weight_factor * (energy - spread)).astype(jnp.bfloat16)
+        slot = table_ref[module]
+        for q in range(quarters):
+            out_ref[slot, q] = corrected[:, :, q * width : (q + 1) * width]
 
 
 def calibrate_send(raw, pedestal, gain, good, bounds, table, n_peak):
     frame_dev, mods, row_dev, cols = raw.shape
     width = cols // n_peak
+    group = 4
     grid_spec = pltpu.PrefetchScalarGridSpec(
         num_scalar_prefetch=2,
-        grid=(mods,),
+        grid=(mods // group,),
         in_specs=[
-            pl.BlockSpec((frame_dev, None, row_dev, cols), lambda m, t, b: (0, m, 0, 0)),
-            pl.BlockSpec((3, None, row_dev, cols), lambda m, t, b: (0, m, 0, 0)),
-            pl.BlockSpec((3, None, row_dev, cols), lambda m, t, b: (0, m, 0, 0)),
-            pl.BlockSpec((None, row_dev, cols), lambda m, t, b: (m, 0, 0)),
+            pl.BlockSpec((frame_dev, group, row_dev, cols), lambda m, t, b: (0, m, 0, 0)),
+            pl.BlockSpec((3, group, row_dev, cols), lambda m, t, b: (0, m, 0, 0)),
+            pl.BlockSpec((3, group, row_dev, cols), lambda m, t, b: (0, m, 0, 0)),
+            pl.BlockSpec((group, row_dev, cols), lambda m, t, b: (m, 0, 0)),
         ],
         out_specs=pl.BlockSpec(
-            (None, n_peak, frame_dev, row_dev, width), lambda m, t, b: (t[m], 0, 0, 0, 0)
+            (mods, n_peak, frame_dev, row_dev, width), lambda m, t, b: (0, 0, 0, 0, 0)
         ),
     )
     return pl.pallas_call(
-        calibrate_kernel,
+        lambda *refs: calibrate_kernel(group, *refs),
         grid_spec=grid_spec,
         out_shape=jax.ShapeDtypeStruct((mods, n_peak, frame_dev, row_dev, width), jnp.bfloat16),
     )(table, bounds.reshape(-1), raw, pedestal, gain, good)

time: 144 us -> 134 us (0.931)
  Pallas kernels: 53.1 us -> 43 us
    pallas_call x1, Pallas kernels: 26.1 us -> 15.9 us  [calibrate_send(): pl.pallas_call(lambda *refs: calibrate_kernel(group, *refs), grid_spec=gr...]
where the time goes in v3:
time: 134 us; the launch traced here: 133 us
  Pallas kernels  43 us (32%)
  local copies, waits for them, and re-layouts  19.8 us (15%)
  starting transfers between devices  18.6 us (14%)
  waiting for transfers between devices  17.5 us (13%)
  other arithmetic  17.2 us (13%)
  matrix products  16 us (12%)
    pallas_call x1, Pallas kernels, gather_sum(): pl.pallas_call(lambda *refs: gather_sum_kernel(n_calib, n_peak, *refs), o...  17.6 us
    all_to_all x1, waiting for transfers between devices, body(): got = lax.all_to_all(send, ('calib', 'peak'), 0, 0, tiled=True)  17.5 us
    pallas_call x1, Pallas kernels, calibrate_send(): pl.pallas_call(lambda *refs: calibrate_kernel(group, *refs), grid_spec=gr...  15.9 us
    dot_general x1, matrix products, body(): jnp.einsum('fk,kp->fp', pieces, hits_3, preferred_element_type=jnp.float32)  13.3 us
    all_to_all x1, starting transfers between devices, body(): got = lax.all_to_all(send, ('calib', 'peak'), 0, 0, tiled=True)  11.5 us
    pallas_call x1, Pallas kernels, score_outputs(): pl.pallas_call(lambda *refs: laplace_kernel(n_peak, *refs), grid=(frames,...  9.48 us
    ppermute x1, starting transfers between devices, body(): left = lax.ppermute(score[:, :, width_here - 1:], 'peak', fwd)  4.71 us
    convert_element_type x1, other arithmetic, body(): hits = hits.astype(jnp.bfloat16)  4.58 us
  transfers between devices with their start and end apart: 3, of which 1 were waited for; matrix products, arithmetic and copies ran while one was open for 11% of the time, Pallas kernels for 0%

profile of v3, /device:TPU:1, one launch (start us, length us, event | category | flops | bytes accessed | tf_op | source)
XLA Modules:
  0.0 132.9 jit_solution(11678429787721510439)
XLA Ops:
  0.6 0.8 copy.31
  1.4 0.7 reshape.182.refs_1_
  2.1 15.9 %shard_map.77 = bf16[32,4,2,16,256]{4,3,2,1,0:T(8,128)(2,1)} custom-call(s32[32]{0:T(128)} %refs_0_.1, s32[224]{0:T(256)} %reshape.182.refs_1_, s32[2,32,16,1024]{3,2,1,0:T(8,128)} %refs_2_.1, f32[3,32,16,1024]{3,2,1,0:T(8,128)} %refs_3_.1, bf16[3,32,16,1024]{3,2,1,0:T(8,128)(2,1)} %refs_4_.1, s32[32,16,1024]{2,1,0:T(8,128)} %refs_5_.1), custom_call_target="tpu_custom_call" | custom-call | tf_op jit(solution)/shard_map/pallas_call | solution.py:131
  18.0 11.5 %all-to-all-start = ((bf16[128,2,16,256]{3,2,1,0:T(8,128)(2,1)}), bf16[128,2,16,256]{3,2,1,0:T(8,128)(2,1)S(1)}, u32[]{:S(2)}, u32[]{:S(2)}) async-start(bf16[128,2,16,256]{3,2,1,0:T(8,128)(2,1)} %bitcast.29), calls=%async_computation | async-start | bytes 4194304 | tf_op jit(solution)/shard_map/all_to_all | solution.py:284
  29.8 1.7 %convert_reduce_fusion = s32[512,256]{1,0:T(8,128)S(1)} fusion(s32[512,256]{1,0:T(8,128)S(1)} %broadcast_add_fusion.1, s32[32]{0:T(128)S(1)} %multiply_multiply_fusion.1), kind=kLoop, calls=%fused_computation.10 | loop fusion | flops 12451840 | bytes 1048704 | tf_op jit(solution)/shard_map/reduce_sum | solution.py:45
  31.5 0.3 copy.40
  31.8 4.6 %convert_convert_fusion = bf16[32,131072]{1,0:T(8,128)(2,1)} fusion(s32[131072]{0:T(1024)S(1)} %bitcast.30), kind=kLoop, calls=%fused_computation.8 | loop fusion | flops 12582912 | bytes 8912896 | tf_op jit(solution)/shard_map/convert_element_type | solution.py:290
  36.6 1.1 constant_dynamic-slice_fusion
  37.8 0.1 broadcast_add_fusion
  37.9 1.7 %convert_reduce_fusion.1 = s32[32,16,256]{2,1,0:T(8,128)S(1)} fusion(s32[32,16,256]{2,1,0:T(8,128)S(1)} %broadcast_add_fusion, s32[31]{0:T(128)S(1)} %multiply_multiply_fusion), kind=kLoop, calls=%fused_computation.11 | loop fusion | flops 12058624 | bytes 1048700 | tf_op jit(solution)/shard_map/reduce_sum | solution.py:34
  39.6 2.5 %select_reduce_fusion = s32[32]{0:T(128)S(1)} fusion(s32[32,16,256]{2,1,0:T(8,128)S(1)} %constant_dynamic-slice_fusion, s32[32,16,256]{2,1,0:T(8,128)S(1)} %convert_reduce_fusion.1), kind=kLoop, calls=%fused_computation.6 | loop fusion | flops 12582880 | bytes 1048704 | tf_op jit(solution)/shard_map/reduce_sum | solution.py:198
  42.1 17.5 %all-to-all-done = bf16[128,2,16,256]{3,2,1,0:T(8,128)(2,1)S(1)} async-done(((bf16[128,2,16,256]{3,2,1,0:T(8,128)(2,1)}), bf16[128,2,16,256]{3,2,1,0:T(8,128)(2,1)S(1)}, u32[]{:S(2)}, u32[]{:S(2)}) %all-to-all-start) | async-done | bytes 2097184 | tf_op jit(solution)/shard_map/all_to_all | solution.py:284
  59.6 1.5 %copy.45 = bf16[32,4,2,16,256]{4,3,0,2,1:T(8,128)(2,1)} copy(bf16[32,4,2,16,256]{4,3,2,1,0:T(8,128)(2,1)S(1)} %bitcast.27) | data formatting | bytes 4194304 | tf_op jit(solution)/shard_map/reshape | solution.py:285
  61.1 2.5 %reshape_reshape.3 = bf16[8,131072]{1,0:T(8,128)(2,1)S(1)} reshape(bf16[4,2,32,16,256]{4,3,2,1,0:T(8,128)(2,1)} %bitcast.28) | data formatting | bytes 4194304 | tf_op jit(solution)/shard_map/reshape;reshape | solution.py:291
  63.7 0.7 reduce-precision_convert_fusion
  64.4 2.7 %fusion.6 = f32[24,32]{1,0:T(8,128)S(1)} fusion(bf16[8,131072]{1,0:T(8,128)(2,1)S(1)} %get-tuple-element.31, bf16[8,131072]{1,0:T(8,128)(2,1)S(1)} %get-tuple-element.30, bf16[8,131072]{1,0:T(8,128)(2,1)S(1)} %reshape_reshape.3, s32[131072]{0:T(1024)S(1)} %bitcast.31), kind=kOutput, calls=%fused_computation.12 | convolution fusion | flops 232783872 | bytes 6818816 | tf_op jit(solution)/shard_map/fp,kp->fk/dot_general | solution.py:298
  67.1 0.7 fusion.15.refs_0_
  67.8 17.6 %shard_map.78 = f32[8,128]{1,0:T(8,128)} custom-call(f32[8,128]{1,0:T(8,128)} %fusion.15.refs_0_), custom_call_target="tpu_custom_call" | custom-call | tf_op jit(solution)/shard_map/pallas_call | solution.py:252
  85.3 0.8 slice_bitcast_fusion
  86.1 0.8 slice_divide_fusion
  87.0 13.3 %fusion = f32[16,131072]{1,0:T(8,128)} fusion(bf16[32,131072]{1,0:T(8,128)(2,1)} %convert_convert_fusion, bf16[16,32]{1,0:T(8,128)(2,1)S(1)} %get-tuple-element.36, bf16[16,32]{1,0:T(8,128)(2,1)S(1)} %get-tuple-element.35, bf16[16,32]{1,0:T(8,128)(2,1)S(1)} %get-tuple-element.34), kind=kOutput, calls=%fused_computation | convolution fusion | flops 478159872 | bytes 16780288 | tf_op jit(solution)/shard_map/fk,kp->fp/dot_general | solution.py:325
  100.2 4.0 %fusion.12 = f32[8,131072]{1,0:T(8,128)S(1)} fusion(bf16[8,131072]{1,0:T(8,128)(2,1)S(1)} %reshape_reshape.3, f32[16,131072]{1,0:T(8,128)} %fusion), kind=kLoop, calls=%fused_computation.22 | loop fusion | flops 3145728 | bytes 14680064 | tf_op jit(solution)/shard_map/div | solution.py:328
  104.2 1.4 %copy.44 = f32[1,8,512,256]{3,2,1,0:T(8,128)S(1)} copy(f32[1,8,512,256]{3,1,2,0:T(8,128)S(1)} %bitcast.26) | data formatting | bytes 8388608
  105.6 1.9 %copy-done = f32[1,8,512,256]{3,2,1,0:T(8,128)} copy-done((f32[1,8,512,256]{3,2,1,0:T(8,128)}, f32[1,8,512,256]{3,2,1,0:T(8,128)S(1)}, u32[]{:S(2)}) %copy-start) | copy-done | bytes 4194328
  107.5 2.0 %fusion.26 = (f32[8,512,1]{2,1,0:T(8,128)}, f32[8,512,1]{2,1,0:T(8,128)S(1)}) fusion(f32[8,512,256]{2,1,0:T(8,128)S(1)} %bitcast.24), kind=kLoop, calls=%fused_computation.68 | loop fusion | bytes 65536 | tf_op jit(solution)/shard_map/slice | solution.py:332
  109.6 2.2 %copy.35 = f32[8,512,1]{1,0,2:T(8,128)S(1)} copy(f32[8,512,1]{2,1,0:T(8,128)} %get-tuple-element.28) | data formatting | bytes 32768 | tf_op jit(solution)/shard_map/slice | solution.py:332
  111.8 2.4 %collective-permute-start.1 = (f32[8,512,1]{1,0,2:T(8,128)S(1)}, f32[8,512,1]{1,0,2:T(8,128)S(1)}, u32[]{:S(2)}, u32[]{:S(2)}) collective-permute-start(f32[8,512,1]{1,0,2:T(8,128)S(1)} %copy.35), channel_id=1, source_target_pairs={{1,0},{2,1},{3,2},{5,4},{6,5},{7,6},{9,8},{10,9},{11,10},{13,12},{... | collective-permute-start | bytes 49160 | tf_op jit(solution)/shard_map/ppermute | solution.py:332
  114.1 0.6 copy.34
  114.7 4.7 %collective-permute-start = (f32[8,512,1]{1,0,2:T(8,128)S(1)}, f32[8,512,1]{1,0,2:T(8,128)S(1)}, u32[]{:S(2)}, u32[]{:S(2)}) collective-permute-start(f32[8,512,1]{1,0,2:T(8,128)S(1)} %copy.34), channel_id=1, source_target_pairs={{0,1},{1,2},{2,3},{4,5},{5,6},{6,7},{8,9},{9,10},{10,11},{12,13},{... | collective-permute-start | bytes 49160 | tf_op jit(solution)/shard_map/ppermute | solution.py:331
  119.5 2.0 %copy.37.refs_2_ = f32[8,512,1]{2,1,0:T(8,128)} copy(f32[8,512,1]{1,0,2:T(8,128)S(1)} %collective-permute-done.1) | data formatting | bytes 32768 | tf_op jit(solution)/shard_map/ppermute | solution.py:332
  121.5 2.0 %copy.36.refs_1_ = f32[8,512,1]{2,1,0:T(8,128)} copy(f32[8,512,1]{1,0,2:T(8,128)S(1)} %collective-permute-done) | data formatting | bytes 32768 | tf_op jit(solution)/shard_map/ppermute | solution.py:331
  123.4 9.5 %shard_map.79 = (bf16[8,512,256]{2,1,0:T(8,128)(2,1)}, bf16[8,512,256]{2,1,0:T(8,128)(2,1)}) custom-call(f32[8,512,256]{2,1,0:T(8,128)} %bitcast.25, f32[8,512,1]{2,1,0:T(8,128)} %copy.36.refs_1_, f32[8,512,1]{2,1,0:T(8,128)} %copy.37.refs_2_), custom_call_target="tpu_custom_call" | custom-call | tf_op jit(solution)/shard_map/pallas_call | solution.py:164
  (21 shorter events, 0.6 us)
Async XLA Ops:
  2.1 27.5 %copy-start.1 = (s32[32]{0:T(128)S(1)}, s32[32]{0:T(128)}, u32[]{:S(2)}) copy-start(s32[32]{0:T(128)} %refs_0_.1) | copy-start | bytes 388
  18.0 41.6 %all-to-all-start = ((bf16[128,2,16,256]{3,2,1,0:T(8,128)(2,1)}), bf16[128,2,16,256]{3,2,1,0:T(8,128)(2,1)S(1)}, u32[]{:S(2)}, u32[]{:S(2)}) async-start(bf16[128,2,16,256]{3,2,1,0:T(8,128)(2,1)} %bitcast.29), calls=%async_computation | async-start | bytes 4194304 | tf_op jit(solution)/shard_map/all_to_all | solution.py:284
  105.6 1.9 %copy-start = (f32[1,8,512,256]{3,2,1,0:T(8,128)}, f32[1,8,512,256]{3,2,1,0:T(8,128)S(1)}, u32[]{:S(2)}) copy-start(f32[1,8,512,256]{3,2,1,0:T(8,128)S(1)} %copy.44) | copy-start | bytes 12582916
  111.8 7.7 %collective-permute-start.1 = (f32[8,512,1]{1,0,2:T(8,128)S(1)}, f32[8,512,1]{1,0,2:T(8,128)S(1)}, u32[]{:S(2)}, u32[]{:S(2)}) collective-permute-start(f32[8,512,1]{1,0,2:T(8,128)S(1)} %copy.35), channel_id=1, source_target_pairs={{1,0},{2,1},{3,2},{5,4},{6,5},{7,6},{9,8},{10,9},{11,10},{13,12},{... | collective-permute-start | bytes 49160 | tf_op jit(solution)/shard_map/ppermute | solution.py:332
  114.7 6.7 %collective-permute-start = (f32[8,512,1]{1,0,2:T(8,128)S(1)}, f32[8,512,1]{1,0,2:T(8,128)S(1)}, u32[]{:S(2)}, u32[]{:S(2)}) collective-permute-start(f32[8,512,1]{1,0,2:T(8,128)S(1)} %copy.34), channel_id=1, source_target_pairs={{0,1},{1,2},{2,3},{4,5},{5,6},{6,7},{8,9},{9,10},{10,11},{12,13},{... | collective-permute-start | bytes 49160 | tf_op jit(solution)/shard_map/ppermute | solution.py:331

commit v4 on v3

--- a/solution.py
+++ b/solution.py
@@ -135,9 +135,20 @@
     )(table, bounds.reshape(-1), raw, pedestal, gain, good)
 
 
-def laplace_kernel(n_peak, score_ref, left_ref, right_ref, snr_ref, bent_ref):
-    score = score_ref[...]
-    rows, cols = score.shape
+def score_kernel(n_peak, levels, low_ref, mean_ref, rms_ref, frame_ref, cycle_ref, left_ref, right_ref, snr_ref, bent_ref):
+    frame_pos = pl.program_id(0)
+    cycle = cycle_ref[...]
+    values = frame_ref[...].astype(jnp.float32)
+    rows, cols = values.shape
+    tops = mean_ref.shape[1] - 1
+    pixel_mean = jnp.zeros((rows, cols), jnp.float32)
+    pixel_rms = jnp.ones((rows, cols), jnp.float32)
+    for j in range(levels):
+        level = jnp.minimum(low_ref[0] + j, tops)
+        hit = cycle == level
+        pixel_mean = jnp.where(hit, mean_ref[frame_pos, level], pixel_mean)
+        pixel_rms = jnp.where(hit, rms_ref[frame_pos, level], pixel_rms)
+    score = (values - pixel_mean) / pixel_rms
     peak_pos = lax.axis_index("peak")
     row_ids = lax.broadcasted_iota(jnp.int32, (rows, cols), 0)
     col_ids = lax.broadcasted_iota(jnp.int32, (rows, cols), 1)
@@ -157,17 +168,24 @@
     bent_ref[...] = total.astype(bent_ref.dtype)
 
 
-def score_outputs(score, left, right, n_peak):
-    frames, rows, cols = score.shape
-    block = pl.BlockSpec((None, rows, cols), lambda f: (f, 0, 0))
-    edge = pl.BlockSpec((None, rows, 1), lambda f: (f, 0, 0))
+def score_outputs(frame, cycle, cycle_average, cycle_rms, left, right, n_peak):
+    frames, rows, cols = frame.shape
+    span = (rows * rows + cols * cols) ** 0.5
+    levels = min(CYCLES, int(span // CYCLE_W) + 3)
+    low = jnp.min(cycle).reshape(1)
+    block = pl.BlockSpec((None, rows, cols), lambda f, *_: (f, 0, 0))
+    edge = pl.BlockSpec((None, rows, 1), lambda f, *_: (f, 0, 0))
+    grid_spec = pltpu.PrefetchScalarGridSpec(
+        num_scalar_prefetch=3,
+        grid=(frames,),
+        in_specs=[block, pl.BlockSpec((rows, cols), lambda f, *_: (0, 0)), edge, edge],
+        out_specs=[block, block],
+    )
     return pl.pallas_call(
-        lambda *refs: laplace_kernel(n_peak, *refs),
-        grid=(frames,),
-        in_specs=[block, edge, edge],
-        out_specs=[block, block],
-        out_shape=[jax.ShapeDtypeStruct(score.shape, jnp.bfloat16)] * 2,
-    )(score, left, right)
+        lambda *refs: score_kernel(n_peak, levels, *refs),
+        grid_spec=grid_spec,
+        out_shape=[jax.ShapeDtypeStruct(frame.shape, jnp.bfloat16)] * 2,
+    )(low, cycle_average, cycle_rms, frame, cycle, left, right)
 
 
 def laplace(padded):
@@ -286,8 +304,13 @@
     frame = jnp.transpose(got, (1, 2, 0, 3, 4)).reshape(frames_all, mrows, width_here)
     slot = lax.axis_index("calib")
     col_dst = lax.axis_index("peak") * width_here + jnp.arange(width_here, dtype=jnp.int32)
-    hits = cycle_onehot(slot, jnp.arange(mrows, dtype=jnp.int32), col_dst, mrows, slot_rows)
-    hits = hits.astype(jnp.bfloat16)
+    ypos = slot // SLOT_C * mrows + jnp.arange(mrows, dtype=jnp.int32)
+    xpos = slot % SLOT_C * COLS + col_dst
+    dy_two = 2 * ypos + 1 - slot_rows * mrows
+    dx_two = 2 * xpos + 1 - SLOT_C * COLS
+    cycle = cycle_index(dy_two[:, None] * dy_two[:, None] + dx_two[None, :] * dx_two[None, :])
+    levels = jnp.arange(CYCLES, dtype=jnp.int32)
+    hits = (cycle.reshape(1, -1) == levels[:, None]).astype(jnp.bfloat16)
     pixels = frame.reshape(frames_all, -1)
     values = pixels.astype(jnp.float32)
     square = values * values
@@ -313,24 +336,16 @@
     second = summed[:, CYCLES : 2 * CYCLES]
     present_flag = summed[0, 2 * CYCLES : 3 * CYCLES]
     cycle_average, cycle_rms = cycle_stats(first, second, present_flag)
-    table_f32 = jnp.concatenate([cycle_average, cycle_rms], axis=0)
-    top_1 = lax.reduce_precision(table_f32, exponent_bits=8, mantissa_bits=7)
-    rest = table_f32 - top_1
-    top_2 = lax.reduce_precision(rest, exponent_bits=8, mantissa_bits=7)
-    piece_1 = top_1.astype(jnp.bfloat16)
-    piece_2 = top_2.astype(jnp.bfloat16)
-    piece_3 = (rest - top_2).astype(jnp.bfloat16)
-    pieces = jnp.concatenate([piece_1, piece_2, piece_3], axis=1)
-    hits_3 = jnp.concatenate([hits, hits, hits], axis=0)
-    lookup = jnp.einsum("fk,kp->fp", pieces, hits_3, preferred_element_type=jnp.float32)
-    pixel_mean = lookup[:frames_all]
-    pixel_rms = lookup[frames_all:]
-    score = ((values - pixel_mean) / pixel_rms).reshape(frames_all, mrows, width_here)
+    edge_cycle = jnp.stack([cycle[:, width_here - 1], cycle[:, 0]], axis=1)
+    edge_values = jnp.stack([frame[:, :, width_here - 1], frame[:, :, 0]], axis=2)
+    edge_mean = jnp.take(cycle_average, edge_cycle, axis=1)
+    edge_rms = jnp.take(cycle_rms, edge_cycle, axis=1)
+    edge_score = (edge_values.astype(jnp.float32) - edge_mean) / edge_rms
     fwd = [(i, i + 1) for i in range(n_peak - 1)]
     bwd = [(i + 1, i) for i in range(n_peak - 1)]
-    left = lax.ppermute(score[:, :, width_here - 1 :], "peak", fwd)
-    right = lax.ppermute(score[:, :, :1], "peak", bwd)
-    snr, bent = score_outputs(score, left, right, n_peak)
+    left = lax.ppermute(edge_score[:, :, :1], "peak", fwd)
+    right = lax.ppermute(edge_score[:, :, 1:], "peak", bwd)
+    snr, bent = score_outputs(frame, cycle, cycle_average, cycle_rms, left, right, n_peak)
     return (snr[:, None], bent[:, None])
 
 

time: 134 us -> 128 us (0.955)
  matrix products: 16 us -> 3.28 us
  other arithmetic: 17.2 us -> 10.9 us
  local copies, waits for them, and re-layouts: 19.8 us -> 25.8 us
  waiting for transfers between devices: 17.5 us -> 22.5 us
  Pallas kernels: 43 us -> 46.7 us
  starting transfers between devices: 18.6 us -> 16.8 us
    dot_general x1 -> x0, matrix products: 13.3 us -> none  [body(): jnp.einsum('fk,kp->fp', pieces, hits_3, preferred_element_type=jnp.float32)]
    gather x0 -> x4, local copies, waits for them, and re-layouts: none -> 5.96 us  [the longest x2 2.99 us: body(): edge_rms = jnp.take(cycle_rms, edge_cycle, axis=1)]
    div x2 -> x1, other arithmetic: 4.85 us -> 0.03 us  [body(): edge_score = (edge_values.astype(jnp.float32) - edge_mean) / edge_rms]
    convert_element_type x2 -> x0, other arithmetic: 4.59 us -> none  [the longest x1 4.58 us: body(): hits = hits.astype(jnp.bfloat16)]
    pallas_call x1, Pallas kernels: 9.48 us -> 13.4 us  [score_outputs(): pl.pallas_call(lambda *refs: score_kernel(n_peak, levels, *refs), grid_sp...]
    all_to_all x1, waiting for transfers between devices: 17.5 us -> 20.7 us  [body(): got = lax.all_to_all(send, ('calib', 'peak'), 0, 0, tiled=True)]
    ppermute x2, waiting for transfers between devices: 0.01 us -> 1.86 us  [the longest x1 1.86 us: body(): right = lax.ppermute(edge_score[:, :, 1:], 'peak', bwd)]
    transpose x0 -> x1, local copies, waits for them, and re-layouts: none -> 1.78 us  [body(): jnp.transpose(got, (1, 2, 0, 3, 4)).reshape(frames_all, mrows, width_here)]
  transfers between devices with their start and end apart: 3 -> 3, of which waited for: 1 -> 2; matrix products, arithmetic and copies ran while one was open for 11% -> 9% of each run, Pallas kernels for 0% -> 0%
where the time goes in v4:
time: 128 us; the launch traced here: 127 us
  Pallas kernels  46.7 us (36%)
  local copies, waits for them, and re-layouts  25.8 us (20%)
  waiting for transfers between devices  22.5 us (18%)
  starting transfers between devices  16.8 us (13%)
  other arithmetic  10.9 us (9%)
  matrix products  3.28 us (3%)
    all_to_all x1, waiting for transfers between devices, body(): got = lax.all_to_all(send, ('calib', 'peak'), 0, 0, tiled=True)  20.7 us
    pallas_call x1, Pallas kernels, gather_sum(): pl.pallas_call(lambda *refs: gather_sum_kernel(n_calib, n_peak, *refs), o...  17.5 us
    pallas_call x1, Pallas kernels, calibrate_send(): pl.pallas_call(lambda *refs: calibrate_kernel(group, *refs), grid_spec=gr...  15.8 us
    pallas_call x1, Pallas kernels, score_outputs(): pl.pallas_call(lambda *refs: score_kernel(n_peak, levels, *refs), grid_sp...  13.4 us
    all_to_all x1, starting transfers between devices, body(): got = lax.all_to_all(send, ('calib', 'peak'), 0, 0, tiled=True)  11.5 us
    slice x2, local copies, waits for them, and re-layouts, body(): frame[:, :, width_here - 1]  3.57 us
    ppermute x1, starting transfers between devices, body(): left = lax.ppermute(edge_score[:, :, :1], 'peak', fwd)  3.4 us
    reduce_sum x2, other arithmetic, cycle_index(): return jnp.sum((dist[..., None] >= lows).astype(jnp.int32), axis=-1)  3.34 us
  transfers between devices with their start and end apart: 3, of which 2 were waited for; matrix products, arithmetic and copies ran while one was open for 9% of the time, Pallas kernels for 0%

profile of v4, /device:TPU:1, one launch (start us, length us, event | category | flops | bytes accessed | tf_op | source)
XLA Modules:
  0.0 127.0 jit_solution(5247914193803375929)
XLA Ops:
  0.6 0.8 copy.71
  1.4 0.7 reshape.185.refs_1_
  2.1 15.8 %shard_map.77 = bf16[32,4,2,16,256]{4,3,2,1,0:T(8,128)(2,1)} custom-call(s32[32]{0:T(128)} %refs_0_.1, s32[224]{0:T(256)} %reshape.185.refs_1_, s32[2,32,16,1024]{3,2,1,0:T(8,128)} %refs_2_.1, f32[3,32,16,1024]{3,2,1,0:T(8,128)} %refs_3_.1, bf16[3,32,16,1024]{3,2,1,0:T(8,128)(2,1)} %refs_4_.1, s32[32,16,1024]{2,1,0:T(8,128)} %refs_5_.1), custom_call_target="tpu_custom_call" | custom-call | tf_op jit(solution)/shard_map/pallas_call | solution.py:131
  17.9 11.5 %all-to-all-start = ((bf16[128,2,16,256]{3,2,1,0:T(8,128)(2,1)}), bf16[128,2,16,256]{3,2,1,0:T(8,128)(2,1)S(1)}, u32[]{:S(2)}, u32[]{:S(2)}) async-start(bf16[128,2,16,256]{3,2,1,0:T(8,128)(2,1)} %bitcast.34), calls=%async_computation | async-start | bytes 4194304 | tf_op jit(solution)/shard_map/all_to_all | solution.py:302
  29.7 1.6 %convert_reduce_fusion.1.refs_4_ = s32[512,256]{1,0:T(8,128)S(1)} fusion(s32[512,256]{1,0:T(8,128)S(1)} %broadcast_add_fusion.1, s32[31]{0:T(128)S(1)} %multiply_multiply_fusion), kind=kLoop, calls=%fused_computation.7 | loop fusion | flops 12058624 | bytes 1048700 | tf_op jit(solution)/shard_map/reduce_sum | solution.py:34
  31.6 1.1 copy.89
  33.1 0.2 reshape.209
  33.4 1.1 constant_dynamic-slice_fusion
  34.7 1.7 %convert_reduce_fusion = s32[32,16,256]{2,1,0:T(8,128)S(1)} fusion(s32[32,16,256]{2,1,0:T(8,128)S(1)} %broadcast_add_fusion, s32[31]{0:T(128)S(1)} %multiply_multiply_fusion), kind=kLoop, calls=%fused_computation.6 | loop fusion | flops 12058624 | bytes 1048700 | tf_op jit(solution)/shard_map/reduce_sum | solution.py:34
  36.4 2.5 %select_reduce_fusion = s32[32]{0:T(128)S(1)} fusion(s32[32,16,256]{2,1,0:T(8,128)S(1)} %constant_dynamic-slice_fusion, s32[32,16,256]{2,1,0:T(8,128)S(1)} %convert_reduce_fusion), kind=kLoop, calls=%fused_computation.2 | loop fusion | flops 12582880 | bytes 1048704 | tf_op jit(solution)/shard_map/reduce_sum | solution.py:216
  38.8 20.7 %all-to-all-done = bf16[128,2,16,256]{3,2,1,0:T(8,128)(2,1)S(1)} async-done(((bf16[128,2,16,256]{3,2,1,0:T(8,128)(2,1)}), bf16[128,2,16,256]{3,2,1,0:T(8,128)(2,1)S(1)}, u32[]{:S(2)}, u32[]{:S(2)}) %all-to-all-start) | async-done | bytes 2097184 | tf_op jit(solution)/shard_map/all_to_all | solution.py:302
  59.5 1.3 %copy-done.3 = bf16[128,2,16,256]{3,2,1,0:T(8,128)(2,1)} copy-done((bf16[128,2,16,256]{3,2,1,0:T(8,128)(2,1)}, bf16[128,2,16,256]{3,2,1,0:T(8,128)(2,1)S(1)}, u32[]{:S(2)}) %copy-start.3) | copy-done | bytes 2097176
  60.8 1.8 %copy.72 = bf16[4,2,32,16,256]{4,3,2,1,0:T(8,128)(2,1)S(1)} copy(bf16[4,2,32,16,256]{4,3,1,0,2:T(8,128)(2,1)} %bitcast.33) | data formatting | bytes 4194304 | tf_op jit(solution)/shard_map/transpose | solution.py:304
  62.6 2.3 %reshape_reshape.3 = bf16[8,131072]{1,0:T(8,128)(2,1)} reshape(bf16[4,2,32,16,256]{4,3,2,1,0:T(8,128)(2,1)S(1)} %copy.72) | data formatting | bytes 4194304 | tf_op jit(solution)/shard_map/reshape;reshape | solution.py:314
  64.9 1.8 %fusion.13 = (bf16[8,512,1]{2,1,0:T(8,128)(2,1)}, bf16[8,512,1]{2,1,0:T(8,128)(2,1)}) fusion(bf16[8,512,256]{2,1,0:T(8,128)(2,1)S(1)} %bitcast.28), kind=kLoop, calls=%fused_computation.51 | loop fusion | bytes 32768 | tf_op jit(solution)/shard_map/slice | solution.py:340
  66.7 1.7 %copy.75 = bf16[8,512,1]{1,0,2:T(8,128)(2,1)S(1)} copy(bf16[8,512,1]{2,1,0:T(8,128)(2,1)} %get-tuple-element.33) | data formatting | bytes 16384 | tf_op jit(solution)/shard_map/slice | solution.py:340
  68.5 1.6 %copy.76 = bf16[8,512,1]{1,0,2:T(8,128)(2,1)S(1)} copy(bf16[8,512,1]{2,1,0:T(8,128)(2,1)} %get-tuple-element.34) | data formatting | bytes 16384 | tf_op jit(solution)/shard_map/slice | solution.py:340
  70.1 2.3 %reduce-precision_convert_fusion = (bf16[8,131072]{1,0:T(8,128)(2,1)S(1)}, bf16[8,131072]{1,0:T(8,128)(2,1)S(1)}) fusion(bf16[8,131072]{1,0:T(8,128)(2,1)} %reshape_reshape.3), kind=kLoop, calls=%fused_computation.15 | loop fusion | flops 6291456 | bytes 6291456 | tf_op jit(solution)/shard_map/convert_element_type | solution.py:318
  72.4 3.3 %fusion = f32[24,32]{1,0:T(8,128)S(1)} fusion(s32[131072]{0:T(1024)S(1)} %bitcast.35, bf16[8,131072]{1,0:T(8,128)(2,1)S(1)} %get-tuple-element.36, bf16[8,131072]{1,0:T(8,128)(2,1)S(1)} %get-tuple-element.35, bf16[8,131072]{1,0:T(8,128)(2,1)S(1)} %copy-done.2), kind=kOutput, calls=%fused_computation.5 | convolution fusion | flops 224395264 | bytes 6818816 | tf_op jit(solution)/shard_map/fp,kp->fk/dot_general | solution.py:321
  75.6 0.7 fusion.8.refs_0_
  76.3 17.5 %shard_map.78 = f32[8,128]{1,0:T(8,128)} custom-call(f32[8,128]{1,0:T(8,128)} %fusion.8.refs_0_), custom_call_target="tpu_custom_call" | custom-call | tf_op jit(solution)/shard_map/pallas_call | solution.py:270
  93.9 0.7 slice_bitcast_fusion
  94.6 0.8 add_sqrt_fusion
  95.6 2.8 %gather_fusion = f32[1024,8]{1,0:T(8,128)S(1)} fusion(f32[8,32]{0,1:T(8,128)S(1)} %copy.80, s32[1024]{0:T(1024)S(1)} %broadcast_clamp_fusion), kind=kCustom, calls=%fused_computation.clone | custom fusion | bytes 69632 | tf_op jit(solution)/shard_map/jit(_take)/gather | solution.py:341
  98.6 2.8 %gather_fusion.1 = f32[1024,8]{1,0:T(8,128)S(1)} fusion(f32[8,32]{0,1:T(8,128)S(1)} %copy.83, s32[1024]{0:T(1024)S(1)} %broadcast_clamp_fusion), kind=kCustom, calls=%fused_computation.1.clone | custom fusion | bytes 69632 | tf_op jit(solution)/shard_map/jit(_take)/gather | solution.py:342
  101.7 3.4 %collective-permute-start = (f32[8,512,1]{1,0,2:T(8,128)S(1)}, f32[8,512,1]{1,0,2:T(8,128)S(1)}, u32[]{:S(2)}, u32[]{:S(2)}) collective-permute-start(f32[8,512,1]{1,0,2:T(8,128)S(1)} %get-tuple-element.40), channel_id=1, source_target_pairs={{0,1},{1,2},{2,3},{4,5},{5,6},{6,7},{8,9},{9,10},{10,11},{12,13},{... | collective-permute-start | bytes 49160 | tf_op jit(solution)/shard_map/ppermute | solution.py:346
  105.1 1.9 %collective-permute-start.1 = (f32[8,512,1]{1,0,2:T(8,128)S(1)}, f32[8,512,1]{1,0,2:T(8,128)S(1)}, u32[]{:S(2)}, u32[]{:S(2)}) collective-permute-start(f32[8,512,1]{1,0,2:T(8,128)S(1)} %get-tuple-element.39), channel_id=1, source_target_pairs={{1,0},{2,1},{3,2},{5,4},{6,5},{7,6},{9,8},{10,9},{11,10},{13,12},{... | collective-permute-start | bytes 49160 | tf_op jit(solution)/shard_map/ppermute | solution.py:347
  107.0 0.8 reduce_min.9
  107.8 2.0 %copy.85.refs_5_ = f32[8,512,1]{2,1,0:T(8,128)} copy(f32[8,512,1]{1,0,2:T(8,128)S(1)} %collective-permute-done) | data formatting | bytes 32768 | tf_op jit(solution)/shard_map/ppermute | solution.py:346
  109.8 1.9 %collective-permute-done.1 = f32[8,512,1]{1,0,2:T(8,128)S(1)} collective-permute-done((f32[8,512,1]{1,0,2:T(8,128)S(1)}, f32[8,512,1]{1,0,2:T(8,128)S(1)}, u32[]{:S(2)}, u32[]{:S(2)}) %collective-permute-start.1) | collective-permute-done | bytes 16416 | tf_op jit(solution)/shard_map/ppermute | solution.py:347
  111.6 2.0 %copy.86.refs_6_ = f32[8,512,1]{2,1,0:T(8,128)} copy(f32[8,512,1]{1,0,2:T(8,128)S(1)} %collective-permute-done.1) | data formatting | bytes 32768 | tf_op jit(solution)/shard_map/ppermute | solution.py:347
  113.6 13.4 %shard_map.79 = (bf16[8,512,256]{2,1,0:T(8,128)(2,1)}, bf16[8,512,256]{2,1,0:T(8,128)(2,1)}) custom-call(s32[1]{0:T(128)} %bitcast.refs_0_, f32[8,32]{1,0:T(8,128)} %copy-done.6, f32[8,32]{1,0:T(8,128)} %copy-done.5, bf16[8,512,256]{2,1,0:T(8,128)(2,1)} %bitcast.29, s32[512,256]{1,0:T(8,128)} %copy-done.1, f32[8,512,1]{2,1,0:T(8,128)} %copy.85.refs_5_, ...), custom_call_target="tpu_custom_call" | custom-call | tf_op jit(solution)/shard_map/pallas_call | solution.py:184
  (42 shorter events, 1.7 us)
Async XLA Ops:
  17.9 11.5 %copy-start.7 = (s32[32]{0:T(128)S(1)}, s32[32]{0:T(128)}, u32[]{:S(2)}) copy-start(s32[32]{0:T(128)} %refs_0_.1) | copy-start | bytes 388
  17.9 41.6 %all-to-all-start = ((bf16[128,2,16,256]{3,2,1,0:T(8,128)(2,1)}), bf16[128,2,16,256]{3,2,1,0:T(8,128)(2,1)S(1)}, u32[]{:S(2)}, u32[]{:S(2)}) async-start(bf16[128,2,16,256]{3,2,1,0:T(8,128)(2,1)} %bitcast.34), calls=%async_computation | async-start | bytes 4194304 | tf_op jit(solution)/shard_map/all_to_all | solution.py:302
  31.3 75.7 %copy-start.1 = (s32[512,256]{1,0:T(8,128)}, s32[512,256]{1,0:T(8,128)S(1)}, u32[]{:S(2)}) copy-start(s32[512,256]{1,0:T(8,128)S(1)} %convert_reduce_fusion.1.refs_4_) | copy-start | bytes 1572868
  59.5 1.3 %copy-start.3 = (bf16[128,2,16,256]{3,2,1,0:T(8,128)(2,1)}, bf16[128,2,16,256]{3,2,1,0:T(8,128)(2,1)S(1)}, u32[]{:S(2)}) copy-start(bf16[128,2,16,256]{3,2,1,0:T(8,128)(2,1)S(1)} %all-to-all-done) | copy-start | bytes 6291460
  62.6 4.1 %copy-start = (bf16[4,2,32,16,256]{4,3,2,1,0:T(8,128)(2,1)}, bf16[4,2,32,16,256]{4,3,2,1,0:T(8,128)(2,1)S(1)}, u32[]{:S(2)}) copy-start(bf16[4,2,32,16,256]{4,3,2,1,0:T(8,128)(2,1)S(1)} %copy.72) | copy-start | bytes 6291460
  66.7 5.6 %copy-start.2 = (bf16[8,131072]{1,0:T(8,128)(2,1)S(1)}, bf16[8,131072]{1,0:T(8,128)(2,1)}, u32[]{:S(2)}) copy-start(bf16[8,131072]{1,0:T(8,128)(2,1)} %reshape_reshape.3) | copy-start | bytes 6291460
  66.7 5.6 %copy-start.4 = (s32[64,2,8,128]{3,1,2,0:T(2,128)S(1)}, s32[64,2,8,128]{3,1,2,0:T(2,128)}, u32[]{:S(2)}) copy-start(s32[64,2,8,128]{3,1,2,0:T(2,128)} %copy.89) | copy-start | bytes 1572868
  95.5 3.0 %copy-start.5 = (f32[8,32]{1,0:T(8,128)}, f32[8,32]{1,0:T(8,128)S(1)}, u32[]{:S(2)}) copy-start(f32[8,32]{1,0:T(8,128)S(1)} %get-tuple-element.43.refs_2_) | copy-start | bytes 3076
  95.5 3.0 %copy-start.6 = (f32[8,32]{1,0:T(8,128)}, f32[8,32]{1,0:T(8,128)S(1)}, u32[]{:S(2)}) copy-start(f32[8,32]{1,0:T(8,128)S(1)} %get-tuple-element.44.refs_1_) | copy-start | bytes 3076
  101.7 6.1 %collective-permute-start = (f32[8,512,1]{1,0,2:T(8,128)S(1)}, f32[8,512,1]{1,0,2:T(8,128)S(1)}, u32[]{:S(2)}, u32[]{:S(2)}) collective-permute-start(f32[8,512,1]{1,0,2:T(8,128)S(1)} %get-tuple-element.40), channel_id=1, source_target_pairs={{0,1},{1,2},{2,3},{4,5},{5,6},{6,7},{8,9},{9,10},{10,11},{12,13},{... | collective-permute-start | bytes 49160 | tf_op jit(solution)/shard_map/ppermute | solution.py:346
  105.1 6.6 %collective-permute-start.1 = (f32[8,512,1]{1,0,2:T(8,128)S(1)}, f32[8,512,1]{1,0,2:T(8,128)S(1)}, u32[]{:S(2)}, u32[]{:S(2)}) collective-permute-start(f32[8,512,1]{1,0,2:T(8,128)S(1)} %get-tuple-element.39), channel_id=1, source_target_pairs={{1,0},{2,1},{3,2},{5,4},{6,5},{7,6},{9,8},{10,9},{11,10},{13,12},{... | collective-permute-start | bytes 49160 | tf_op jit(solution)/shard_map/ppermute | solution.py:347

commit v5 on v4

--- a/solution.py
+++ b/solution.py
@@ -114,7 +114,7 @@
 def calibrate_send(raw, pedestal, gain, good, bounds, table, n_peak):
     frame_dev, mods, row_dev, cols = raw.shape
     width = cols // n_peak
-    group = 4
+    group = 8
     grid_spec = pltpu.PrefetchScalarGridSpec(
         num_scalar_prefetch=2,
         grid=(mods // group,),
@@ -338,8 +338,15 @@
     cycle_average, cycle_rms = cycle_stats(first, second, present_flag)
     edge_cycle = jnp.stack([cycle[:, width_here - 1], cycle[:, 0]], axis=1)
     edge_values = jnp.stack([frame[:, :, width_here - 1], frame[:, :, 0]], axis=2)
-    edge_mean = jnp.take(cycle_average, edge_cycle, axis=1)
-    edge_rms = jnp.take(cycle_rms, edge_cycle, axis=1)
+    edge_hits = (edge_cycle.reshape(1, -1) == levels[:, None]).astype(jnp.float32)
+    edge_table = jnp.einsum(
+        "fk,kp->fp",
+        jnp.concatenate([cycle_average, cycle_rms], axis=0),
+        edge_hits,
+        precision=precise_variant,
+    ).reshape(2 * frames_all, mrows, 2)
+    edge_mean = edge_table[:frames_all]
+    edge_rms = edge_table[frames_all:]
     edge_score = (edge_values.astype(jnp.float32) - edge_mean) / edge_rms
     fwd = [(i, i + 1) for i in range(n_peak - 1)]
     bwd = [(i + 1, i) for i in range(n_peak - 1)]

time: 128 us -> 123 us (0.961)
  local copies, waits for them, and re-layouts: 25.8 us -> 20.5 us
  starting transfers between devices: 16.8 us -> 18.6 us
  waiting for transfers between devices: 22.5 us -> 20.9 us
    gather x4 -> x0, local copies, waits for them, and re-layouts: 5.96 us -> none  [the longest x2 2.99 us: body(): edge_rms = jnp.take(cycle_rms, edge_cycle, axis=1)]
    ppermute x1, waiting for transfers between devices: 1.86 us -> 0.01 us  [body(): right = lax.ppermute(edge_score[:, :, 1:], 'peak', bwd)]
    ppermute x1, starting transfers between devices: 3.4 us -> 4.71 us  [body(): left = lax.ppermute(edge_score[:, :, :1], 'peak', fwd)]
  transfers between devices with their start and end apart: 3 -> 3, of which waited for: 2 -> 1; matrix products, arithmetic and copies ran while one was open for 9% -> 10% of each run, Pallas kernels for 0% -> 0%
where the time goes in v5:
time: 123 us
  Pallas kernels  47.1 us (38%)
  waiting for transfers between devices  20.9 us (17%)
  local copies, waits for them, and re-layouts  20.5 us (17%)
  starting transfers between devices  18.6 us (15%)
  other arithmetic  11.1 us (9%)
  matrix products  3.42 us (3%)
    all_to_all x1, waiting for transfers between devices, body(): got = lax.all_to_all(send, ('calib', 'peak'), 0, 0, tiled=True)  20.9 us
    pallas_call x1, Pallas kernels, gather_sum(): pl.pallas_call(lambda *refs: gather_sum_kernel(n_calib, n_peak, *refs), o...  17.5 us
    pallas_call x1, Pallas kernels, calibrate_send(): pl.pallas_call(lambda *refs: calibrate_kernel(group, *refs), grid_spec=gr...  16.2 us
    pallas_call x1, Pallas kernels, score_outputs(): pl.pallas_call(lambda *refs: score_kernel(n_peak, levels, *refs), grid_sp...  13.4 us
    all_to_all x1, starting transfers between devices, body(): got = lax.all_to_all(send, ('calib', 'peak'), 0, 0, tiled=True)  11.5 us
    ppermute x1, starting transfers between devices, body(): left = lax.ppermute(edge_score[:, :, :1], 'peak', fwd)  4.71 us
    slice x2, local copies, waits for them, and re-layouts, body(): frame[:, :, width_here - 1]  3.42 us
    reduce_sum x2, other arithmetic, cycle_index(): return jnp.sum((dist[..., None] >= lows).astype(jnp.int32), axis=-1)  3.34 us
  transfers between devices with their start and end apart: 3, of which 1 were waited for; matrix products, arithmetic and copies ran while one was open for 10% of the time, Pallas kernels for 0%

profile of v5, /device:TPU:1, one launch (start us, length us, event | category | flops | bytes accessed | tf_op | source)
XLA Modules:
  0.0 122.7 jit_solution(15363663678597441456)
XLA Ops:
  0.6 0.8 copy.58
  1.4 0.7 reshape.185.refs_1_
  2.1 16.2 %shard_map.77 = bf16[32,4,2,16,256]{4,3,2,1,0:T(8,128)(2,1)} custom-call(s32[32]{0:T(128)} %refs_0_.1, s32[224]{0:T(256)} %reshape.185.refs_1_, s32[2,32,16,1024]{3,2,1,0:T(8,128)} %refs_2_.1, f32[3,32,16,1024]{3,2,1,0:T(8,128)} %refs_3_.1, bf16[3,32,16,1024]{3,2,1,0:T(8,128)(2,1)} %refs_4_.1, s32[32,16,1024]{2,1,0:T(8,128)} %refs_5_.1), custom_call_target="tpu_custom_call" | custom-call | tf_op jit(solution)/shard_map/pallas_call | solution.py:131
  18.3 11.5 %all-to-all-start = ((bf16[128,2,16,256]{3,2,1,0:T(8,128)(2,1)}), bf16[128,2,16,256]{3,2,1,0:T(8,128)(2,1)S(1)}, u32[]{:S(2)}, u32[]{:S(2)}) async-start(bf16[128,2,16,256]{3,2,1,0:T(8,128)(2,1)} %bitcast.30), calls=%async_computation | async-start | bytes 4194304 | tf_op jit(solution)/shard_map/all_to_all | solution.py:302
  30.1 1.6 %convert_reduce_fusion.1.refs_4_ = s32[512,256]{1,0:T(8,128)S(1)} fusion(s32[512,256]{1,0:T(8,128)S(1)} %broadcast_add_fusion.1, s32[31]{0:T(128)S(1)} %multiply_multiply_fusion), kind=kLoop, calls=%fused_computation.5 | loop fusion | flops 12058624 | bytes 1048700 | tf_op jit(solution)/shard_map/reduce_sum | solution.py:34
  31.9 1.1 copy.73
  33.5 1.1 constant_dynamic-slice_fusion
  34.8 1.7 %convert_reduce_fusion = s32[32,16,256]{2,1,0:T(8,128)S(1)} fusion(s32[32,16,256]{2,1,0:T(8,128)S(1)} %broadcast_add_fusion, s32[31]{0:T(128)S(1)} %multiply_multiply_fusion), kind=kLoop, calls=%fused_computation.4 | loop fusion | flops 12058624 | bytes 1048700 | tf_op jit(solution)/shard_map/reduce_sum | solution.py:34
  36.5 2.5 %select_reduce_fusion = s32[32]{0:T(128)S(1)} fusion(s32[32,16,256]{2,1,0:T(8,128)S(1)} %constant_dynamic-slice_fusion, s32[32,16,256]{2,1,0:T(8,128)S(1)} %convert_reduce_fusion), kind=kLoop, calls=%fused_computation | loop fusion | flops 12582880 | bytes 1048704 | tf_op jit(solution)/shard_map/reduce_sum | solution.py:216
  39.0 20.9 %all-to-all-done = bf16[128,2,16,256]{3,2,1,0:T(8,128)(2,1)S(1)} async-done(((bf16[128,2,16,256]{3,2,1,0:T(8,128)(2,1)}), bf16[128,2,16,256]{3,2,1,0:T(8,128)(2,1)S(1)}, u32[]{:S(2)}, u32[]{:S(2)}) %all-to-all-start) | async-done | bytes 2097184 | tf_op jit(solution)/shard_map/all_to_all | solution.py:302
  59.9 1.3 %copy-done.3 = bf16[128,2,16,256]{3,2,1,0:T(8,128)(2,1)} copy-done((bf16[128,2,16,256]{3,2,1,0:T(8,128)(2,1)}, bf16[128,2,16,256]{3,2,1,0:T(8,128)(2,1)S(1)}, u32[]{:S(2)}) %copy-start.3) | copy-done | bytes 2097176
  61.2 1.8 %copy.59 = bf16[4,2,32,16,256]{4,3,2,1,0:T(8,128)(2,1)S(1)} copy(bf16[4,2,32,16,256]{4,3,1,0,2:T(8,128)(2,1)} %bitcast.29) | data formatting | bytes 4194304 | tf_op jit(solution)/shard_map/transpose | solution.py:304
  63.0 2.3 %reshape_reshape.3 = bf16[8,131072]{1,0:T(8,128)(2,1)} reshape(bf16[4,2,32,16,256]{4,3,2,1,0:T(8,128)(2,1)S(1)} %copy.59) | data formatting | bytes 4194304 | tf_op jit(solution)/shard_map/reshape;reshape | solution.py:314
  65.3 1.8 %fusion.19 = (bf16[8,512,1]{2,1,0:T(8,128)(2,1)}, bf16[8,512,1]{2,1,0:T(8,128)(2,1)}) fusion(bf16[8,512,256]{2,1,0:T(8,128)(2,1)S(1)} %bitcast.26), kind=kLoop, calls=%fused_computation.54 | loop fusion | bytes 32768 | tf_op jit(solution)/shard_map/slice | solution.py:340
  67.1 1.6 %copy.62 = bf16[8,512,1]{1,0,2:T(8,128)(2,1)S(1)} copy(bf16[8,512,1]{2,1,0:T(8,128)(2,1)} %get-tuple-element.30) | data formatting | bytes 16384 | tf_op jit(solution)/shard_map/slice | solution.py:340
  68.7 1.7 %copy.63 = bf16[8,512,1]{1,0,2:T(8,128)(2,1)S(1)} copy(bf16[8,512,1]{2,1,0:T(8,128)(2,1)} %get-tuple-element.31) | data formatting | bytes 16384 | tf_op jit(solution)/shard_map/slice | solution.py:340
  70.5 0.2 copy.65
  70.7 2.3 %reduce-precision_convert_fusion = (bf16[8,131072]{1,0:T(8,128)(2,1)S(1)}, bf16[8,131072]{1,0:T(8,128)(2,1)S(1)}) fusion(bf16[8,131072]{1,0:T(8,128)(2,1)} %reshape_reshape.3), kind=kLoop, calls=%fused_computation.13 | loop fusion | flops 6291456 | bytes 6291456 | tf_op jit(solution)/shard_map/convert_element_type | solution.py:318
  73.1 3.2 %fusion = f32[24,32]{1,0:T(8,128)S(1)} fusion(s32[131072]{0:T(1024)S(1)} %bitcast.35, bf16[8,131072]{1,0:T(8,128)(2,1)S(1)} %get-tuple-element.33, bf16[8,131072]{1,0:T(8,128)(2,1)S(1)} %get-tuple-element.32, bf16[8,131072]{1,0:T(8,128)(2,1)S(1)} %copy-done.2), kind=kOutput, calls=%fused_computation.3 | convolution fusion | flops 224395264 | bytes 6818816 | tf_op jit(solution)/shard_map/fp,kp->fk/dot_general | solution.py:321
  76.3 0.7 fusion.13.refs_0_
  77.0 17.5 %shard_map.78 = f32[8,128]{1,0:T(8,128)} custom-call(f32[8,128]{1,0:T(8,128)} %fusion.13.refs_0_), custom_call_target="tpu_custom_call" | custom-call | tf_op jit(solution)/shard_map/pallas_call | solution.py:270
  94.6 0.7 slice_bitcast_fusion
  95.3 0.8 add_sqrt_fusion
  96.3 0.2 copy.64
  96.5 0.2 copy.66
  96.8 0.4 fusion.20
  97.3 2.4 %collective-permute-start.1 = (f32[8,512,1]{1,0,2:T(8,128)S(1)}, f32[8,512,1]{1,0,2:T(8,128)S(1)}, u32[]{:S(2)}, u32[]{:S(2)}) collective-permute-start(f32[8,512,1]{1,0,2:T(8,128)S(1)} %copy.68), channel_id=1, source_target_pairs={{1,0},{2,1},{3,2},{5,4},{6,5},{7,6},{9,8},{10,9},{11,10},{13,12},{... | collective-permute-start | bytes 49160 | tf_op jit(solution)/shard_map/ppermute | solution.py:354
  99.8 4.7 %collective-permute-start = (f32[8,512,1]{1,0,2:T(8,128)S(1)}, f32[8,512,1]{1,0,2:T(8,128)S(1)}, u32[]{:S(2)}, u32[]{:S(2)}) collective-permute-start(f32[8,512,1]{1,0,2:T(8,128)S(1)} %copy.67), channel_id=1, source_target_pairs={{0,1},{1,2},{2,3},{4,5},{5,6},{6,7},{8,9},{9,10},{10,11},{12,13},{... | collective-permute-start | bytes 49160 | tf_op jit(solution)/shard_map/ppermute | solution.py:353
  104.5 0.8 reduce_min.9
  105.3 2.0 %copy.70.refs_6_ = f32[8,512,1]{2,1,0:T(8,128)} copy(f32[8,512,1]{1,0,2:T(8,128)S(1)} %collective-permute-done.1) | data formatting | bytes 32768 | tf_op jit(solution)/shard_map/ppermute | solution.py:354
  107.3 2.0 %copy.69.refs_5_ = f32[8,512,1]{2,1,0:T(8,128)} copy(f32[8,512,1]{1,0,2:T(8,128)S(1)} %collective-permute-done) | data formatting | bytes 32768 | tf_op jit(solution)/shard_map/ppermute | solution.py:353
  109.3 13.4 %shard_map.79 = (bf16[8,512,256]{2,1,0:T(8,128)(2,1)}, bf16[8,512,256]{2,1,0:T(8,128)(2,1)}) custom-call(s32[1]{0:T(128)} %bitcast.refs_0_, f32[8,32]{1,0:T(8,128)} %copy-done.6, f32[8,32]{1,0:T(8,128)} %copy-done.5, bf16[8,512,256]{2,1,0:T(8,128)(2,1)} %bitcast.27, s32[512,256]{1,0:T(8,128)} %copy-done.1, f32[8,512,1]{2,1,0:T(8,128)} %copy.69.refs_5_, ...), custom_call_target="tpu_custom_call" | custom-call | tf_op jit(solution)/shard_map/pallas_call | solution.py:184
  (40 shorter events, 1.5 us)
Async XLA Ops:
  18.3 11.5 %copy-start.7 = (s32[32]{0:T(128)S(1)}, s32[32]{0:T(128)}, u32[]{:S(2)}) copy-start(s32[32]{0:T(128)} %refs_0_.1) | copy-start | bytes 388
  18.3 41.6 %all-to-all-start = ((bf16[128,2,16,256]{3,2,1,0:T(8,128)(2,1)}), bf16[128,2,16,256]{3,2,1,0:T(8,128)(2,1)S(1)}, u32[]{:S(2)}, u32[]{:S(2)}) async-start(bf16[128,2,16,256]{3,2,1,0:T(8,128)(2,1)} %bitcast.30), calls=%async_computation | async-start | bytes 4194304 | tf_op jit(solution)/shard_map/all_to_all | solution.py:302
  31.7 72.8 %copy-start.1 = (s32[512,256]{1,0:T(8,128)}, s32[512,256]{1,0:T(8,128)S(1)}, u32[]{:S(2)}) copy-start(s32[512,256]{1,0:T(8,128)S(1)} %convert_reduce_fusion.1.refs_4_) | copy-start | bytes 1572868
  59.9 1.3 %copy-start.3 = (bf16[128,2,16,256]{3,2,1,0:T(8,128)(2,1)}, bf16[128,2,16,256]{3,2,1,0:T(8,128)(2,1)S(1)}, u32[]{:S(2)}) copy-start(bf16[128,2,16,256]{3,2,1,0:T(8,128)(2,1)S(1)} %all-to-all-done) | copy-start | bytes 6291460
  63.0 4.1 %copy-start = (bf16[4,2,32,16,256]{4,3,2,1,0:T(8,128)(2,1)}, bf16[4,2,32,16,256]{4,3,2,1,0:T(8,128)(2,1)S(1)}, u32[]{:S(2)}) copy-start(bf16[4,2,32,16,256]{4,3,2,1,0:T(8,128)(2,1)S(1)} %copy.59) | copy-start | bytes 6291460
  68.7 4.4 %copy-start.2 = (bf16[8,131072]{1,0:T(8,128)(2,1)S(1)}, bf16[8,131072]{1,0:T(8,128)(2,1)}, u32[]{:S(2)}) copy-start(bf16[8,131072]{1,0:T(8,128)(2,1)} %reshape_reshape.3) | copy-start | bytes 6291460
  70.7 2.4 %copy-start.4 = (s32[64,2,8,128]{3,1,2,0:T(2,128)S(1)}, s32[64,2,8,128]{3,1,2,0:T(2,128)}, u32[]{:S(2)}) copy-start(s32[64,2,8,128]{3,1,2,0:T(2,128)} %copy.73) | copy-start | bytes 1572868
  96.1 13.1 %copy-start.5 = (f32[8,32]{1,0:T(8,128)}, f32[8,32]{1,0:T(8,128)S(1)}, u32[]{:S(2)}) copy-start(f32[8,32]{1,0:T(8,128)S(1)} %get-tuple-element.42.refs_2_) | copy-start | bytes 3076
  96.1 13.1 %copy-start.6 = (f32[8,32]{1,0:T(8,128)}, f32[8,32]{1,0:T(8,128)S(1)}, u32[]{:S(2)}) copy-start(f32[8,32]{1,0:T(8,128)S(1)} %get-tuple-element.43.refs_1_) | copy-start | bytes 3076
  97.3 8.0 %collective-permute-start.1 = (f32[8,512,1]{1,0,2:T(8,128)S(1)}, f32[8,512,1]{1,0,2:T(8,128)S(1)}, u32[]{:S(2)}, u32[]{:S(2)}) collective-permute-start(f32[8,512,1]{1,0,2:T(8,128)S(1)} %copy.68), channel_id=1, source_target_pairs={{1,0},{2,1},{3,2},{5,4},{6,5},{7,6},{9,8},{10,9},{11,10},{13,12},{... | collective-permute-start | bytes 49160 | tf_op jit(solution)/shard_map/ppermute | solution.py:354
  99.8 7.5 %collective-permute-start = (f32[8,512,1]{1,0,2:T(8,128)S(1)}, f32[8,512,1]{1,0,2:T(8,128)S(1)}, u32[]{:S(2)}, u32[]{:S(2)}) collective-permute-start(f32[8,512,1]{1,0,2:T(8,128)S(1)} %copy.67), channel_id=1, source_target_pairs={{0,1},{1,2},{2,3},{4,5},{5,6},{6,7},{8,9},{9,10},{10,11},{12,13},{... | collective-permute-start | bytes 49160 | tf_op jit(solution)/shard_map/ppermute | solution.py:353

commit v6 on v5

--- a/solution.py
+++ b/solution.py
@@ -216,52 +216,92 @@
     return jnp.sum(hit, axis=(0, 1, 2)).astype(jnp.float32)
 
 
-def gather_sum_kernel(n_calib, n_peak, x_ref, o_ref, buf, send_sem, recv_sem):
-    total = n_calib * n_peak
-    me = lax.axis_index("calib") * n_peak + lax.axis_index("peak")
-    buf[total - 1] = x_ref[...]
+def gather_sum_kernel(
+    n_calib, n_peak, x_ref, o_ref, near, far, partial, near_send, near_recv, far_send, far_recv
+):
+    my_calib = lax.axis_index("calib")
+    my_peak = lax.axis_index("peak")
+    near[n_peak - 1] = x_ref[...]
     barrier = pltpu.get_barrier_semaphore()
 
-    def peer_of(step):
-        peer = lax.rem(me + step, total)
-        return (peer // n_peak, peer % n_peak)
-
-    def greet(step, carry):
+    def peak_peer(step):
+        return (my_calib, lax.rem(my_peak + step, n_peak))
+
+    def calib_peer(step):
+        return (lax.rem(my_calib + step, n_calib), my_peak)
+
+    def greet_peak(step, carry):
         pl.semaphore_signal(
-            barrier, inc=1, device_id=peer_of(step), device_id_type=pl.DeviceIdType.MESH
+            barrier, inc=1, device_id=peak_peer(step), device_id_type=pl.DeviceIdType.MESH
         )
         return carry
 
-    lax.fori_loop(1, total, greet, 0)
-    pl.semaphore_wait(barrier, total - 1)
-
-    def send(step, carry):
+    def greet_calib(step, carry):
+        pl.semaphore_signal(
+            barrier, inc=1, device_id=calib_peer(step), device_id_type=pl.DeviceIdType.MESH
+        )
+        return carry
+
+    lax.fori_loop(1, n_peak, greet_peak, 0)
+    lax.fori_loop(1, n_calib, greet_calib, 0)
+    pl.semaphore_wait(barrier, n_peak - 1 + n_calib - 1)
+
+    def send_near(step, carry):
         pltpu.make_async_remote_copy(
             src_ref=x_ref,
-            dst_ref=buf.at[total - 1 - step],
-            send_sem=send_sem,
-            recv_sem=recv_sem,
-            device_id=peer_of(step),
+            dst_ref=near.at[n_peak - 1 - step],
+            send_sem=near_send,
+            recv_sem=near_recv,
+            device_id=peak_peer(step),
             device_id_type=pl.DeviceIdType.MESH,
         ).start()
         return carry
 
-    lax.fori_loop(1, total, send, 0)
-    every = pltpu.make_async_remote_copy(
-        src_ref=buf.at[pl.ds(0, total - 1)],
-        dst_ref=buf.at[pl.ds(0, total - 1)],
-        send_sem=send_sem,
-        recv_sem=recv_sem,
-        device_id=peer_of(1),
+    lax.fori_loop(1, n_peak, send_near, 0)
+    every_near = pltpu.make_async_remote_copy(
+        src_ref=near.at[pl.ds(0, n_peak - 1)],
+        dst_ref=near.at[pl.ds(0, n_peak - 1)],
+        send_sem=near_send,
+        recv_sem=near_recv,
+        device_id=peak_peer(1),
         device_id_type=pl.DeviceIdType.MESH,
     )
-    every.wait_send()
-    every.wait_recv()
-
-    def add(source, acc):
-        return acc + buf[lax.rem(source - me - 1 + 2 * total, total)]
-
-    o_ref[...] = lax.fori_loop(0, total, add, jnp.zeros(x_ref.shape, x_ref.dtype))
+    every_near.wait_send()
+    every_near.wait_recv()
+
+    def add_near(source, acc):
+        return acc + near[lax.rem(source - my_peak - 1 + 2 * n_peak, n_peak)]
+
+    partial[...] = lax.fori_loop(0, n_peak, add_near, jnp.zeros(x_ref.shape, x_ref.dtype))
+    far[n_calib - 1] = partial[...]
+
+    def send_far(step, carry):
+        pltpu.make_async_remote_copy(
+            src_ref=partial,
+            dst_ref=far.at[n_calib - 1 - step],
+            send_sem=far_send,
+            recv_sem=far_recv,
+            device_id=calib_peer(step),
+            device_id_type=pl.DeviceIdType.MESH,
+        ).start()
+        return carry
+
+    lax.fori_loop(1, n_calib, send_far, 0)
+    every_far = pltpu.make_async_remote_copy(
+        src_ref=far.at[pl.ds(0, n_calib - 1)],
+        dst_ref=far.at[pl.ds(0, n_calib - 1)],
+        send_sem=far_send,
+        recv_sem=far_recv,
+        device_id=calib_peer(1),
+        device_id_type=pl.DeviceIdType.MESH,
+    )
+    every_far.wait_send()
+    every_far.wait_recv()
+
+    def add_far(source, acc):
+        return acc + far[lax.rem(source - my_calib - 1 + 2 * n_calib, n_calib)]
+
+    o_ref[...] = lax.fori_loop(0, n_calib, add_far, jnp.zeros(x_ref.shape, x_ref.dtype))
 
 
 def gather_sum(x):
@@ -273,7 +313,11 @@
         in_specs=[pl.BlockSpec(memory_space=pltpu.VMEM)],
         out_specs=pl.BlockSpec(memory_space=pltpu.VMEM),
         scratch_shapes=[
-            pltpu.VMEM((n_calib * n_peak,) + x.shape, x.dtype),
+            pltpu.VMEM((n_peak,) + x.shape, x.dtype),
+            pltpu.VMEM((n_calib,) + x.shape, x.dtype),
+            pltpu.VMEM(x.shape, x.dtype),
+            pltpu.SemaphoreType.DMA,
+            pltpu.SemaphoreType.DMA,
             pltpu.SemaphoreType.DMA,
             pltpu.SemaphoreType.DMA,
         ],

time: 123 us -> 118 us (0.959)
  Pallas kernels: 47.1 us -> 42 us
    pallas_call x1, Pallas kernels: 17.5 us -> 12.4 us  [gather_sum(): pl.pallas_call(lambda *refs: gather_sum_kernel(n_calib, n_peak, *refs), o...]
where the time goes in v6:
time: 118 us
  Pallas kernels  42 us (36%)
  waiting for transfers between devices  20.9 us (18%)
  local copies, waits for them, and re-layouts  20.5 us (17%)
  starting transfers between devices  18.6 us (16%)
  other arithmetic  11.1 us (9%)
  matrix products  3.42 us (3%)
    all_to_all x1, waiting for transfers between devices, body(): got = lax.all_to_all(send, ('calib', 'peak'), 0, 0, tiled=True)  20.9 us
    pallas_call x1, Pallas kernels, calibrate_send(): pl.pallas_call(lambda *refs: calibrate_kernel(group, *refs), grid_spec=gr...  16.2 us
    pallas_call x1, Pallas kernels, score_outputs(): pl.pallas_call(lambda *refs: score_kernel(n_peak, levels, *refs), grid_sp...  13.4 us
    pallas_call x1, Pallas kernels, gather_sum(): pl.pallas_call(lambda *refs: gather_sum_kernel(n_calib, n_peak, *refs), o...  12.4 us
    all_to_all x1, starting transfers between devices, body(): got = lax.all_to_all(send, ('calib', 'peak'), 0, 0, tiled=True)  11.5 us
    ppermute x1, starting transfers between devices, body(): left = lax.ppermute(edge_score[:, :, :1], 'peak', fwd)  3.78 us
    slice x2, local copies, waits for them, and re-layouts, body(): frame[:, :, width_here - 1]  3.42 us
    reduce_sum x2, other arithmetic, cycle_index(): return jnp.sum((dist[..., None] >= lows).astype(jnp.int32), axis=-1)  3.34 us
  transfers between devices with their start and end apart: 3, of which 1 were waited for; matrix products, arithmetic and copies ran while one was open for 10% of the time, Pallas kernels for 0%

profile of v6, /device:TPU:1, one launch (start us, length us, event | category | flops | bytes accessed | tf_op | source)
XLA Modules:
  0.0 117.5 jit_solution(10929279249201880534)
XLA Ops:
  0.6 0.8 copy.58
  1.4 0.7 reshape.185.refs_1_
  2.1 16.2 %shard_map.77 = bf16[32,4,2,16,256]{4,3,2,1,0:T(8,128)(2,1)} custom-call(s32[32]{0:T(128)} %refs_0_.1, s32[224]{0:T(256)} %reshape.185.refs_1_, s32[2,32,16,1024]{3,2,1,0:T(8,128)} %refs_2_.1, f32[3,32,16,1024]{3,2,1,0:T(8,128)} %refs_3_.1, bf16[3,32,16,1024]{3,2,1,0:T(8,128)(2,1)} %refs_4_.1, s32[32,16,1024]{2,1,0:T(8,128)} %refs_5_.1), custom_call_target="tpu_custom_call" | custom-call | tf_op jit(solution)/shard_map/pallas_call | solution.py:131
  18.3 11.5 %all-to-all-start = ((bf16[128,2,16,256]{3,2,1,0:T(8,128)(2,1)}), bf16[128,2,16,256]{3,2,1,0:T(8,128)(2,1)S(1)}, u32[]{:S(2)}, u32[]{:S(2)}) async-start(bf16[128,2,16,256]{3,2,1,0:T(8,128)(2,1)} %bitcast.30), calls=%async_computation | async-start | bytes 4194304 | tf_op jit(solution)/shard_map/all_to_all | solution.py:346
  30.1 1.6 %convert_reduce_fusion.1.refs_4_ = s32[512,256]{1,0:T(8,128)S(1)} fusion(s32[512,256]{1,0:T(8,128)S(1)} %broadcast_add_fusion.1, s32[31]{0:T(128)S(1)} %multiply_multiply_fusion), kind=kLoop, calls=%fused_computation.5 | loop fusion | flops 12058624 | bytes 1048700 | tf_op jit(solution)/shard_map/reduce_sum | solution.py:34
  31.9 1.1 copy.73
  33.5 1.1 constant_dynamic-slice_fusion
  34.8 1.7 %convert_reduce_fusion = s32[32,16,256]{2,1,0:T(8,128)S(1)} fusion(s32[32,16,256]{2,1,0:T(8,128)S(1)} %broadcast_add_fusion, s32[31]{0:T(128)S(1)} %multiply_multiply_fusion), kind=kLoop, calls=%fused_computation.4 | loop fusion | flops 12058624 | bytes 1048700 | tf_op jit(solution)/shard_map/reduce_sum | solution.py:34
  36.5 2.5 %select_reduce_fusion = s32[32]{0:T(128)S(1)} fusion(s32[32,16,256]{2,1,0:T(8,128)S(1)} %constant_dynamic-slice_fusion, s32[32,16,256]{2,1,0:T(8,128)S(1)} %convert_reduce_fusion), kind=kLoop, calls=%fused_computation | loop fusion | flops 12582880 | bytes 1048704 | tf_op jit(solution)/shard_map/reduce_sum | solution.py:216
  39.0 20.9 %all-to-all-done = bf16[128,2,16,256]{3,2,1,0:T(8,128)(2,1)S(1)} async-done(((bf16[128,2,16,256]{3,2,1,0:T(8,128)(2,1)}), bf16[128,2,16,256]{3,2,1,0:T(8,128)(2,1)S(1)}, u32[]{:S(2)}, u32[]{:S(2)}) %all-to-all-start) | async-done | bytes 2097184 | tf_op jit(solution)/shard_map/all_to_all | solution.py:346
  59.9 1.3 %copy-done.3 = bf16[128,2,16,256]{3,2,1,0:T(8,128)(2,1)} copy-done((bf16[128,2,16,256]{3,2,1,0:T(8,128)(2,1)}, bf16[128,2,16,256]{3,2,1,0:T(8,128)(2,1)S(1)}, u32[]{:S(2)}) %copy-start.3) | copy-done | bytes 2097176
  61.2 1.8 %copy.59 = bf16[4,2,32,16,256]{4,3,2,1,0:T(8,128)(2,1)S(1)} copy(bf16[4,2,32,16,256]{4,3,1,0,2:T(8,128)(2,1)} %bitcast.29) | data formatting | bytes 4194304 | tf_op jit(solution)/shard_map/transpose | solution.py:348
  63.0 2.3 %reshape_reshape.3 = bf16[8,131072]{1,0:T(8,128)(2,1)} reshape(bf16[4,2,32,16,256]{4,3,2,1,0:T(8,128)(2,1)S(1)} %copy.59) | data formatting | bytes 4194304 | tf_op jit(solution)/shard_map/reshape;reshape | solution.py:358
  65.3 1.8 %fusion.19 = (bf16[8,512,1]{2,1,0:T(8,128)(2,1)}, bf16[8,512,1]{2,1,0:T(8,128)(2,1)}) fusion(bf16[8,512,256]{2,1,0:T(8,128)(2,1)S(1)} %bitcast.26), kind=kLoop, calls=%fused_computation.54 | loop fusion | bytes 32768 | tf_op jit(solution)/shard_map/slice | solution.py:384
  67.1 1.6 %copy.62 = bf16[8,512,1]{1,0,2:T(8,128)(2,1)S(1)} copy(bf16[8,512,1]{2,1,0:T(8,128)(2,1)} %get-tuple-element.30) | data formatting | bytes 16384 | tf_op jit(solution)/shard_map/slice | solution.py:384
  68.7 1.7 %copy.63 = bf16[8,512,1]{1,0,2:T(8,128)(2,1)S(1)} copy(bf16[8,512,1]{2,1,0:T(8,128)(2,1)} %get-tuple-element.31) | data formatting | bytes 16384 | tf_op jit(solution)/shard_map/slice | solution.py:384
  70.5 0.2 copy.65
  70.7 2.3 %reduce-precision_convert_fusion = (bf16[8,131072]{1,0:T(8,128)(2,1)S(1)}, bf16[8,131072]{1,0:T(8,128)(2,1)S(1)}) fusion(bf16[8,131072]{1,0:T(8,128)(2,1)} %reshape_reshape.3), kind=kLoop, calls=%fused_computation.13 | loop fusion | flops 6291456 | bytes 6291456 | tf_op jit(solution)/shard_map/convert_element_type | solution.py:362
  73.1 3.2 %fusion = f32[24,32]{1,0:T(8,128)S(1)} fusion(s32[131072]{0:T(1024)S(1)} %bitcast.35, bf16[8,131072]{1,0:T(8,128)(2,1)S(1)} %get-tuple-element.33, bf16[8,131072]{1,0:T(8,128)(2,1)S(1)} %get-tuple-element.32, bf16[8,131072]{1,0:T(8,128)(2,1)S(1)} %copy-done.2), kind=kOutput, calls=%fused_computation.3 | convolution fusion | flops 224395264 | bytes 6818816 | tf_op jit(solution)/shard_map/fp,kp->fk/dot_general | solution.py:365
  76.3 0.7 fusion.13.refs_0_
  77.0 12.4 %shard_map.78 = f32[8,128]{1,0:T(8,128)} custom-call(f32[8,128]{1,0:T(8,128)} %fusion.13.refs_0_), custom_call_target="tpu_custom_call" | custom-call | tf_op jit(solution)/shard_map/pallas_call | solution.py:310
  89.4 0.7 slice_bitcast_fusion
  90.2 0.8 add_sqrt_fusion
  91.2 0.2 copy.64
  91.4 0.2 copy.66
  91.7 0.4 fusion.20
  92.2 3.3 %collective-permute-start.1 = (f32[8,512,1]{1,0,2:T(8,128)S(1)}, f32[8,512,1]{1,0,2:T(8,128)S(1)}, u32[]{:S(2)}, u32[]{:S(2)}) collective-permute-start(f32[8,512,1]{1,0,2:T(8,128)S(1)} %copy.68), channel_id=1, source_target_pairs={{1,0},{2,1},{3,2},{5,4},{6,5},{7,6},{9,8},{10,9},{11,10},{13,12},{... | collective-permute-start | bytes 49160 | tf_op jit(solution)/shard_map/ppermute | solution.py:398
  95.6 3.8 %collective-permute-start = (f32[8,512,1]{1,0,2:T(8,128)S(1)}, f32[8,512,1]{1,0,2:T(8,128)S(1)}, u32[]{:S(2)}, u32[]{:S(2)}) collective-permute-start(f32[8,512,1]{1,0,2:T(8,128)S(1)} %copy.67), channel_id=1, source_target_pairs={{0,1},{1,2},{2,3},{4,5},{5,6},{6,7},{8,9},{9,10},{10,11},{12,13},{... | collective-permute-start | bytes 49160 | tf_op jit(solution)/shard_map/ppermute | solution.py:397
  99.4 0.8 reduce_min.9
  100.2 2.0 %copy.70.refs_6_ = f32[8,512,1]{2,1,0:T(8,128)} copy(f32[8,512,1]{1,0,2:T(8,128)S(1)} %collective-permute-done.1) | data formatting | bytes 32768 | tf_op jit(solution)/shard_map/ppermute | solution.py:398
  102.2 2.0 %copy.69.refs_5_ = f32[8,512,1]{2,1,0:T(8,128)} copy(f32[8,512,1]{1,0,2:T(8,128)S(1)} %collective-permute-done) | data formatting | bytes 32768 | tf_op jit(solution)/shard_map/ppermute | solution.py:397
  104.1 13.4 %shard_map.79 = (bf16[8,512,256]{2,1,0:T(8,128)(2,1)}, bf16[8,512,256]{2,1,0:T(8,128)(2,1)}) custom-call(s32[1]{0:T(128)} %bitcast.refs_0_, f32[8,32]{1,0:T(8,128)} %copy-done.6, f32[8,32]{1,0:T(8,128)} %copy-done.5, bf16[8,512,256]{2,1,0:T(8,128)(2,1)} %bitcast.27, s32[512,256]{1,0:T(8,128)} %copy-done.1, f32[8,512,1]{2,1,0:T(8,128)} %copy.69.refs_5_, ...), custom_call_target="tpu_custom_call" | custom-call | tf_op jit(solution)/shard_map/pallas_call | solution.py:184
  (40 shorter events, 1.5 us)
Async XLA Ops:
  18.3 11.5 %copy-start.7 = (s32[32]{0:T(128)S(1)}, s32[32]{0:T(128)}, u32[]{:S(2)}) copy-start(s32[32]{0:T(128)} %refs_0_.1) | copy-start | bytes 388
  18.3 41.6 %all-to-all-start = ((bf16[128,2,16,256]{3,2,1,0:T(8,128)(2,1)}), bf16[128,2,16,256]{3,2,1,0:T(8,128)(2,1)S(1)}, u32[]{:S(2)}, u32[]{:S(2)}) async-start(bf16[128,2,16,256]{3,2,1,0:T(8,128)(2,1)} %bitcast.30), calls=%async_computation | async-start | bytes 4194304 | tf_op jit(solution)/shard_map/all_to_all | solution.py:346
  31.7 67.7 %copy-start.1 = (s32[512,256]{1,0:T(8,128)}, s32[512,256]{1,0:T(8,128)S(1)}, u32[]{:S(2)}) copy-start(s32[512,256]{1,0:T(8,128)S(1)} %convert_reduce_fusion.1.refs_4_) | copy-start | bytes 1572868
  59.9 1.3 %copy-start.3 = (bf16[128,2,16,256]{3,2,1,0:T(8,128)(2,1)}, bf16[128,2,16,256]{3,2,1,0:T(8,128)(2,1)S(1)}, u32[]{:S(2)}) copy-start(bf16[128,2,16,256]{3,2,1,0:T(8,128)(2,1)S(1)} %all-to-all-done) | copy-start | bytes 6291460
  63.0 4.1 %copy-start = (bf16[4,2,32,16,256]{4,3,2,1,0:T(8,128)(2,1)}, bf16[4,2,32,16,256]{4,3,2,1,0:T(8,128)(2,1)S(1)}, u32[]{:S(2)}) copy-start(bf16[4,2,32,16,256]{4,3,2,1,0:T(8,128)(2,1)S(1)} %copy.59) | copy-start | bytes 6291460
  68.7 4.4 %copy-start.2 = (bf16[8,131072]{1,0:T(8,128)(2,1)S(1)}, bf16[8,131072]{1,0:T(8,128)(2,1)}, u32[]{:S(2)}) copy-start(bf16[8,131072]{1,0:T(8,128)(2,1)} %reshape_reshape.3) | copy-start | bytes 6291460
  70.7 2.4 %copy-start.4 = (s32[64,2,8,128]{3,1,2,0:T(2,128)S(1)}, s32[64,2,8,128]{3,1,2,0:T(2,128)}, u32[]{:S(2)}) copy-start(s32[64,2,8,128]{3,1,2,0:T(2,128)} %copy.73) | copy-start | bytes 1572868
  91.0 13.1 %copy-start.5 = (f32[8,32]{1,0:T(8,128)}, f32[8,32]{1,0:T(8,128)S(1)}, u32[]{:S(2)}) copy-start(f32[8,32]{1,0:T(8,128)S(1)} %get-tuple-element.42.refs_2_) | copy-start | bytes 3076
  91.0 13.1 %copy-start.6 = (f32[8,32]{1,0:T(8,128)}, f32[8,32]{1,0:T(8,128)S(1)}, u32[]{:S(2)}) copy-start(f32[8,32]{1,0:T(8,128)S(1)} %get-tuple-element.43.refs_1_) | copy-start | bytes 3076
  92.2 8.0 %collective-permute-start.1 = (f32[8,512,1]{1,0,2:T(8,128)S(1)}, f32[8,512,1]{1,0,2:T(8,128)S(1)}, u32[]{:S(2)}, u32[]{:S(2)}) collective-permute-start(f32[8,512,1]{1,0,2:T(8,128)S(1)} %copy.68), channel_id=1, source_target_pairs={{1,0},{2,1},{3,2},{5,4},{6,5},{7,6},{9,8},{10,9},{11,10},{13,12},{... | collective-permute-start | bytes 49160 | tf_op jit(solution)/shard_map/ppermute | solution.py:398
  95.6 6.6 %collective-permute-start = (f32[8,512,1]{1,0,2:T(8,128)S(1)}, f32[8,512,1]{1,0,2:T(8,128)S(1)}, u32[]{:S(2)}, u32[]{:S(2)}) collective-permute-start(f32[8,512,1]{1,0,2:T(8,128)S(1)} %copy.67), channel_id=1, source_target_pairs={{0,1},{1,2},{2,3},{4,5},{5,6},{6,7},{8,9},{9,10},{10,11},{12,13},{... | collective-permute-start | bytes 49160 | tf_op jit(solution)/shard_map/ppermute | solution.py:397

commit v7 on v6

--- a/solution.py
+++ b/solution.py
@@ -136,10 +136,10 @@
 
 
 def score_kernel(n_peak, levels, low_ref, mean_ref, rms_ref, frame_ref, cycle_ref, left_ref, right_ref, snr_ref, bent_ref):
-    frame_pos = pl.program_id(0)
+    frame_pos = pl.program_id(0) * pl.num_programs(1) + pl.program_id(1)
     cycle = cycle_ref[...]
-    values = frame_ref[...].astype(jnp.float32)
-    rows, cols = values.shape
+    rows, cols = cycle.shape
+    values = frame_ref[...].astype(jnp.float32).reshape(rows, cols)
     tops = mean_ref.shape[1] - 1
     pixel_mean = jnp.zeros((rows, cols), jnp.float32)
     pixel_rms = jnp.ones((rows, cols), jnp.float32)
@@ -168,24 +168,27 @@
     bent_ref[...] = total.astype(bent_ref.dtype)
 
 
-def score_outputs(frame, cycle, cycle_average, cycle_rms, left, right, n_peak):
-    frames, rows, cols = frame.shape
+def score_outputs(got, cycle, cycle_average, cycle_rms, left, right, n_peak):
+    n_calib, _, frame_dev, row_dev, cols = got.shape
+    rows, _ = cycle.shape
+    frames = n_peak * frame_dev
     span = (rows * rows + cols * cols) ** 0.5
     levels = min(CYCLES, int(span // CYCLE_W) + 3)
     low = jnp.min(cycle).reshape(1)
-    block = pl.BlockSpec((None, rows, cols), lambda f, *_: (f, 0, 0))
-    edge = pl.BlockSpec((None, rows, 1), lambda f, *_: (f, 0, 0))
+    source = pl.BlockSpec((n_calib, None, None, row_dev, cols), lambda p, f, *_: (0, p, f, 0, 0))
+    block = pl.BlockSpec((None, rows, cols), lambda p, f, *_: (p * frame_dev + f, 0, 0))
+    edge = pl.BlockSpec((None, rows, 1), lambda p, f, *_: (p * frame_dev + f, 0, 0))
     grid_spec = pltpu.PrefetchScalarGridSpec(
         num_scalar_prefetch=3,
-        grid=(frames,),
-        in_specs=[block, pl.BlockSpec((rows, cols), lambda f, *_: (0, 0)), edge, edge],
+        grid=(n_peak, frame_dev),
+        in_specs=[source, pl.BlockSpec((rows, cols), lambda p, f, *_: (0, 0)), edge, edge],
         out_specs=[block, block],
     )
     return pl.pallas_call(
         lambda *refs: score_kernel(n_peak, levels, *refs),
         grid_spec=grid_spec,
-        out_shape=[jax.ShapeDtypeStruct(frame.shape, jnp.bfloat16)] * 2,
-    )(low, cycle_average, cycle_rms, frame, cycle, left, right)
+        out_shape=[jax.ShapeDtypeStruct((frames, rows, cols), jnp.bfloat16)] * 2,
+    )(low, cycle_average, cycle_rms, got, cycle, left, right)
 
 
 def laplace(padded):
@@ -345,7 +348,6 @@
     present_part = local_present(good, table, row_src, mrows, slot_rows)
     got = lax.all_to_all(send, ("calib", "peak"), 0, 0, tiled=True)
     got = got.reshape(n_calib, n_peak, frame_dev, row_dev, width_here)
-    frame = jnp.transpose(got, (1, 2, 0, 3, 4)).reshape(frames_all, mrows, width_here)
     slot = lax.axis_index("calib")
     col_dst = lax.axis_index("peak") * width_here + jnp.arange(width_here, dtype=jnp.int32)
     ypos = slot // SLOT_C * mrows + jnp.arange(mrows, dtype=jnp.int32)
@@ -354,17 +356,20 @@
     dx_two = 2 * xpos + 1 - SLOT_C * COLS
     cycle = cycle_index(dy_two[:, None] * dy_two[:, None] + dx_two[None, :] * dx_two[None, :])
     levels = jnp.arange(CYCLES, dtype=jnp.int32)
-    hits = (cycle.reshape(1, -1) == levels[:, None]).astype(jnp.bfloat16)
-    pixels = frame.reshape(frames_all, -1)
-    values = pixels.astype(jnp.float32)
+    hits = (cycle[None] == levels[:, None, None]).astype(jnp.bfloat16)
+    hits = hits.reshape(CYCLES, n_calib, row_dev, width_here)
+    values = got.astype(jnp.float32)
     square = values * values
     square_top = lax.reduce_precision(square, exponent_bits=8, mantissa_bits=7)
     square_hi = square_top.astype(jnp.bfloat16)
     square_lo = (square - square_top).astype(jnp.bfloat16)
-    stacked = jnp.concatenate([pixels, square_hi, square_lo], axis=0)
-    sums = jnp.einsum("fp,kp->fk", stacked, hits, preferred_element_type=jnp.float32)
-    first = sums[:frames_all]
-    second = sums[frames_all : 2 * frames_all] + sums[2 * frames_all :]
+
+    def cycle_sums(part):
+        sums = jnp.einsum("ipfrc,kirc->pfk", part, hits, preferred_element_type=jnp.float32)
+        return sums.reshape(frames_all, CYCLES)
+
+    first = cycle_sums(got)
+    second = cycle_sums(square_hi) + cycle_sums(square_lo)
     lanes = 128
     packed = jnp.concatenate(
         [
@@ -381,7 +386,8 @@
     present_flag = summed[0, 2 * CYCLES : 3 * CYCLES]
     cycle_average, cycle_rms = cycle_stats(first, second, present_flag)
     edge_cycle = jnp.stack([cycle[:, width_here - 1], cycle[:, 0]], axis=1)
-    edge_values = jnp.stack([frame[:, :, width_here - 1], frame[:, :, 0]], axis=2)
+    edge_values = jnp.stack([got[..., width_here - 1], got[..., 0]], axis=-1)
+    edge_values = jnp.transpose(edge_values, (1, 2, 0, 3, 4)).reshape(frames_all, mrows, 2)
     edge_hits = (edge_cycle.reshape(1, -1) == levels[:, None]).astype(jnp.float32)
     edge_table = jnp.einsum(
         "fk,kp->fp",
@@ -396,7 +402,7 @@
     bwd = [(i + 1, i) for i in range(n_peak - 1)]
     left = lax.ppermute(edge_score[:, :, :1], "peak", fwd)
     right = lax.ppermute(edge_score[:, :, 1:], "peak", bwd)
-    snr, bent = score_outputs(frame, cycle, cycle_average, cycle_rms, left, right, n_peak)
+    snr, bent = score_outputs(got, cycle, cycle_average, cycle_rms, left, right, n_peak)
     return (snr[:, None], bent[:, None])
 
 

time: 118 us -> 122 us (1.034)
  matrix products: 3.42 us -> 9.12 us
  local copies, waits for them, and re-layouts: 20.5 us -> 15.3 us
  waiting for transfers between devices: 20.9 us -> 23.7 us
    dot_general x1 -> x3, matrix products: 3.25 us -> 8.95 us  [cycle_sums(): jnp.einsum('ipfrc,kirc->pfk', part, hits, preferred_element_type=jnp.floa...]
    unnamed x18 -> x15, local copies, waits for them, and re-layouts: 3.2 us -> 0.79 us
    another operation x2 -> x1, local copies, waits for them, and re-layouts: 2.27 us -> 0.01 us  [the longest x1 2.27 us: body(): pixels = frame.reshape(frames_all, -1)]
    ppermute x1, waiting for transfers between devices: 0.01 us -> 1.84 us  [body(): right = lax.ppermute(edge_score[:, :, 1:], 'peak', bwd)]
    transpose x1 -> x0, local copies, waits for them, and re-layouts: 1.78 us -> none  [body(): jnp.transpose(got, (1, 2, 0, 3, 4)).reshape(frames_all, mrows, width_here)]
    ppermute x1, starting transfers between devices: 3.29 us -> 1.92 us  [body(): right = lax.ppermute(edge_score[:, :, 1:], 'peak', bwd)]
    slice x4 -> x3, local copies, waits for them, and re-layouts: 5.26 us -> 6.62 us  [body(): edge_values = jnp.stack([got[..., width_here - 1], got[..., 0]], axis=-1)]
    ppermute x1, starting transfers between devices: 3.78 us -> 5 us  [body(): left = lax.ppermute(edge_score[:, :, :1], 'peak', fwd)]
  transfers between devices with their start and end apart: 3 -> 3, of which waited for: 1 -> 2; matrix products, arithmetic and copies ran while one was open for 10% -> 9% of each run, Pallas kernels for 0% -> 0%
where the time goes in v7:
time: 122 us; the launch traced here: 121 us
  Pallas kernels  42 us (34%)
  waiting for transfers between devices  23.7 us (19%)
  starting transfers between devices  18.6 us (15%)
  local copies, waits for them, and re-layouts  15.3 us (13%)
  other arithmetic  11.8 us (10%)
  matrix products  9.12 us (7%)
    all_to_all x1, waiting for transfers between devices, body(): got = lax.all_to_all(send, ('calib', 'peak'), 0, 0, tiled=True)  21.8 us
    pallas_call x1, Pallas kernels, calibrate_send(): pl.pallas_call(lambda *refs: calibrate_kernel(group, *refs), grid_spec=gr...  16.2 us
    pallas_call x1, Pallas kernels, score_outputs(): pl.pallas_call(lambda *refs: score_kernel(n_peak, levels, *refs), grid_sp...  13.3 us
    pallas_call x1, Pallas kernels, gather_sum(): pl.pallas_call(lambda *refs: gather_sum_kernel(n_calib, n_peak, *refs), o...  12.4 us
    all_to_all x1, starting transfers between devices, body(): got = lax.all_to_all(send, ('calib', 'peak'), 0, 0, tiled=True)  11.7 us
    dot_general x3, matrix products, cycle_sums(): jnp.einsum('ipfrc,kirc->pfk', part, hits, preferred_element_type=jnp.floa...  8.95 us
    slice x3, local copies, waits for them, and re-layouts, body(): edge_values = jnp.stack([got[..., width_here - 1], got[..., 0]], axis=-1)  6.62 us
    ppermute x1, starting transfers between devices, body(): left = lax.ppermute(edge_score[:, :, :1], 'peak', fwd)  5 us
  transfers between devices with their start and end apart: 3, of which 2 were waited for; matrix products, arithmetic and copies ran while one was open for 9% of the time, Pallas kernels for 0%

profile of v7, /device:TPU:1, one launch (start us, length us, event | category | flops | bytes accessed | tf_op | source)
XLA Modules:
  0.0 121.4 jit_solution(6433376790198792632)
XLA Ops:
  0.6 0.8 copy.76
  1.4 0.7 reshape.193.refs_1_
  2.1 16.2 %shard_map.77 = bf16[32,4,2,16,256]{4,3,2,1,0:T(8,128)(2,1)} custom-call(s32[32]{0:T(128)} %refs_0_.1, s32[224]{0:T(256)} %reshape.193.refs_1_, s32[2,32,16,1024]{3,2,1,0:T(8,128)} %refs_2_.1, f32[3,32,16,1024]{3,2,1,0:T(8,128)} %refs_3_.1, bf16[3,32,16,1024]{3,2,1,0:T(8,128)(2,1)} %refs_4_.1, s32[32,16,1024]{2,1,0:T(8,128)} %refs_5_.1), custom_call_target="tpu_custom_call" | custom-call | tf_op jit(solution)/shard_map/pallas_call | solution.py:131
  18.3 11.7 %all-to-all-start = ((bf16[128,2,16,256]{3,2,1,0:T(8,128)(2,1)}), bf16[128,2,16,256]{3,2,1,0:T(8,128)(2,1)S(1)}, u32[]{:S(2)}, u32[]{:S(2)}) async-start(bf16[128,2,16,256]{3,2,1,0:T(8,128)(2,1)} %bitcast.53), calls=%async_computation | async-start | bytes 4194304 | tf_op jit(solution)/shard_map/all_to_all | solution.py:349
  30.2 1.6 %convert_reduce_fusion.1.refs_4_ = s32[512,256]{1,0:T(8,128)S(1)} fusion(s32[512,256]{1,0:T(8,128)S(1)} %broadcast_add_fusion.1, s32[31]{0:T(128)S(1)} %multiply_multiply_fusion), kind=kLoop, calls=%fused_computation.7 | loop fusion | flops 12058624 | bytes 1048700 | tf_op jit(solution)/shard_map/reduce_sum | solution.py:34
  32.6 1.1 constant_dynamic-slice_fusion
  33.9 1.7 %convert_reduce_fusion = s32[32,16,256]{2,1,0:T(8,128)S(1)} fusion(s32[32,16,256]{2,1,0:T(8,128)S(1)} %broadcast_add_fusion, s32[31]{0:T(128)S(1)} %multiply_multiply_fusion), kind=kLoop, calls=%fused_computation.6 | loop fusion | flops 12058624 | bytes 1048700 | tf_op jit(solution)/shard_map/reduce_sum | solution.py:34
  35.6 2.5 %select_reduce_fusion = s32[32]{0:T(128)S(1)} fusion(s32[32,16,256]{2,1,0:T(8,128)S(1)} %constant_dynamic-slice_fusion, s32[32,16,256]{2,1,0:T(8,128)S(1)} %convert_reduce_fusion), kind=kLoop, calls=%fused_computation | loop fusion | flops 12582880 | bytes 1048704 | tf_op jit(solution)/shard_map/reduce_sum | solution.py:219
  38.0 21.8 %all-to-all-done = bf16[128,2,16,256]{3,2,1,0:T(8,128)(2,1)S(1)} async-done(((bf16[128,2,16,256]{3,2,1,0:T(8,128)(2,1)}), bf16[128,2,16,256]{3,2,1,0:T(8,128)(2,1)S(1)}, u32[]{:S(2)}, u32[]{:S(2)}) %all-to-all-start) | async-done | bytes 2097184 | tf_op jit(solution)/shard_map/all_to_all | solution.py:349
  59.9 1.9 %fusion.32 = (bf16[32,4,2,16,1]{4,3,2,1,0:T(8,128)(2,1)}, bf16[32,4,2,16,1]{4,3,2,1,0:T(8,128)(2,1)}) fusion(bf16[32,4,2,16,256]{4,3,2,1,0:T(8,128)(2,1)S(1)} %bitcast.46), kind=kLoop, calls=%fused_computation.58 | loop fusion | bytes 32768 | tf_op jit(solution)/shard_map/slice | solution.py:389
  61.8 3.0 %fusion.6 = (bf16[32,4,2,16,256]{4,3,2,1,0:T(8,128)(2,1)}, bf16[32,4,2,16,256]{4,3,2,1,0:T(8,128)(2,1)}) fusion(bf16[32,4,2,16,256]{4,3,2,1,0:T(8,128)(2,1)S(1)} %bitcast.47), kind=kLoop, calls=%fused_computation.13 | loop fusion | flops 6291456 | bytes 6291456 | tf_op jit(solution)/shard_map/convert_element_type | solution.py:365
  64.8 2.3 %copy.81 = bf16[32,4,2,16,1]{0,3,4,2,1:T(8,128)(2,1)S(1)} copy(bf16[32,4,2,16,1]{4,3,2,1,0:T(8,128)(2,1)} %get-tuple-element.30) | data formatting | bytes 16384 | tf_op jit(solution)/shard_map/slice | solution.py:389
  67.2 2.3 %copy.82 = bf16[32,4,2,16,1]{0,3,4,2,1:T(8,128)(2,1)S(1)} copy(bf16[32,4,2,16,1]{4,3,2,1,0:T(8,128)(2,1)} %get-tuple-element.31) | data formatting | bytes 16384 | tf_op jit(solution)/shard_map/slice | solution.py:389
  69.9 3.1 %fusion.10 = f32[8,32]{1,0:T(8,128)S(1)} fusion(s32[32,16,256]{2,1,0:T(8,128)S(1)} %bitcast.50, bf16[8,256,32,16]{1,3,0,2:T(8,128)(2,1)S(1)} %bitcast.48), kind=kOutput, calls=%fused_computation.18 | convolution fusion | flops 71303168 | bytes 2622464 | tf_op jit(solution)/shard_map/ipfrc,kirc->pfk/dot_general | solution.py:368
  73.0 2.9 %fusion.13 = f32[8,32]{1,0:T(8,128)S(1)} fusion(s32[32,16,256]{2,1,0:T(8,128)S(1)} %bitcast.51, bf16[8,256,32,16]{1,3,0,2:T(8,128)(2,1)S(1)} %bitcast.55), kind=kOutput, calls=%fused_computation.19 | convolution fusion | flops 71303168 | bytes 2622464 | tf_op jit(solution)/shard_map/ipfrc,kirc->pfk/dot_general | solution.py:368
  75.9 3.0 %fusion.19 = f32[8,32]{1,0:T(8,128)S(1)} fusion(f32[8,32]{1,0:T(8,128)S(1)} %fusion.13, s32[32,16,256]{2,1,0:T(8,128)S(1)} %bitcast.52, bf16[8,256,32,16]{1,3,0,2:T(8,128)(2,1)S(1)} %bitcast.54), kind=kOutput, calls=%fused_computation.21 | convolution fusion | flops 71303424 | bytes 2623488 | tf_op jit(solution)/shard_map/ipfrc,kirc->pfk/dot_general | solution.py:368
  78.8 0.7 fusion.27.refs_0_
  79.5 12.4 %shard_map.78 = f32[8,128]{1,0:T(8,128)} custom-call(f32[8,128]{1,0:T(8,128)} %fusion.27.refs_0_), custom_call_target="tpu_custom_call" | custom-call | tf_op jit(solution)/shard_map/pallas_call | solution.py:313
  91.9 0.8 slice_bitcast_fusion
  92.7 0.8 add_sqrt_fusion
  93.5 0.2 fusion.22
  93.7 0.2 copy.84
  93.9 0.2 copy.85
  94.1 0.2 copy.86
  94.3 0.2 copy.87
  94.5 5.0 %collective-permute-start = (f32[8,512,1]{1,0,2:T(8,128)S(1)}, f32[8,512,1]{1,0,2:T(8,128)S(1)}, u32[]{:S(2)}, u32[]{:S(2)}) collective-permute-start(f32[8,512,1]{1,0,2:T(8,128)S(1)} %get-tuple-element.39), channel_id=1, source_target_pairs={{0,1},{1,2},{2,3},{4,5},{5,6},{6,7},{8,9},{9,10},{10,11},{12,13},{... | collective-permute-start | bytes 49160 | tf_op jit(solution)/shard_map/ppermute | solution.py:403
  99.5 1.9 %collective-permute-start.1 = (f32[8,512,1]{1,0,2:T(8,128)S(1)}, f32[8,512,1]{1,0,2:T(8,128)S(1)}, u32[]{:S(2)}, u32[]{:S(2)}) collective-permute-start(f32[8,512,1]{1,0,2:T(8,128)S(1)} %get-tuple-element.38), channel_id=1, source_target_pairs={{1,0},{2,1},{3,2},{5,4},{6,5},{7,6},{9,8},{10,9},{11,10},{13,12},{... | collective-permute-start | bytes 49160 | tf_op jit(solution)/shard_map/ppermute | solution.py:404
  101.5 0.8 reduce_min.9
  102.3 2.0 %copy.88.refs_5_ = f32[8,512,1]{2,1,0:T(8,128)} copy(f32[8,512,1]{1,0,2:T(8,128)S(1)} %collective-permute-done) | data formatting | bytes 32768 | tf_op jit(solution)/shard_map/ppermute | solution.py:403
  104.3 1.8 %collective-permute-done.1 = f32[8,512,1]{1,0,2:T(8,128)S(1)} collective-permute-done((f32[8,512,1]{1,0,2:T(8,128)S(1)}, f32[8,512,1]{1,0,2:T(8,128)S(1)}, u32[]{:S(2)}, u32[]{:S(2)}) %collective-permute-start.1) | collective-permute-done | bytes 16416 | tf_op jit(solution)/shard_map/ppermute | solution.py:404
  106.1 2.0 %copy.89.refs_6_ = f32[8,512,1]{2,1,0:T(8,128)} copy(f32[8,512,1]{1,0,2:T(8,128)S(1)} %collective-permute-done.1) | data formatting | bytes 32768 | tf_op jit(solution)/shard_map/ppermute | solution.py:404
  108.1 13.3 %shard_map.79 = (bf16[8,512,256]{2,1,0:T(8,128)(2,1)}, bf16[8,512,256]{2,1,0:T(8,128)(2,1)}) custom-call(s32[1]{0:T(128)} %bitcast.refs_0_, f32[8,32]{1,0:T(8,128)} %copy-done.5, f32[8,32]{1,0:T(8,128)} %copy-done.4, bf16[32,4,2,16,256]{4,3,2,1,0:T(8,128)(2,1)} %bitcast.49, s32[512,256]{1,0:T(8,128)} %copy-done.1, f32[8,512,1]{2,1,0:T(8,128)} %copy.88.refs_5_, ...), custom_call_target="tpu_custom_call" | custom-call | tf_op jit(solution)/shard_map/pallas_call | solution.py:187
  (37 shorter events, 1.4 us)
Async XLA Ops:
  18.3 11.7 %copy-start.6 = (s32[32]{0:T(128)S(1)}, s32[32]{0:T(128)}, u32[]{:S(2)}) copy-start(s32[32]{0:T(128)} %refs_0_.1) | copy-start | bytes 388
  18.3 41.6 %all-to-all-start = ((bf16[128,2,16,256]{3,2,1,0:T(8,128)(2,1)}), bf16[128,2,16,256]{3,2,1,0:T(8,128)(2,1)S(1)}, u32[]{:S(2)}, u32[]{:S(2)}) async-start(bf16[128,2,16,256]{3,2,1,0:T(8,128)(2,1)} %bitcast.53), calls=%async_computation | async-start | bytes 4194304 | tf_op jit(solution)/shard_map/all_to_all | solution.py:349
  31.9 69.6 %copy-start.1 = (s32[512,256]{1,0:T(8,128)}, s32[512,256]{1,0:T(8,128)S(1)}, u32[]{:S(2)}) copy-start(s32[512,256]{1,0:T(8,128)S(1)} %convert_reduce_fusion.1.refs_4_) | copy-start | bytes 1572868
  59.9 10.0 %copy-start = (bf16[128,2,16,256]{3,2,1,0:T(8,128)(2,1)}, bf16[128,2,16,256]{3,2,1,0:T(8,128)(2,1)S(1)}, u32[]{:S(2)}) copy-start(bf16[128,2,16,256]{3,2,1,0:T(8,128)(2,1)S(1)} %all-to-all-done) | copy-start | bytes 6291460
  69.9 3.1 %copy-start.3 = (bf16[32,4,2,16,256]{4,3,2,1,0:T(8,128)(2,1)S(1)}, bf16[32,4,2,16,256]{4,3,2,1,0:T(8,128)(2,1)}, u32[]{:S(2)}) copy-start(bf16[32,4,2,16,256]{4,3,2,1,0:T(8,128)(2,1)} %get-tuple-element.33) | copy-start | bytes 6291460
  73.0 2.9 %copy-start.2 = (bf16[32,4,2,16,256]{4,3,2,1,0:T(8,128)(2,1)S(1)}, bf16[32,4,2,16,256]{4,3,2,1,0:T(8,128)(2,1)}, u32[]{:S(2)}) copy-start(bf16[32,4,2,16,256]{4,3,2,1,0:T(8,128)(2,1)} %get-tuple-element.32) | copy-start | bytes 6291460
  93.5 14.6 %copy-start.4 = (f32[8,32]{1,0:T(8,128)}, f32[8,32]{1,0:T(8,128)S(1)}, u32[]{:S(2)}) copy-start(f32[8,32]{1,0:T(8,128)S(1)} %get-tuple-element.40.refs_2_) | copy-start | bytes 3076
  93.5 14.6 %copy-start.5 = (f32[8,32]{1,0:T(8,128)}, f32[8,32]{1,0:T(8,128)S(1)}, u32[]{:S(2)}) copy-start(f32[8,32]{1,0:T(8,128)S(1)} %get-tuple-element.41.refs_1_) | copy-start | bytes 3076
  94.5 7.8 %collective-permute-start = (f32[8,512,1]{1,0,2:T(8,128)S(1)}, f32[8,512,1]{1,0,2:T(8,128)S(1)}, u32[]{:S(2)}, u32[]{:S(2)}) collective-permute-start(f32[8,512,1]{1,0,2:T(8,128)S(1)} %get-tuple-element.39), channel_id=1, source_target_pairs={{0,1},{1,2},{2,3},{4,5},{5,6},{6,7},{8,9},{9,10},{10,11},{12,13},{... | collective-permute-start | bytes 49160 | tf_op jit(solution)/shard_map/ppermute | solution.py:403
  99.5 6.6 %collective-permute-start.1 = (f32[8,512,1]{1,0,2:T(8,128)S(1)}, f32[8,512,1]{1,0,2:T(8,128)S(1)}, u32[]{:S(2)}, u32[]{:S(2)}) collective-permute-start(f32[8,512,1]{1,0,2:T(8,128)S(1)} %get-tuple-element.38), channel_id=1, source_target_pairs={{1,0},{2,1},{3,2},{5,4},{6,5},{7,6},{9,8},{10,9},{11,10},{13,12},{... | collective-permute-start | bytes 49160 | tf_op jit(solution)/shard_map/ppermute | solution.py:404

commit v8 on v6

--- a/solution.py
+++ b/solution.py
@@ -135,7 +135,10 @@
     )(table, bounds.reshape(-1), raw, pedestal, gain, good)
 
 
-def score_kernel(n_peak, levels, low_ref, mean_ref, rms_ref, frame_ref, cycle_ref, left_ref, right_ref, snr_ref, bent_ref):
+def score_kernel(
+    n_peak, levels, low_ref, mean_ref, rms_ref, frame_ref, cycle_ref, left_ref, right_ref,
+    left_cycle_ref, right_cycle_ref, snr_ref, bent_ref
+):
     frame_pos = pl.program_id(0)
     cycle = cycle_ref[...]
     values = frame_ref[...].astype(jnp.float32)
@@ -152,8 +155,20 @@
     peak_pos = lax.axis_index("peak")
     row_ids = lax.broadcasted_iota(jnp.int32, (rows, cols), 0)
     col_ids = lax.broadcasted_iota(jnp.int32, (rows, cols), 1)
-    left_col = jnp.where(peak_pos == 0, 0.0, left_ref[...])
-    right_col = jnp.where(peak_pos == n_peak - 1, 0.0, right_ref[...])
+    def edge_score(edge_ref, edge_cycle_ref):
+        edge_values = edge_ref[...].astype(jnp.float32)
+        edge_cycle = edge_cycle_ref[...]
+        edge_mean = jnp.zeros(edge_values.shape, jnp.float32)
+        edge_rms = jnp.ones(edge_values.shape, jnp.float32)
+        for j in range(levels):
+            level = jnp.minimum(low_ref[0] + j, tops)
+            hit = edge_cycle == level
+            edge_mean = jnp.where(hit, mean_ref[frame_pos, level], edge_mean)
+            edge_rms = jnp.where(hit, rms_ref[frame_pos, level], edge_rms)
+        return (edge_values - edge_mean) / edge_rms
+
+    left_col = jnp.where(peak_pos == 0, 0.0, edge_score(left_ref, left_cycle_ref))
+    right_col = jnp.where(peak_pos == n_peak - 1, 0.0, edge_score(right_ref, right_cycle_ref))
     total = 4.0 * score
     for shift in (1, rows - 1):
         moved = pltpu.roll(score, shift, 0)
@@ -168,24 +183,25 @@
     bent_ref[...] = total.astype(bent_ref.dtype)
 
 
-def score_outputs(frame, cycle, cycle_average, cycle_rms, left, right, n_peak):
+def score_outputs(frame, cycle, low, cycle_average, cycle_rms, left, right, left_cycle, right_cycle, n_peak):
     frames, rows, cols = frame.shape
-    span = (rows * rows + cols * cols) ** 0.5
+    span = (rows * rows + (cols + 2) * (cols + 2)) ** 0.5
     levels = min(CYCLES, int(span // CYCLE_W) + 3)
-    low = jnp.min(cycle).reshape(1)
     block = pl.BlockSpec((None, rows, cols), lambda f, *_: (f, 0, 0))
     edge = pl.BlockSpec((None, rows, 1), lambda f, *_: (f, 0, 0))
+    fixed = pl.BlockSpec((rows, cols), lambda f, *_: (0, 0))
+    fixed_edge = pl.BlockSpec((rows, 1), lambda f, *_: (0, 0))
     grid_spec = pltpu.PrefetchScalarGridSpec(
         num_scalar_prefetch=3,
         grid=(frames,),
-        in_specs=[block, pl.BlockSpec((rows, cols), lambda f, *_: (0, 0)), edge, edge],
+        in_specs=[block, fixed, edge, edge, fixed_edge, fixed_edge],
         out_specs=[block, block],
     )
     return pl.pallas_call(
         lambda *refs: score_kernel(n_peak, levels, *refs),
         grid_spec=grid_spec,
         out_shape=[jax.ShapeDtypeStruct(frame.shape, jnp.bfloat16)] * 2,
-    )(low, cycle_average, cycle_rms, frame, cycle, left, right)
+    )(low, cycle_average, cycle_rms, frame, cycle, left, right, left_cycle, right_cycle)
 
 
 def laplace(padded):
@@ -304,13 +320,15 @@
     o_ref[...] = lax.fori_loop(0, n_calib, add_far, jnp.zeros(x_ref.shape, x_ref.dtype))
 
 
-def gather_sum(x):
+def gather_sum(x, *after):
     n_calib = lax.axis_size("calib")
     n_peak = lax.axis_size("peak")
+    held = len(after)
     return pl.pallas_call(
-        lambda *refs: gather_sum_kernel(n_calib, n_peak, *refs),
+        lambda x_ref, *refs: gather_sum_kernel(n_calib, n_peak, x_ref, *refs[held:]),
         out_shape=jax.ShapeDtypeStruct(x.shape, x.dtype),
-        in_specs=[pl.BlockSpec(memory_space=pltpu.VMEM)],
+        in_specs=[pl.BlockSpec(memory_space=pltpu.VMEM)]
+        + [pl.BlockSpec(memory_space=pl.ANY)] * held,
         out_specs=pl.BlockSpec(memory_space=pltpu.VMEM),
         scratch_shapes=[
             pltpu.VMEM((n_peak,) + x.shape, x.dtype),
@@ -322,7 +340,7 @@
             pltpu.SemaphoreType.DMA,
         ],
         compiler_params=pltpu.CompilerParams(collective_id=0, has_side_effects=True),
-    )(x)
+    )(x, *after)
 
 
 def cycle_stats(first, second, present_flag):
@@ -353,6 +371,15 @@
     dy_two = 2 * ypos + 1 - slot_rows * mrows
     dx_two = 2 * xpos + 1 - SLOT_C * COLS
     cycle = cycle_index(dy_two[:, None] * dy_two[:, None] + dx_two[None, :] * dx_two[None, :])
+    side_x = jnp.stack([dx_two[0] - 2, dx_two[width_here - 1] + 2])
+    side_cycle = cycle_index(dy_two[:, None] * dy_two[:, None] + side_x[None, :] * side_x[None, :])
+    left_cycle = side_cycle[:, :1]
+    right_cycle = side_cycle[:, 1:]
+    low = jnp.minimum(jnp.min(cycle), jnp.min(side_cycle)).reshape(1)
+    fwd = [(i, i + 1) for i in range(n_peak - 1)]
+    bwd = [(i + 1, i) for i in range(n_peak - 1)]
+    left = lax.ppermute(frame[:, :, width_here - 1 :], "peak", fwd)
+    right = lax.ppermute(frame[:, :, :1], "peak", bwd)
     levels = jnp.arange(CYCLES, dtype=jnp.int32)
     hits = (cycle.reshape(1, -1) == levels[:, None]).astype(jnp.bfloat16)
     pixels = frame.reshape(frames_all, -1)
@@ -375,28 +402,14 @@
         ],
         axis=1,
     )
-    summed = gather_sum(packed)
+    summed = gather_sum(packed, left, right)
     first = summed[:, :CYCLES]
     second = summed[:, CYCLES : 2 * CYCLES]
     present_flag = summed[0, 2 * CYCLES : 3 * CYCLES]
     cycle_average, cycle_rms = cycle_stats(first, second, present_flag)
-    edge_cycle = jnp.stack([cycle[:, width_here - 1], cycle[:, 0]], axis=1)
-    edge_values = jnp.stack([frame[:, :, width_here - 1], frame[:, :, 0]], axis=2)
-    edge_hits = (edge_cycle.reshape(1, -1) == levels[:, None]).astype(jnp.float32)
-    edge_table = jnp.einsum(
-        "fk,kp->fp",
-        jnp.concatenate([cycle_average, cycle_rms], axis=0),
-        edge_hits,
-        precision=precise_variant,
-    ).reshape(2 * frames_all, mrows, 2)
-    edge_mean = edge_table[:frames_all]
-    edge_rms = edge_table[frames_all:]
-    edge_score = (edge_values.astype(jnp.float32) - edge_mean) / edge_rms
-    fwd = [(i, i + 1) for i in range(n_peak - 1)]
-    bwd = [(i + 1, i) for i in range(n_peak - 1)]
-    left = lax.ppermute(edge_score[:, :, :1], "peak", fwd)
-    right = lax.ppermute(edge_score[:, :, 1:], "peak", bwd)
-    snr, bent = score_outputs(frame, cycle, cycle_average, cycle_rms, left, right, n_peak)
+    snr, bent = score_outputs(
+        frame, cycle, low, cycle_average, cycle_rms, left, right, left_cycle, right_cycle, n_peak
+    )
     return (snr[:, None], bent[:, None])
 
 

time: 118 us -> 118 us (level)
  Pallas kernels: 42 us -> 45 us
  waiting for transfers between devices: 20.9 us -> 17.9 us
  local copies, waits for them, and re-layouts: 20.5 us -> 17.7 us
  between operations: 0.94 us -> 3.33 us
  other arithmetic: 11.1 us -> 12.5 us
    all_to_all x1, waiting for transfers between devices: 20.9 us -> 15.6 us  [body(): got = lax.all_to_all(send, ('calib', 'peak'), 0, 0, tiled=True)]
    pallas_call x1, Pallas kernels: 13.4 us -> 17.3 us  [score_outputs(): pl.pallas_call(lambda *refs: score_kernel(n_peak, levels, *refs), grid_sp...]
    ppermute x2, waiting for transfers between devices: 0.01 us -> 2.24 us  [the longest x1 2.24 us: body(): right = lax.ppermute(frame[:, :, :1], 'peak', bwd)]
    slice x10 -> x5, local copies, waits for them, and re-layouts: 6.28 us -> 4.04 us  [the longest x2 1.85 us: body(): right = lax.ppermute(frame[:, :, :1], 'peak', bwd)]
    unnamed x18 -> x14, local copies, waits for them, and re-layouts: 3.2 us -> 4.1 us
    reduce_sum x2 -> x3, other arithmetic: 3.34 us -> 3.48 us  [cycle_index(): return jnp.sum((dist[..., None] >= lows).astype(jnp.int32), axis=-1)]
  transfers between devices with their start and end apart: 3 -> 3, of which waited for: 1 -> 2; matrix products, arithmetic and copies ran while one was open for 10% -> 12% of each run, Pallas kernels for 0% -> 0%
where the time goes in v8:
time: 118 us; the launch traced here: 117 us
  Pallas kernels  45 us (38%)
  waiting for transfers between devices  17.9 us (15%)
  local copies, waits for them, and re-layouts  17.7 us (15%)
  starting transfers between devices  17.5 us (15%)
  other arithmetic  12.5 us (11%)
  between operations  3.33 us (3%)
  matrix products  3.25 us (3%)
    pallas_call x1, Pallas kernels, score_outputs(): pl.pallas_call(lambda *refs: score_kernel(n_peak, levels, *refs), grid_sp...  17.3 us
    pallas_call x1, Pallas kernels, calibrate_send(): pl.pallas_call(lambda *refs: calibrate_kernel(group, *refs), grid_spec=gr...  16.2 us
    all_to_all x1, waiting for transfers between devices, body(): got = lax.all_to_all(send, ('calib', 'peak'), 0, 0, tiled=True)  15.6 us
    all_to_all x1, starting transfers between devices, body(): got = lax.all_to_all(send, ('calib', 'peak'), 0, 0, tiled=True)  11.5 us
    pallas_call x1, Pallas kernels, gather_sum(): pl.pallas_call(lambda x_ref, *refs: gather_sum_kernel(n_calib, n_peak, x_...  11.4 us
    unnamed x14, local copies, waits for them, and re-layouts  4.1 us
    ppermute x1, starting transfers between devices, body(): left = lax.ppermute(frame[:, :, width_here - 1:], 'peak', fwd)  3.87 us
    reduce_sum x3, other arithmetic, cycle_index(): return jnp.sum((dist[..., None] >= lows).astype(jnp.int32), axis=-1)  3.48 us
  transfers between devices with their start and end apart: 3, of which 2 were waited for; matrix products, arithmetic and copies ran while one was open for 12% of the time, Pallas kernels for 0%

profile of v8, /device:TPU:1, one launch (start us, length us, event | category | flops | bytes accessed | tf_op | source)
XLA Modules:
  0.0 117.2 jit_solution(11069620394919209641)
XLA Ops:
  0.6 0.8 copy.43
  1.4 0.7 reshape.231.refs_1_
  2.1 16.2 %shard_map.77 = bf16[32,4,2,16,256]{4,3,2,1,0:T(8,128)(2,1)} custom-call(s32[32]{0:T(128)} %refs_0_.1, s32[224]{0:T(256)} %reshape.231.refs_1_, s32[2,32,16,1024]{3,2,1,0:T(8,128)} %refs_2_.1, f32[3,32,16,1024]{3,2,1,0:T(8,128)} %refs_3_.1, bf16[3,32,16,1024]{3,2,1,0:T(8,128)(2,1)} %refs_4_.1, s32[32,16,1024]{2,1,0:T(8,128)} %refs_5_.1), custom_call_target="tpu_custom_call" | custom-call | tf_op jit(solution)/shard_map/pallas_call | solution.py:131
  18.3 11.5 %all-to-all-start = ((bf16[128,2,16,256]{3,2,1,0:T(8,128)(2,1)}), bf16[128,2,16,256]{3,2,1,0:T(8,128)(2,1)S(1)}, u32[]{:S(2)}, u32[]{:S(2)}) async-start(bf16[128,2,16,256]{3,2,1,0:T(8,128)(2,1)} %bitcast.24), calls=%async_computation | async-start | bytes 4194304 | tf_op jit(solution)/shard_map/all_to_all | solution.py:364
  30.0 1.6 %convert_reduce_fusion.1.refs_4_ = s32[512,256]{1,0:T(8,128)S(1)} fusion(s32[512,256]{1,0:T(8,128)S(1)} %broadcast_add_fusion.1, s32[31]{0:T(128)S(1)} %multiply_multiply_fusion), kind=kLoop, calls=%fused_computation.5 | loop fusion | flops 12058624 | bytes 1048700 | tf_op jit(solution)/shard_map/reduce_sum | solution.py:34
  32.2 0.8 reduce_min.18
  32.9 0.6 fusion.18
  35.0 0.7 reduce_min.19
  35.7 0.9 copy.57.refs_7_
  36.6 0.9 copy.58.refs_8_
  38.8 1.1 constant_dynamic-slice_fusion
  40.1 1.7 %convert_reduce_fusion = s32[32,16,256]{2,1,0:T(8,128)S(1)} fusion(s32[32,16,256]{2,1,0:T(8,128)S(1)} %broadcast_add_fusion, s32[31]{0:T(128)S(1)} %multiply_multiply_fusion), kind=kLoop, calls=%fused_computation.4 | loop fusion | flops 12058624 | bytes 1048700 | tf_op jit(solution)/shard_map/reduce_sum | solution.py:34
  41.8 2.5 %select_reduce_fusion = s32[32]{0:T(128)S(1)} fusion(s32[32,16,256]{2,1,0:T(8,128)S(1)} %constant_dynamic-slice_fusion, s32[32,16,256]{2,1,0:T(8,128)S(1)} %convert_reduce_fusion), kind=kLoop, calls=%fused_computation | loop fusion | flops 12582880 | bytes 1048704 | tf_op jit(solution)/shard_map/reduce_sum | solution.py:232
  44.3 15.6 %all-to-all-done = bf16[128,2,16,256]{3,2,1,0:T(8,128)(2,1)S(1)} async-done(((bf16[128,2,16,256]{3,2,1,0:T(8,128)(2,1)}), bf16[128,2,16,256]{3,2,1,0:T(8,128)(2,1)S(1)}, u32[]{:S(2)}, u32[]{:S(2)}) %all-to-all-start) | async-done | bytes 2097184 | tf_op jit(solution)/shard_map/all_to_all | solution.py:364
  59.9 1.3 %copy-done.2 = bf16[128,2,16,256]{3,2,1,0:T(8,128)(2,1)} copy-done((bf16[128,2,16,256]{3,2,1,0:T(8,128)(2,1)}, bf16[128,2,16,256]{3,2,1,0:T(8,128)(2,1)S(1)}, u32[]{:S(2)}) %copy-start.2) | copy-done | bytes 2097176
  61.2 1.8 %copy.44 = bf16[4,2,32,16,256]{4,3,2,1,0:T(8,128)(2,1)S(1)} copy(bf16[4,2,32,16,256]{4,3,1,0,2:T(8,128)(2,1)} %bitcast.22) | data formatting | bytes 4194304 | tf_op jit(solution)/shard_map/transpose | solution.py:366
  63.0 2.3 %reshape_reshape.3 = bf16[8,131072]{1,0:T(8,128)(2,1)} reshape(bf16[4,2,32,16,256]{4,3,2,1,0:T(8,128)(2,1)S(1)} %copy.44) | data formatting | bytes 4194304 | tf_op jit(solution)/shard_map/reshape;reshape | solution.py:385
  65.3 2.4 %reduce-precision_convert_fusion = (bf16[8,131072]{1,0:T(8,128)(2,1)S(1)}, bf16[8,131072]{1,0:T(8,128)(2,1)S(1)}) fusion(bf16[8,131072]{1,0:T(8,128)(2,1)} %reshape_reshape.3), kind=kLoop, calls=%fused_computation.13 | loop fusion | flops 6291456 | bytes 6291456 | tf_op jit(solution)/shard_map/convert_element_type | solution.py:389
  67.7 3.2 %fusion = f32[24,32]{1,0:T(8,128)S(1)} fusion(s32[131072]{0:T(1024)S(1)} %bitcast.25, bf16[8,131072]{1,0:T(8,128)(2,1)S(1)} %get-tuple-element.33, bf16[8,131072]{1,0:T(8,128)(2,1)S(1)} %get-tuple-element.32, bf16[8,131072]{1,0:T(8,128)(2,1)S(1)} %copy-done.1), kind=kOutput, calls=%fused_computation.3 | convolution fusion | flops 224395264 | bytes 6818816 | tf_op jit(solution)/shard_map/fp,kp->fk/dot_general | solution.py:392
  71.0 1.5 %fusion.15 = (bf16[8,512,1]{2,1,0:T(8,128)(2,1)S(1)}, bf16[8,512,1]{2,1,0:T(8,128)(2,1)}) fusion(bf16[8,512,256]{2,1,0:T(8,128)(2,1)S(1)} %bitcast.20), kind=kLoop, calls=%fused_computation.49 | loop fusion | bytes 32768 | tf_op jit(solution)/shard_map/slice | solution.py:382
  72.5 1.6 %copy.47 = bf16[8,512,1]{1,0,2:T(8,128)(2,1)S(1)} copy(bf16[8,512,1]{2,1,0:T(8,128)(2,1)} %get-tuple-element.31) | data formatting | bytes 16384 | tf_op jit(solution)/shard_map/slice | solution.py:381
  74.0 3.9 %collective-permute-start = (bf16[8,512,1]{1,0,2:T(8,128)(2,1)S(1)}, bf16[8,512,1]{1,0,2:T(8,128)(2,1)S(1)}, u32[]{:S(2)}, u32[]{:S(2)}) collective-permute-start(bf16[8,512,1]{1,0,2:T(8,128)(2,1)S(1)} %copy.47), channel_id=1, source_target_pairs={{0,1},{1,2},{2,3},{4,5},{5,6},{6,7},{8,9},{9,10},{10,11},{12,13},{... | collective-permute-start | bytes 24584 | tf_op jit(solution)/shard_map/ppermute | solution.py:381
  77.9 0.4 copy.48
  78.3 2.1 %collective-permute-start.1 = (bf16[8,512,1]{1,0,2:T(8,128)(2,1)S(1)}, bf16[8,512,1]{1,0,2:T(8,128)(2,1)S(1)}, u32[]{:S(2)}, u32[]{:S(2)}) collective-permute-start(bf16[8,512,1]{1,0,2:T(8,128)(2,1)S(1)} %copy.48), channel_id=1, source_target_pairs={{1,0},{2,1},{3,2},{5,4},{6,5},{7,6},{9,8},{10,9},{11,10},{13,12},{... | collective-permute-start | bytes 24584 | tf_op jit(solution)/shard_map/ppermute | solution.py:382
  80.4 0.7 fusion.9.x_ref
  81.1 1.4 %copy.49.refs_0_.refs_5_ = bf16[8,512,1]{2,1,0:T(8,128)(2,1)} copy(bf16[8,512,1]{1,0,2:T(8,128)(2,1)S(1)} %collective-permute-done) | data formatting | bytes 16384 | tf_op jit(solution)/shard_map/ppermute | solution.py:381
  82.5 2.2 %collective-permute-done.1 = bf16[8,512,1]{1,0,2:T(8,128)(2,1)S(1)} collective-permute-done((bf16[8,512,1]{1,0,2:T(8,128)(2,1)S(1)}, bf16[8,512,1]{1,0,2:T(8,128)(2,1)S(1)}, u32[]{:S(2)}, u32[]{:S(2)}) %collective-permute-start.1) | collective-permute-done | bytes 8224 | tf_op jit(solution)/shard_map/ppermute | solution.py:382
  84.8 1.4 %copy.50.refs_1_.refs_6_ = bf16[8,512,1]{2,1,0:T(8,128)(2,1)} copy(bf16[8,512,1]{1,0,2:T(8,128)(2,1)S(1)} %collective-permute-done.1) | data formatting | bytes 16384 | tf_op jit(solution)/shard_map/ppermute | solution.py:382
  86.2 11.4 %shard_map.78 = f32[8,128]{1,0:T(8,128)} custom-call(f32[8,128]{1,0:T(8,128)} %fusion.9.x_ref, bf16[8,512,1]{2,1,0:T(8,128)(2,1)} %copy.49.refs_0_.refs_5_, bf16[8,512,1]{2,1,0:T(8,128)(2,1)} %copy.50.refs_1_.refs_6_), custom_call_target="tpu_custom_call" | custom-call | tf_op jit(solution)/shard_map/pallas_call | solution.py:327
  97.6 0.8 slice_bitcast_fusion
  98.4 1.4 %add_sqrt_fusion = (f32[8,32]{1,0:T(8,128)}, f32[8,32]{1,0:T(8,128)}) fusion(f32[8,128]{1,0:T(8,128)} %shard_map.78, f32[32]{0:T(128)S(1)} %slice_bitcast_fusion), kind=kLoop, calls=%fused_computation.27 | loop fusion | flops 768 | bytes 4224 | tf_op jit(solution)/shard_map/sqrt | solution.py:348
  99.8 17.3 %shard_map.79 = (bf16[8,512,256]{2,1,0:T(8,128)(2,1)}, bf16[8,512,256]{2,1,0:T(8,128)(2,1)}) custom-call(s32[1]{0:T(128)} %bitcast.refs_0_, f32[8,32]{1,0:T(8,128)} %get-tuple-element.37.refs_1_, f32[8,32]{1,0:T(8,128)} %get-tuple-element.36.refs_2_, bf16[8,512,256]{2,1,0:T(8,128)(2,1)} %bitcast.21, s32[512,256]{1,0:T(8,128)} %copy-done.3, ...), custom_call_target="tpu_custom_call" | custom-call | tf_op jit(solution)/shard_map/pallas_call | solution.py:200
  (30 shorter events, 1.2 us)
Async XLA Ops:
  18.3 11.5 %copy-start.4 = (s32[32]{0:T(128)S(1)}, s32[32]{0:T(128)}, u32[]{:S(2)}) copy-start(s32[32]{0:T(128)} %refs_0_.1) | copy-start | bytes 388
  18.3 41.6 %all-to-all-start = ((bf16[128,2,16,256]{3,2,1,0:T(8,128)(2,1)}), bf16[128,2,16,256]{3,2,1,0:T(8,128)(2,1)S(1)}, u32[]{:S(2)}, u32[]{:S(2)}) async-start(bf16[128,2,16,256]{3,2,1,0:T(8,128)(2,1)} %bitcast.24), calls=%async_computation | async-start | bytes 4194304 | tf_op jit(solution)/shard_map/all_to_all | solution.py:364
  31.7 31.3 %copy-start.3 = (s32[512,256]{1,0:T(8,128)}, s32[512,256]{1,0:T(8,128)S(1)}, u32[]{:S(2)}) copy-start(s32[512,256]{1,0:T(8,128)S(1)} %convert_reduce_fusion.1.refs_4_) | copy-start | bytes 1572868
  59.9 1.3 %copy-start.2 = (bf16[128,2,16,256]{3,2,1,0:T(8,128)(2,1)}, bf16[128,2,16,256]{3,2,1,0:T(8,128)(2,1)S(1)}, u32[]{:S(2)}) copy-start(bf16[128,2,16,256]{3,2,1,0:T(8,128)(2,1)S(1)} %all-to-all-done) | copy-start | bytes 6291460
  63.0 8.0 %copy-start = (bf16[4,2,32,16,256]{4,3,2,1,0:T(8,128)(2,1)}, bf16[4,2,32,16,256]{4,3,2,1,0:T(8,128)(2,1)S(1)}, u32[]{:S(2)}) copy-start(bf16[4,2,32,16,256]{4,3,2,1,0:T(8,128)(2,1)S(1)} %copy.44) | copy-start | bytes 6291460
  65.3 2.4 %copy-start.1 = (bf16[8,131072]{1,0:T(8,128)(2,1)S(1)}, bf16[8,131072]{1,0:T(8,128)(2,1)}, u32[]{:S(2)}) copy-start(bf16[8,131072]{1,0:T(8,128)(2,1)} %reshape_reshape.3) | copy-start | bytes 6291460
  74.0 7.1 %collective-permute-start = (bf16[8,512,1]{1,0,2:T(8,128)(2,1)S(1)}, bf16[8,512,1]{1,0,2:T(8,128)(2,1)S(1)}, u32[]{:S(2)}, u32[]{:S(2)}) collective-permute-start(bf16[8,512,1]{1,0,2:T(8,128)(2,1)S(1)} %copy.47), channel_id=1, source_target_pairs={{0,1},{1,2},{2,3},{4,5},{5,6},{6,7},{8,9},{9,10},{10,11},{12,13},{... | collective-permute-start | bytes 24584 | tf_op jit(solution)/shard_map/ppermute | solution.py:381
  78.3 6.5 %collective-permute-start.1 = (bf16[8,512,1]{1,0,2:T(8,128)(2,1)S(1)}, bf16[8,512,1]{1,0,2:T(8,128)(2,1)S(1)}, u32[]{:S(2)}, u32[]{:S(2)}) collective-permute-start(bf16[8,512,1]{1,0,2:T(8,128)(2,1)S(1)} %copy.48), channel_id=1, source_target_pairs={{1,0},{2,1},{3,2},{5,4},{6,5},{7,6},{9,8},{10,9},{11,10},{13,12},{... | collective-permute-start | bytes 24584 | tf_op jit(solution)/shard_map/ppermute | solution.py:382

commit v9 on v5

--- a/solution.py
+++ b/solution.py
@@ -216,67 +216,100 @@
     return jnp.sum(hit, axis=(0, 1, 2)).astype(jnp.float32)
 
 
-def gather_sum_kernel(n_calib, n_peak, x_ref, o_ref, buf, send_sem, recv_sem):
-    total = n_calib * n_peak
-    me = lax.axis_index("calib") * n_peak + lax.axis_index("peak")
-    buf[total - 1] = x_ref[...]
+def gather_sum_kernel(stages, x_ref, o_ref, *scratch):
+    count = len(stages)
+    bufs = scratch[:count]
+    partials = scratch[count : 2 * count]
+    sems = scratch[2 * count :]
+    me = (lax.axis_index("calib"), lax.axis_index("peak"))
+
+    def peer(stage, step):
+        axis, size, stride = stages[stage]
+        pos = (me[axis] // stride) % size
+        target = me[axis] + (lax.rem(pos + step, size) - pos) * stride
+        return (target, me[1]) if axis == 0 else (me[0], target)
+
+    def position(stage):
+        axis, size, stride = stages[stage]
+        return (me[axis] // stride) % size
+
     barrier = pltpu.get_barrier_semaphore()
-
-    def peer_of(step):
-        peer = lax.rem(me + step, total)
-        return (peer // n_peak, peer % n_peak)
-
-    def greet(step, carry):
-        pl.semaphore_signal(
-            barrier, inc=1, device_id=peer_of(step), device_id_type=pl.DeviceIdType.MESH
-        )
-        return carry
-
-    lax.fori_loop(1, total, greet, 0)
-    pl.semaphore_wait(barrier, total - 1)
-
-    def send(step, carry):
-        pltpu.make_async_remote_copy(
-            src_ref=x_ref,
-            dst_ref=buf.at[total - 1 - step],
+    peers = 0
+    for stage, (axis, size, stride) in enumerate(stages):
+        peers += size - 1
+
+        def greet(step, carry, stage=stage):
+            pl.semaphore_signal(
+                barrier, inc=1, device_id=peer(stage, step), device_id_type=pl.DeviceIdType.MESH
+            )
+            return carry
+
+        lax.fori_loop(1, size, greet, 0)
+    pl.semaphore_wait(barrier, peers)
+
+    source = x_ref
+    for stage, (axis, size, stride) in enumerate(stages):
+        buf = bufs[stage]
+        send_sem = sems[2 * stage]
+        recv_sem = sems[2 * stage + 1]
+        buf[size - 1] = source[...]
+
+        def send(step, carry, stage=stage, buf=buf, send_sem=send_sem, recv_sem=recv_sem, source=source, size=size):
+            pltpu.make_async_remote_copy(
+                src_ref=source,
+                dst_ref=buf.at[size - 1 - step],
+                send_sem=send_sem,
+                recv_sem=recv_sem,
+                device_id=peer(stage, step),
+                device_id_type=pl.DeviceIdType.MESH,
+            ).start()
+            return carry
+
+        lax.fori_loop(1, size, send, 0)
+        every = pltpu.make_async_remote_copy(
+            src_ref=buf.at[pl.ds(0, size - 1)],
+            dst_ref=buf.at[pl.ds(0, size - 1)],
             send_sem=send_sem,
             recv_sem=recv_sem,
-            device_id=peer_of(step),
+            device_id=peer(stage, 1),
             device_id_type=pl.DeviceIdType.MESH,
-        ).start()
-        return carry
-
-    lax.fori_loop(1, total, send, 0)
-    every = pltpu.make_async_remote_copy(
-        src_ref=buf.at[pl.ds(0, total - 1)],
-        dst_ref=buf.at[pl.ds(0, total - 1)],
-        send_sem=send_sem,
-        recv_sem=recv_sem,
-        device_id=peer_of(1),
-        device_id_type=pl.DeviceIdType.MESH,
-    )
-    every.wait_send()
-    every.wait_recv()
-
-    def add(source, acc):
-        return acc + buf[lax.rem(source - me - 1 + 2 * total, total)]
-
-    o_ref[...] = lax.fori_loop(0, total, add, jnp.zeros(x_ref.shape, x_ref.dtype))
+        )
+        every.wait_send()
+        every.wait_recv()
+        pos = position(stage)
+
+        def add(origin, acc, buf=buf, pos=pos, size=size):
+            return acc + buf[lax.rem(origin - pos - 1 + 2 * size, size)]
+
+        total = lax.fori_loop(0, size, add, jnp.zeros(x_ref.shape, x_ref.dtype))
+        if stage == count - 1:
+            o_ref[...] = total
+        else:
+            partials[stage][...] = total
+            source = partials[stage]
 
 
 def gather_sum(x):
     n_calib = lax.axis_size("calib")
     n_peak = lax.axis_size("peak")
+    stages = [(1, n_peak, 1)]
+    stride = 1
+    for size in (4, 4, 2):
+        if n_calib % (stride * size) == 0 and stride * size <= n_calib:
+            stages.append((0, size, stride))
+            stride *= size
+    if stride < n_calib:
+        stages.append((0, n_calib // stride, stride))
+    count = len(stages)
+    scratch = [pltpu.VMEM((size,) + x.shape, x.dtype) for _, size, _ in stages]
+    scratch += [pltpu.VMEM(x.shape, x.dtype) for _ in range(count)]
+    scratch += [pltpu.SemaphoreType.DMA] * (2 * count)
     return pl.pallas_call(
-        lambda *refs: gather_sum_kernel(n_calib, n_peak, *refs),
+        lambda *refs: gather_sum_kernel(stages, *refs),
         out_shape=jax.ShapeDtypeStruct(x.shape, x.dtype),
         in_specs=[pl.BlockSpec(memory_space=pltpu.VMEM)],
         out_specs=pl.BlockSpec(memory_space=pltpu.VMEM),
-        scratch_shapes=[
-            pltpu.VMEM((n_calib * n_peak,) + x.shape, x.dtype),
-            pltpu.SemaphoreType.DMA,
-            pltpu.SemaphoreType.DMA,
-        ],
+        scratch_shapes=scratch,
         compiler_params=pltpu.CompilerParams(collective_id=0, has_side_effects=True),
     )(x)
 

time: 123 us -> 121 us (0.984)
  Pallas kernels: 47.1 us -> 42.9 us
  starting transfers between devices: 18.6 us -> 20 us
    pallas_call x1, Pallas kernels: 17.5 us -> 13.3 us  [gather_sum(): pl.pallas_call(lambda *refs: gather_sum_kernel(stages, *refs), out_shape=...]
    ppermute x1, starting transfers between devices: 2.36 us -> 4.62 us  [body(): right = lax.ppermute(edge_score[:, :, 1:], 'peak', bwd)]
where the time goes in v9:
time: 121 us; the launch traced here: 120 us
  Pallas kernels  42.9 us (35%)
  waiting for transfers between devices  20.9 us (17%)
  local copies, waits for them, and re-layouts  20.5 us (17%)
  starting transfers between devices  20 us (17%)
  other arithmetic  11.1 us (9%)
  matrix products  3.42 us (3%)
    all_to_all x1, waiting for transfers between devices, body(): got = lax.all_to_all(send, ('calib', 'peak'), 0, 0, tiled=True)  20.9 us
    pallas_call x1, Pallas kernels, calibrate_send(): pl.pallas_call(lambda *refs: calibrate_kernel(group, *refs), grid_spec=gr...  16.2 us
    pallas_call x1, Pallas kernels, score_outputs(): pl.pallas_call(lambda *refs: score_kernel(n_peak, levels, *refs), grid_sp...  13.4 us
    pallas_call x1, Pallas kernels, gather_sum(): pl.pallas_call(lambda *refs: gather_sum_kernel(stages, *refs), out_shape=...  13.3 us
    all_to_all x1, starting transfers between devices, body(): got = lax.all_to_all(send, ('calib', 'peak'), 0, 0, tiled=True)  11.5 us
    ppermute x1, starting transfers between devices, body(): right = lax.ppermute(edge_score[:, :, 1:], 'peak', bwd)  4.62 us
    ppermute x1, starting transfers between devices, body(): left = lax.ppermute(edge_score[:, :, :1], 'peak', fwd)  3.83 us
    slice x2, local copies, waits for them, and re-layouts, body(): frame[:, :, width_here - 1]  3.42 us
  transfers between devices with their start and end apart: 3, of which 1 were waited for; matrix products, arithmetic and copies ran while one was open for 10% of the time, Pallas kernels for 0%

profile of v9, /device:TPU:1, one launch (start us, length us, event | category | flops | bytes accessed | tf_op | source)
XLA Modules:
  0.0 119.8 jit_solution(5635084115786363202)
XLA Ops:
  0.6 0.8 copy.58
  1.4 0.7 reshape.185.refs_1_
  2.1 16.2 %shard_map.77 = bf16[32,4,2,16,256]{4,3,2,1,0:T(8,128)(2,1)} custom-call(s32[32]{0:T(128)} %refs_0_.1, s32[224]{0:T(256)} %reshape.185.refs_1_, s32[2,32,16,1024]{3,2,1,0:T(8,128)} %refs_2_.1, f32[3,32,16,1024]{3,2,1,0:T(8,128)} %refs_3_.1, bf16[3,32,16,1024]{3,2,1,0:T(8,128)(2,1)} %refs_4_.1, s32[32,16,1024]{2,1,0:T(8,128)} %refs_5_.1), custom_call_target="tpu_custom_call" | custom-call | tf_op jit(solution)/shard_map/pallas_call | solution.py:131
  18.3 11.5 %all-to-all-start = ((bf16[128,2,16,256]{3,2,1,0:T(8,128)(2,1)}), bf16[128,2,16,256]{3,2,1,0:T(8,128)(2,1)S(1)}, u32[]{:S(2)}, u32[]{:S(2)}) async-start(bf16[128,2,16,256]{3,2,1,0:T(8,128)(2,1)} %bitcast.30), calls=%async_computation | async-start | bytes 4194304 | tf_op jit(solution)/shard_map/all_to_all | solution.py:335
  30.1 1.6 %convert_reduce_fusion.1.refs_4_ = s32[512,256]{1,0:T(8,128)S(1)} fusion(s32[512,256]{1,0:T(8,128)S(1)} %broadcast_add_fusion.1, s32[31]{0:T(128)S(1)} %multiply_multiply_fusion), kind=kLoop, calls=%fused_computation.5 | loop fusion | flops 12058624 | bytes 1048700 | tf_op jit(solution)/shard_map/reduce_sum | solution.py:34
  31.9 1.1 copy.73
  33.5 1.1 constant_dynamic-slice_fusion
  34.8 1.7 %convert_reduce_fusion = s32[32,16,256]{2,1,0:T(8,128)S(1)} fusion(s32[32,16,256]{2,1,0:T(8,128)S(1)} %broadcast_add_fusion, s32[31]{0:T(128)S(1)} %multiply_multiply_fusion), kind=kLoop, calls=%fused_computation.4 | loop fusion | flops 12058624 | bytes 1048700 | tf_op jit(solution)/shard_map/reduce_sum | solution.py:34
  36.5 2.5 %select_reduce_fusion = s32[32]{0:T(128)S(1)} fusion(s32[32,16,256]{2,1,0:T(8,128)S(1)} %constant_dynamic-slice_fusion, s32[32,16,256]{2,1,0:T(8,128)S(1)} %convert_reduce_fusion), kind=kLoop, calls=%fused_computation | loop fusion | flops 12582880 | bytes 1048704 | tf_op jit(solution)/shard_map/reduce_sum | solution.py:216
  39.0 20.9 %all-to-all-done = bf16[128,2,16,256]{3,2,1,0:T(8,128)(2,1)S(1)} async-done(((bf16[128,2,16,256]{3,2,1,0:T(8,128)(2,1)}), bf16[128,2,16,256]{3,2,1,0:T(8,128)(2,1)S(1)}, u32[]{:S(2)}, u32[]{:S(2)}) %all-to-all-start) | async-done | bytes 2097184 | tf_op jit(solution)/shard_map/all_to_all | solution.py:335
  59.9 1.3 %copy-done.3 = bf16[128,2,16,256]{3,2,1,0:T(8,128)(2,1)} copy-done((bf16[128,2,16,256]{3,2,1,0:T(8,128)(2,1)}, bf16[128,2,16,256]{3,2,1,0:T(8,128)(2,1)S(1)}, u32[]{:S(2)}) %copy-start.3) | copy-done | bytes 2097176
  61.2 1.8 %copy.59 = bf16[4,2,32,16,256]{4,3,2,1,0:T(8,128)(2,1)S(1)} copy(bf16[4,2,32,16,256]{4,3,1,0,2:T(8,128)(2,1)} %bitcast.29) | data formatting | bytes 4194304 | tf_op jit(solution)/shard_map/transpose | solution.py:337
  63.0 2.3 %reshape_reshape.3 = bf16[8,131072]{1,0:T(8,128)(2,1)} reshape(bf16[4,2,32,16,256]{4,3,2,1,0:T(8,128)(2,1)S(1)} %copy.59) | data formatting | bytes 4194304 | tf_op jit(solution)/shard_map/reshape;reshape | solution.py:347
  65.3 1.8 %fusion.19 = (bf16[8,512,1]{2,1,0:T(8,128)(2,1)}, bf16[8,512,1]{2,1,0:T(8,128)(2,1)}) fusion(bf16[8,512,256]{2,1,0:T(8,128)(2,1)S(1)} %bitcast.26), kind=kLoop, calls=%fused_computation.54 | loop fusion | bytes 32768 | tf_op jit(solution)/shard_map/slice | solution.py:373
  67.1 1.6 %copy.62 = bf16[8,512,1]{1,0,2:T(8,128)(2,1)S(1)} copy(bf16[8,512,1]{2,1,0:T(8,128)(2,1)} %get-tuple-element.30) | data formatting | bytes 16384 | tf_op jit(solution)/shard_map/slice | solution.py:373
  68.7 1.7 %copy.63 = bf16[8,512,1]{1,0,2:T(8,128)(2,1)S(1)} copy(bf16[8,512,1]{2,1,0:T(8,128)(2,1)} %get-tuple-element.31) | data formatting | bytes 16384 | tf_op jit(solution)/shard_map/slice | solution.py:373
  70.5 0.2 copy.65
  70.7 2.3 %reduce-precision_convert_fusion = (bf16[8,131072]{1,0:T(8,128)(2,1)S(1)}, bf16[8,131072]{1,0:T(8,128)(2,1)S(1)}) fusion(bf16[8,131072]{1,0:T(8,128)(2,1)} %reshape_reshape.3), kind=kLoop, calls=%fused_computation.13 | loop fusion | flops 6291456 | bytes 6291456 | tf_op jit(solution)/shard_map/convert_element_type | solution.py:351
  73.1 3.2 %fusion = f32[24,32]{1,0:T(8,128)S(1)} fusion(s32[131072]{0:T(1024)S(1)} %bitcast.35, bf16[8,131072]{1,0:T(8,128)(2,1)S(1)} %get-tuple-element.33, bf16[8,131072]{1,0:T(8,128)(2,1)S(1)} %get-tuple-element.32, bf16[8,131072]{1,0:T(8,128)(2,1)S(1)} %copy-done.2), kind=kOutput, calls=%fused_computation.3 | convolution fusion | flops 224395264 | bytes 6818816 | tf_op jit(solution)/shard_map/fp,kp->fk/dot_general | solution.py:354
  76.3 0.7 fusion.13.refs_0_
  77.0 13.3 %shard_map.78 = f32[8,128]{1,0:T(8,128)} custom-call(f32[8,128]{1,0:T(8,128)} %fusion.13.refs_0_), custom_call_target="tpu_custom_call" | custom-call | tf_op jit(solution)/shard_map/pallas_call | solution.py:307
  90.4 0.7 slice_bitcast_fusion
  91.1 0.8 add_sqrt_fusion
  92.1 0.2 copy.64
  92.3 0.2 copy.66
  92.6 0.4 fusion.20
  93.1 4.6 %collective-permute-start.1 = (f32[8,512,1]{1,0,2:T(8,128)S(1)}, f32[8,512,1]{1,0,2:T(8,128)S(1)}, u32[]{:S(2)}, u32[]{:S(2)}) collective-permute-start(f32[8,512,1]{1,0,2:T(8,128)S(1)} %copy.68), channel_id=1, source_target_pairs={{1,0},{2,1},{3,2},{5,4},{6,5},{7,6},{9,8},{10,9},{11,10},{13,12},{... | collective-permute-start | bytes 49160 | tf_op jit(solution)/shard_map/ppermute | solution.py:387
  97.8 3.8 %collective-permute-start = (f32[8,512,1]{1,0,2:T(8,128)S(1)}, f32[8,512,1]{1,0,2:T(8,128)S(1)}, u32[]{:S(2)}, u32[]{:S(2)}) collective-permute-start(f32[8,512,1]{1,0,2:T(8,128)S(1)} %copy.67), channel_id=1, source_target_pairs={{0,1},{1,2},{2,3},{4,5},{5,6},{6,7},{8,9},{9,10},{10,11},{12,13},{... | collective-permute-start | bytes 49160 | tf_op jit(solution)/shard_map/ppermute | solution.py:386
  101.7 0.8 reduce_min.9
  102.5 2.0 %copy.70.refs_6_ = f32[8,512,1]{2,1,0:T(8,128)} copy(f32[8,512,1]{1,0,2:T(8,128)S(1)} %collective-permute-done.1) | data formatting | bytes 32768 | tf_op jit(solution)/shard_map/ppermute | solution.py:387
  104.5 2.0 %copy.69.refs_5_ = f32[8,512,1]{2,1,0:T(8,128)} copy(f32[8,512,1]{1,0,2:T(8,128)S(1)} %collective-permute-done) | data formatting | bytes 32768 | tf_op jit(solution)/shard_map/ppermute | solution.py:386
  106.4 13.4 %shard_map.79 = (bf16[8,512,256]{2,1,0:T(8,128)(2,1)}, bf16[8,512,256]{2,1,0:T(8,128)(2,1)}) custom-call(s32[1]{0:T(128)} %bitcast.refs_0_, f32[8,32]{1,0:T(8,128)} %copy-done.6, f32[8,32]{1,0:T(8,128)} %copy-done.5, bf16[8,512,256]{2,1,0:T(8,128)(2,1)} %bitcast.27, s32[512,256]{1,0:T(8,128)} %copy-done.1, f32[8,512,1]{2,1,0:T(8,128)} %copy.69.refs_5_, ...), custom_call_target="tpu_custom_call" | custom-call | tf_op jit(solution)/shard_map/pallas_call | solution.py:184
  (40 shorter events, 1.5 us)
Async XLA Ops:
  18.3 11.5 %copy-start.7 = (s32[32]{0:T(128)S(1)}, s32[32]{0:T(128)}, u32[]{:S(2)}) copy-start(s32[32]{0:T(128)} %refs_0_.1) | copy-start | bytes 388
  18.3 41.6 %all-to-all-start = ((bf16[128,2,16,256]{3,2,1,0:T(8,128)(2,1)}), bf16[128,2,16,256]{3,2,1,0:T(8,128)(2,1)S(1)}, u32[]{:S(2)}, u32[]{:S(2)}) async-start(bf16[128,2,16,256]{3,2,1,0:T(8,128)(2,1)} %bitcast.30), calls=%async_computation | async-start | bytes 4194304 | tf_op jit(solution)/shard_map/all_to_all | solution.py:335
  31.7 70.0 %copy-start.1 = (s32[512,256]{1,0:T(8,128)}, s32[512,256]{1,0:T(8,128)S(1)}, u32[]{:S(2)}) copy-start(s32[512,256]{1,0:T(8,128)S(1)} %convert_reduce_fusion.1.refs_4_) | copy-start | bytes 1572868
  59.9 1.3 %copy-start.3 = (bf16[128,2,16,256]{3,2,1,0:T(8,128)(2,1)}, bf16[128,2,16,256]{3,2,1,0:T(8,128)(2,1)S(1)}, u32[]{:S(2)}) copy-start(bf16[128,2,16,256]{3,2,1,0:T(8,128)(2,1)S(1)} %all-to-all-done) | copy-start | bytes 6291460
  63.0 4.1 %copy-start = (bf16[4,2,32,16,256]{4,3,2,1,0:T(8,128)(2,1)}, bf16[4,2,32,16,256]{4,3,2,1,0:T(8,128)(2,1)S(1)}, u32[]{:S(2)}) copy-start(bf16[4,2,32,16,256]{4,3,2,1,0:T(8,128)(2,1)S(1)} %copy.59) | copy-start | bytes 6291460
  68.7 4.4 %copy-start.2 = (bf16[8,131072]{1,0:T(8,128)(2,1)S(1)}, bf16[8,131072]{1,0:T(8,128)(2,1)}, u32[]{:S(2)}) copy-start(bf16[8,131072]{1,0:T(8,128)(2,1)} %reshape_reshape.3) | copy-start | bytes 6291460
  70.7 2.4 %copy-start.4 = (s32[64,2,8,128]{3,1,2,0:T(2,128)S(1)}, s32[64,2,8,128]{3,1,2,0:T(2,128)}, u32[]{:S(2)}) copy-start(s32[64,2,8,128]{3,1,2,0:T(2,128)} %copy.73) | copy-start | bytes 1572868
  91.9 14.5 %copy-start.5 = (f32[8,32]{1,0:T(8,128)}, f32[8,32]{1,0:T(8,128)S(1)}, u32[]{:S(2)}) copy-start(f32[8,32]{1,0:T(8,128)S(1)} %get-tuple-element.42.refs_2_) | copy-start | bytes 3076
  91.9 14.5 %copy-start.6 = (f32[8,32]{1,0:T(8,128)}, f32[8,32]{1,0:T(8,128)S(1)}, u32[]{:S(2)}) copy-start(f32[8,32]{1,0:T(8,128)S(1)} %get-tuple-element.43.refs_1_) | copy-start | bytes 3076
  93.1 9.4 %collective-permute-start.1 = (f32[8,512,1]{1,0,2:T(8,128)S(1)}, f32[8,512,1]{1,0,2:T(8,128)S(1)}, u32[]{:S(2)}, u32[]{:S(2)}) collective-permute-start(f32[8,512,1]{1,0,2:T(8,128)S(1)} %copy.68), channel_id=1, source_target_pairs={{1,0},{2,1},{3,2},{5,4},{6,5},{7,6},{9,8},{10,9},{11,10},{13,12},{... | collective-permute-start | bytes 49160 | tf_op jit(solution)/shard_map/ppermute | solution.py:387
  97.8 6.6 %collective-permute-start = (f32[8,512,1]{1,0,2:T(8,128)S(1)}, f32[8,512,1]{1,0,2:T(8,128)S(1)}, u32[]{:S(2)}, u32[]{:S(2)}) collective-permute-start(f32[8,512,1]{1,0,2:T(8,128)S(1)} %copy.67), channel_id=1, source_target_pairs={{0,1},{1,2},{2,3},{4,5},{5,6},{6,7},{8,9},{9,10},{10,11},{12,13},{... | collective-permute-start | bytes 49160 | tf_op jit(solution)/shard_map/ppermute | solution.py:386

commit v10 on v6

--- a/solution.py
+++ b/solution.py
@@ -135,54 +135,62 @@
     )(table, bounds.reshape(-1), raw, pedestal, gain, good)
 
 
-def score_kernel(n_peak, levels, low_ref, mean_ref, rms_ref, frame_ref, cycle_ref, left_ref, right_ref, snr_ref, bent_ref):
-    frame_pos = pl.program_id(0)
+def score_kernel(n_peak, levels, per, low_ref, mean_ref, rms_ref, frame_ref, cycle_ref, left_ref, right_ref, snr_ref, bent_ref):
     cycle = cycle_ref[...]
-    values = frame_ref[...].astype(jnp.float32)
-    rows, cols = values.shape
+    rows, cols = cycle.shape
     tops = mean_ref.shape[1] - 1
-    pixel_mean = jnp.zeros((rows, cols), jnp.float32)
-    pixel_rms = jnp.ones((rows, cols), jnp.float32)
-    for j in range(levels):
-        level = jnp.minimum(low_ref[0] + j, tops)
-        hit = cycle == level
-        pixel_mean = jnp.where(hit, mean_ref[frame_pos, level], pixel_mean)
-        pixel_rms = jnp.where(hit, rms_ref[frame_pos, level], pixel_rms)
-    score = (values - pixel_mean) / pixel_rms
     peak_pos = lax.axis_index("peak")
     row_ids = lax.broadcasted_iota(jnp.int32, (rows, cols), 0)
     col_ids = lax.broadcasted_iota(jnp.int32, (rows, cols), 1)
-    left_col = jnp.where(peak_pos == 0, 0.0, left_ref[...])
-    right_col = jnp.where(peak_pos == n_peak - 1, 0.0, right_ref[...])
-    total = 4.0 * score
+    row_shifts = []
     for shift in (1, rows - 1):
-        moved = pltpu.roll(score, shift, 0)
         source = pltpu.roll(row_ids, shift, 0)
-        total = total - jnp.where(jnp.abs(source - row_ids) == 1, moved, 0.0)
+        row_shifts.append((shift, jnp.abs(source - row_ids) == 1))
+    col_shifts = []
     for shift in (1, cols - 1):
-        moved = pltpu.roll(score, shift, 1)
         source = pltpu.roll(col_ids, shift, 1)
-        near = jnp.where(source == cols - 1, left_col, right_col)
-        total = total - jnp.where(jnp.abs(source - col_ids) == 1, moved, near)
-    snr_ref[...] = score.astype(snr_ref.dtype)
-    bent_ref[...] = total.astype(bent_ref.dtype)
+        col_shifts.append((shift, jnp.abs(source - col_ids) == 1, source == cols - 1))
+    hits = []
+    for j in range(levels):
+        level = jnp.minimum(low_ref[0] + j, tops)
+        hits.append((level, cycle == level))
+    for inner in range(per):
+        frame_pos = pl.program_id(0) * per + inner
+        values = frame_ref[inner].astype(jnp.float32)
+        pixel_mean = jnp.zeros((rows, cols), jnp.float32)
+        pixel_rms = jnp.ones((rows, cols), jnp.float32)
+        for level, hit in hits:
+            pixel_mean = jnp.where(hit, mean_ref[frame_pos, level], pixel_mean)
+            pixel_rms = jnp.where(hit, rms_ref[frame_pos, level], pixel_rms)
+        score = (values - pixel_mean) / pixel_rms
+        left_col = jnp.where(peak_pos == 0, 0.0, left_ref[inner])
+        right_col = jnp.where(peak_pos == n_peak - 1, 0.0, right_ref[inner])
+        total = 4.0 * score
+        for shift, inside in row_shifts:
+            total = total - jnp.where(inside, pltpu.roll(score, shift, 0), 0.0)
+        for shift, inside, wrapped_left in col_shifts:
+            near = jnp.where(wrapped_left, left_col, right_col)
+            total = total - jnp.where(inside, pltpu.roll(score, shift, 1), near)
+        snr_ref[inner] = score.astype(snr_ref.dtype)
+        bent_ref[inner] = total.astype(bent_ref.dtype)
 
 
 def score_outputs(frame, cycle, cycle_average, cycle_rms, left, right, n_peak):
     frames, rows, cols = frame.shape
     span = (rows * rows + cols * cols) ** 0.5
-    levels = min(CYCLES, int(span // CYCLE_W) + 3)
+    levels = min(CYCLES, int(span // CYCLE_W) + 2)
+    per = 2 if frames % 2 == 0 else 1
     low = jnp.min(cycle).reshape(1)
-    block = pl.BlockSpec((None, rows, cols), lambda f, *_: (f, 0, 0))
-    edge = pl.BlockSpec((None, rows, 1), lambda f, *_: (f, 0, 0))
+    block = pl.BlockSpec((per, rows, cols), lambda f, *_: (f, 0, 0))
+    edge = pl.BlockSpec((per, rows, 1), lambda f, *_: (f, 0, 0))
     grid_spec = pltpu.PrefetchScalarGridSpec(
         num_scalar_prefetch=3,
-        grid=(frames,),
+        grid=(frames // per,),
         in_specs=[block, pl.BlockSpec((rows, cols), lambda f, *_: (0, 0)), edge, edge],
         out_specs=[block, block],
     )
     return pl.pallas_call(
-        lambda *refs: score_kernel(n_peak, levels, *refs),
+        lambda *refs: score_kernel(n_peak, levels, per, *refs),
         grid_spec=grid_spec,
         out_shape=[jax.ShapeDtypeStruct(frame.shape, jnp.bfloat16)] * 2,
     )(low, cycle_average, cycle_rms, frame, cycle, left, right)

time: 118 us -> 118 us (level)
  no operation moved by 1% of the time
where the time goes in v10:
time: 118 us; the launch traced here: 117 us
  Pallas kernels  41.4 us (35%)
  waiting for transfers between devices  20.9 us (18%)
  local copies, waits for them, and re-layouts  20.5 us (17%)
  starting transfers between devices  18.8 us (16%)
  other arithmetic  11.1 us (9%)
  matrix products  3.42 us (3%)
    all_to_all x1, waiting for transfers between devices, body(): got = lax.all_to_all(send, ('calib', 'peak'), 0, 0, tiled=True)  20.9 us
    pallas_call x1, Pallas kernels, calibrate_send(): pl.pallas_call(lambda *refs: calibrate_kernel(group, *refs), grid_spec=gr...  16.2 us
    pallas_call x1, Pallas kernels, score_outputs(): pl.pallas_call(lambda *refs: score_kernel(n_peak, levels, per, *refs), gr...  12.7 us
    pallas_call x1, Pallas kernels, gather_sum(): pl.pallas_call(lambda *refs: gather_sum_kernel(n_calib, n_peak, *refs), o...  12.4 us
    all_to_all x1, starting transfers between devices, body(): got = lax.all_to_all(send, ('calib', 'peak'), 0, 0, tiled=True)  11.5 us
    ppermute x1, starting transfers between devices, body(): left = lax.ppermute(edge_score[:, :, :1], 'peak', fwd)  4 us
    slice x2, local copies, waits for them, and re-layouts, body(): frame[:, :, width_here - 1]  3.42 us
    reduce_sum x2, other arithmetic, cycle_index(): return jnp.sum((dist[..., None] >= lows).astype(jnp.int32), axis=-1)  3.34 us
  transfers between devices with their start and end apart: 3, of which 1 were waited for; matrix products, arithmetic and copies ran while one was open for 10% of the time, Pallas kernels for 0%

profile of v10, /device:TPU:1, one launch (start us, length us, event | category | flops | bytes accessed | tf_op | source)
XLA Modules:
  0.0 117.1 jit_solution(9299709081732651216)
XLA Ops:
  0.6 0.8 copy.58
  1.4 0.7 reshape.185.refs_1_
  2.1 16.2 %shard_map.77 = bf16[32,4,2,16,256]{4,3,2,1,0:T(8,128)(2,1)} custom-call(s32[32]{0:T(128)} %refs_0_.1, s32[224]{0:T(256)} %reshape.185.refs_1_, s32[2,32,16,1024]{3,2,1,0:T(8,128)} %refs_2_.1, f32[3,32,16,1024]{3,2,1,0:T(8,128)} %refs_3_.1, bf16[3,32,16,1024]{3,2,1,0:T(8,128)(2,1)} %refs_4_.1, s32[32,16,1024]{2,1,0:T(8,128)} %refs_5_.1), custom_call_target="tpu_custom_call" | custom-call | tf_op jit(solution)/shard_map/pallas_call | solution.py:131
  18.3 11.5 %all-to-all-start = ((bf16[128,2,16,256]{3,2,1,0:T(8,128)(2,1)}), bf16[128,2,16,256]{3,2,1,0:T(8,128)(2,1)S(1)}, u32[]{:S(2)}, u32[]{:S(2)}) async-start(bf16[128,2,16,256]{3,2,1,0:T(8,128)(2,1)} %bitcast.30), calls=%async_computation | async-start | bytes 4194304 | tf_op jit(solution)/shard_map/all_to_all | solution.py:354
  30.1 1.6 %convert_reduce_fusion.1.refs_4_ = s32[512,256]{1,0:T(8,128)S(1)} fusion(s32[512,256]{1,0:T(8,128)S(1)} %broadcast_add_fusion.1, s32[31]{0:T(128)S(1)} %multiply_multiply_fusion), kind=kLoop, calls=%fused_computation.5 | loop fusion | flops 12058624 | bytes 1048700 | tf_op jit(solution)/shard_map/reduce_sum | solution.py:34
  31.9 1.1 copy.73
  33.5 1.1 constant_dynamic-slice_fusion
  34.8 1.7 %convert_reduce_fusion = s32[32,16,256]{2,1,0:T(8,128)S(1)} fusion(s32[32,16,256]{2,1,0:T(8,128)S(1)} %broadcast_add_fusion, s32[31]{0:T(128)S(1)} %multiply_multiply_fusion), kind=kLoop, calls=%fused_computation.4 | loop fusion | flops 12058624 | bytes 1048700 | tf_op jit(solution)/shard_map/reduce_sum | solution.py:34
  36.5 2.5 %select_reduce_fusion = s32[32]{0:T(128)S(1)} fusion(s32[32,16,256]{2,1,0:T(8,128)S(1)} %constant_dynamic-slice_fusion, s32[32,16,256]{2,1,0:T(8,128)S(1)} %convert_reduce_fusion), kind=kLoop, calls=%fused_computation | loop fusion | flops 12582880 | bytes 1048704 | tf_op jit(solution)/shard_map/reduce_sum | solution.py:224
  39.0 20.9 %all-to-all-done = bf16[128,2,16,256]{3,2,1,0:T(8,128)(2,1)S(1)} async-done(((bf16[128,2,16,256]{3,2,1,0:T(8,128)(2,1)}), bf16[128,2,16,256]{3,2,1,0:T(8,128)(2,1)S(1)}, u32[]{:S(2)}, u32[]{:S(2)}) %all-to-all-start) | async-done | bytes 2097184 | tf_op jit(solution)/shard_map/all_to_all | solution.py:354
  59.9 1.3 %copy-done.3 = bf16[128,2,16,256]{3,2,1,0:T(8,128)(2,1)} copy-done((bf16[128,2,16,256]{3,2,1,0:T(8,128)(2,1)}, bf16[128,2,16,256]{3,2,1,0:T(8,128)(2,1)S(1)}, u32[]{:S(2)}) %copy-start.3) | copy-done | bytes 2097176
  61.2 1.8 %copy.59 = bf16[4,2,32,16,256]{4,3,2,1,0:T(8,128)(2,1)S(1)} copy(bf16[4,2,32,16,256]{4,3,1,0,2:T(8,128)(2,1)} %bitcast.29) | data formatting | bytes 4194304 | tf_op jit(solution)/shard_map/transpose | solution.py:356
  63.0 2.3 %reshape_reshape.3 = bf16[8,131072]{1,0:T(8,128)(2,1)} reshape(bf16[4,2,32,16,256]{4,3,2,1,0:T(8,128)(2,1)S(1)} %copy.59) | data formatting | bytes 4194304 | tf_op jit(solution)/shard_map/reshape;reshape | solution.py:366
  65.3 1.8 %fusion.19 = (bf16[8,512,1]{2,1,0:T(8,128)(2,1)}, bf16[8,512,1]{2,1,0:T(8,128)(2,1)}) fusion(bf16[8,512,256]{2,1,0:T(8,128)(2,1)S(1)} %bitcast.26), kind=kLoop, calls=%fused_computation.54 | loop fusion | bytes 32768 | tf_op jit(solution)/shard_map/slice | solution.py:392
  67.1 1.6 %copy.62 = bf16[8,512,1]{1,0,2:T(8,128)(2,1)S(1)} copy(bf16[8,512,1]{2,1,0:T(8,128)(2,1)} %get-tuple-element.30) | data formatting | bytes 16384 | tf_op jit(solution)/shard_map/slice | solution.py:392
  68.7 1.7 %copy.63 = bf16[8,512,1]{1,0,2:T(8,128)(2,1)S(1)} copy(bf16[8,512,1]{2,1,0:T(8,128)(2,1)} %get-tuple-element.31) | data formatting | bytes 16384 | tf_op jit(solution)/shard_map/slice | solution.py:392
  70.5 0.2 copy.65
  70.7 2.3 %reduce-precision_convert_fusion = (bf16[8,131072]{1,0:T(8,128)(2,1)S(1)}, bf16[8,131072]{1,0:T(8,128)(2,1)S(1)}) fusion(bf16[8,131072]{1,0:T(8,128)(2,1)} %reshape_reshape.3), kind=kLoop, calls=%fused_computation.13 | loop fusion | flops 6291456 | bytes 6291456 | tf_op jit(solution)/shard_map/convert_element_type | solution.py:370
  73.1 3.2 %fusion = f32[24,32]{1,0:T(8,128)S(1)} fusion(s32[131072]{0:T(1024)S(1)} %bitcast.35, bf16[8,131072]{1,0:T(8,128)(2,1)S(1)} %get-tuple-element.33, bf16[8,131072]{1,0:T(8,128)(2,1)S(1)} %get-tuple-element.32, bf16[8,131072]{1,0:T(8,128)(2,1)S(1)} %copy-done.2), kind=kOutput, calls=%fused_computation.3 | convolution fusion | flops 224395264 | bytes 6818816 | tf_op jit(solution)/shard_map/fp,kp->fk/dot_general | solution.py:373
  76.3 0.7 fusion.13.refs_0_
  77.0 12.4 %shard_map.78 = f32[8,128]{1,0:T(8,128)} custom-call(f32[8,128]{1,0:T(8,128)} %fusion.13.refs_0_), custom_call_target="tpu_custom_call" | custom-call | tf_op jit(solution)/shard_map/pallas_call | solution.py:318
  89.4 0.7 slice_bitcast_fusion
  90.2 0.8 add_sqrt_fusion
  91.2 0.2 copy.64
  91.4 0.2 copy.66
  91.7 0.4 fusion.20
  92.2 3.3 %collective-permute-start.1 = (f32[8,512,1]{1,0,2:T(8,128)S(1)}, f32[8,512,1]{1,0,2:T(8,128)S(1)}, u32[]{:S(2)}, u32[]{:S(2)}) collective-permute-start(f32[8,512,1]{1,0,2:T(8,128)S(1)} %copy.68), channel_id=1, source_target_pairs={{1,0},{2,1},{3,2},{5,4},{6,5},{7,6},{9,8},{10,9},{11,10},{13,12},{... | collective-permute-start | bytes 49160 | tf_op jit(solution)/shard_map/ppermute | solution.py:406
  95.6 4.0 %collective-permute-start = (f32[8,512,1]{1,0,2:T(8,128)S(1)}, f32[8,512,1]{1,0,2:T(8,128)S(1)}, u32[]{:S(2)}, u32[]{:S(2)}) collective-permute-start(f32[8,512,1]{1,0,2:T(8,128)S(1)} %copy.67), channel_id=1, source_target_pairs={{0,1},{1,2},{2,3},{4,5},{5,6},{6,7},{8,9},{9,10},{10,11},{12,13},{... | collective-permute-start | bytes 49160 | tf_op jit(solution)/shard_map/ppermute | solution.py:405
  99.6 0.8 reduce_min.9
  100.4 2.0 %copy.70.refs_6_ = f32[8,512,1]{2,1,0:T(8,128)} copy(f32[8,512,1]{1,0,2:T(8,128)S(1)} %collective-permute-done.1) | data formatting | bytes 32768 | tf_op jit(solution)/shard_map/ppermute | solution.py:406
  102.4 2.0 %copy.69.refs_5_ = f32[8,512,1]{2,1,0:T(8,128)} copy(f32[8,512,1]{1,0,2:T(8,128)S(1)} %collective-permute-done) | data formatting | bytes 32768 | tf_op jit(solution)/shard_map/ppermute | solution.py:405
  104.4 12.7 %shard_map.79 = (bf16[8,512,256]{2,1,0:T(8,128)(2,1)}, bf16[8,512,256]{2,1,0:T(8,128)(2,1)}) custom-call(s32[1]{0:T(128)} %bitcast.refs_0_, f32[8,32]{1,0:T(8,128)} %copy-done.6, f32[8,32]{1,0:T(8,128)} %copy-done.5, bf16[8,512,256]{2,1,0:T(8,128)(2,1)} %bitcast.27, s32[512,256]{1,0:T(8,128)} %copy-done.1, f32[8,512,1]{2,1,0:T(8,128)} %copy.69.refs_5_, ...), custom_call_target="tpu_custom_call" | custom-call | tf_op jit(solution)/shard_map/pallas_call | solution.py:192
  (40 shorter events, 1.5 us)
Async XLA Ops:
  18.3 11.5 %copy-start.7 = (s32[32]{0:T(128)S(1)}, s32[32]{0:T(128)}, u32[]{:S(2)}) copy-start(s32[32]{0:T(128)} %refs_0_.1) | copy-start | bytes 388
  18.3 41.6 %all-to-all-start = ((bf16[128,2,16,256]{3,2,1,0:T(8,128)(2,1)}), bf16[128,2,16,256]{3,2,1,0:T(8,128)(2,1)S(1)}, u32[]{:S(2)}, u32[]{:S(2)}) async-start(bf16[128,2,16,256]{3,2,1,0:T(8,128)(2,1)} %bitcast.30), calls=%async_computation | async-start | bytes 4194304 | tf_op jit(solution)/shard_map/all_to_all | solution.py:354
  31.7 67.9 %copy-start.1 = (s32[512,256]{1,0:T(8,128)}, s32[512,256]{1,0:T(8,128)S(1)}, u32[]{:S(2)}) copy-start(s32[512,256]{1,0:T(8,128)S(1)} %convert_reduce_fusion.1.refs_4_) | copy-start | bytes 1572868
  59.9 1.3 %copy-start.3 = (bf16[128,2,16,256]{3,2,1,0:T(8,128)(2,1)}, bf16[128,2,16,256]{3,2,1,0:T(8,128)(2,1)S(1)}, u32[]{:S(2)}) copy-start(bf16[128,2,16,256]{3,2,1,0:T(8,128)(2,1)S(1)} %all-to-all-done) | copy-start | bytes 6291460
  63.0 4.1 %copy-start = (bf16[4,2,32,16,256]{4,3,2,1,0:T(8,128)(2,1)}, bf16[4,2,32,16,256]{4,3,2,1,0:T(8,128)(2,1)S(1)}, u32[]{:S(2)}) copy-start(bf16[4,2,32,16,256]{4,3,2,1,0:T(8,128)(2,1)S(1)} %copy.59) | copy-start | bytes 6291460
  68.7 4.4 %copy-start.2 = (bf16[8,131072]{1,0:T(8,128)(2,1)S(1)}, bf16[8,131072]{1,0:T(8,128)(2,1)}, u32[]{:S(2)}) copy-start(bf16[8,131072]{1,0:T(8,128)(2,1)} %reshape_reshape.3) | copy-start | bytes 6291460
  70.7 2.4 %copy-start.4 = (s32[64,2,8,128]{3,1,2,0:T(2,128)S(1)}, s32[64,2,8,128]{3,1,2,0:T(2,128)}, u32[]{:S(2)}) copy-start(s32[64,2,8,128]{3,1,2,0:T(2,128)} %copy.73) | copy-start | bytes 1572868
  91.0 13.4 %copy-start.5 = (f32[8,32]{1,0:T(8,128)}, f32[8,32]{1,0:T(8,128)S(1)}, u32[]{:S(2)}) copy-start(f32[8,32]{1,0:T(8,128)S(1)} %get-tuple-element.42.refs_2_) | copy-start | bytes 3076
  91.0 13.4 %copy-start.6 = (f32[8,32]{1,0:T(8,128)}, f32[8,32]{1,0:T(8,128)S(1)}, u32[]{:S(2)}) copy-start(f32[8,32]{1,0:T(8,128)S(1)} %get-tuple-element.43.refs_1_) | copy-start | bytes 3076
  92.2 8.2 %collective-permute-start.1 = (f32[8,512,1]{1,0,2:T(8,128)S(1)}, f32[8,512,1]{1,0,2:T(8,128)S(1)}, u32[]{:S(2)}, u32[]{:S(2)}) collective-permute-start(f32[8,512,1]{1,0,2:T(8,128)S(1)} %copy.68), channel_id=1, source_target_pairs={{1,0},{2,1},{3,2},{5,4},{6,5},{7,6},{9,8},{10,9},{11,10},{13,12},{... | collective-permute-start | bytes 49160 | tf_op jit(solution)/shard_map/ppermute | solution.py:406
  95.6 6.8 %collective-permute-start = (f32[8,512,1]{1,0,2:T(8,128)S(1)}, f32[8,512,1]{1,0,2:T(8,128)S(1)}, u32[]{:S(2)}, u32[]{:S(2)}) collective-permute-start(f32[8,512,1]{1,0,2:T(8,128)S(1)} %copy.67), channel_id=1, source_target_pairs={{0,1},{1,2},{2,3},{4,5},{5,6},{6,7},{8,9},{9,10},{10,11},{12,13},{... | collective-permute-start | bytes 49160 | tf_op jit(solution)/shard_map/ppermute | solution.py:405

commit v11 on v10

--- a/solution.py
+++ b/solution.py
@@ -80,8 +80,8 @@
     for inner in range(group):
         module = step * group + inner
         raw = raw_ref[:, inner]
-        code = raw // 2048
-        counts_adc = (raw % 2048).astype(jnp.float32)
+        code = lax.shift_right_logical(raw, 11)
+        counts_adc = (raw & 2047).astype(jnp.float32)
         base = jnp.where(
             code == 0, ped_ref[0, inner], jnp.where(code == 1, ped_ref[1, inner], ped_ref[2, inner])
         )

time: 118 us -> 115 us (0.975)
  Pallas kernels: 41.4 us -> 38.8 us
    pallas_call x1, Pallas kernels: 16.2 us -> 13.6 us  [calibrate_send(): pl.pallas_call(lambda *refs: calibrate_kernel(group, *refs), grid_spec=gr...]
where the time goes in v11:
time: 115 us
  Pallas kernels  38.8 us (34%)
  waiting for transfers between devices  20.9 us (18%)
  local copies, waits for them, and re-layouts  20.5 us (18%)
  starting transfers between devices  18.8 us (16%)
  other arithmetic  11.1 us (10%)
  matrix products  3.42 us (3%)
    all_to_all x1, waiting for transfers between devices, body(): got = lax.all_to_all(send, ('calib', 'peak'), 0, 0, tiled=True)  20.9 us
    pallas_call x1, Pallas kernels, calibrate_send(): pl.pallas_call(lambda *refs: calibrate_kernel(group, *refs), grid_spec=gr...  13.6 us
    pallas_call x1, Pallas kernels, score_outputs(): pl.pallas_call(lambda *refs: score_kernel(n_peak, levels, per, *refs), gr...  12.7 us
    pallas_call x1, Pallas kernels, gather_sum(): pl.pallas_call(lambda *refs: gather_sum_kernel(n_calib, n_peak, *refs), o...  12.4 us
    all_to_all x1, starting transfers between devices, body(): got = lax.all_to_all(send, ('calib', 'peak'), 0, 0, tiled=True)  11.5 us
    ppermute x1, starting transfers between devices, body(): left = lax.ppermute(edge_score[:, :, :1], 'peak', fwd)  4 us
    slice x2, local copies, waits for them, and re-layouts, body(): frame[:, :, width_here - 1]  3.42 us
    reduce_sum x2, other arithmetic, cycle_index(): return jnp.sum((dist[..., None] >= lows).astype(jnp.int32), axis=-1)  3.34 us
  transfers between devices with their start and end apart: 3, of which 1 were waited for; matrix products, arithmetic and copies ran while one was open for 10% of the time, Pallas kernels for 0%

profile of v11, /device:TPU:1, one launch (start us, length us, event | category | flops | bytes accessed | tf_op | source)
XLA Modules:
  0.0 114.5 jit_solution(14758820999285426245)
XLA Ops:
  0.6 0.8 copy.58
  1.4 0.7 reshape.185.refs_1_
  2.1 13.6 %shard_map.77 = bf16[32,4,2,16,256]{4,3,2,1,0:T(8,128)(2,1)} custom-call(s32[32]{0:T(128)} %refs_0_.1, s32[224]{0:T(256)} %reshape.185.refs_1_, s32[2,32,16,1024]{3,2,1,0:T(8,128)} %refs_2_.1, f32[3,32,16,1024]{3,2,1,0:T(8,128)} %refs_3_.1, bf16[3,32,16,1024]{3,2,1,0:T(8,128)(2,1)} %refs_4_.1, s32[32,16,1024]{2,1,0:T(8,128)} %refs_5_.1), custom_call_target="tpu_custom_call" | custom-call | tf_op jit(solution)/shard_map/pallas_call | solution.py:131
  15.7 11.5 %all-to-all-start = ((bf16[128,2,16,256]{3,2,1,0:T(8,128)(2,1)}), bf16[128,2,16,256]{3,2,1,0:T(8,128)(2,1)S(1)}, u32[]{:S(2)}, u32[]{:S(2)}) async-start(bf16[128,2,16,256]{3,2,1,0:T(8,128)(2,1)} %bitcast.30), calls=%async_computation | async-start | bytes 4194304 | tf_op jit(solution)/shard_map/all_to_all | solution.py:354
  27.5 1.6 %convert_reduce_fusion.1.refs_4_ = s32[512,256]{1,0:T(8,128)S(1)} fusion(s32[512,256]{1,0:T(8,128)S(1)} %broadcast_add_fusion.1, s32[31]{0:T(128)S(1)} %multiply_multiply_fusion), kind=kLoop, calls=%fused_computation.5 | loop fusion | flops 12058624 | bytes 1048700 | tf_op jit(solution)/shard_map/reduce_sum | solution.py:34
  29.3 1.1 copy.73
  30.9 1.1 constant_dynamic-slice_fusion
  32.2 1.7 %convert_reduce_fusion = s32[32,16,256]{2,1,0:T(8,128)S(1)} fusion(s32[32,16,256]{2,1,0:T(8,128)S(1)} %broadcast_add_fusion, s32[31]{0:T(128)S(1)} %multiply_multiply_fusion), kind=kLoop, calls=%fused_computation.4 | loop fusion | flops 12058624 | bytes 1048700 | tf_op jit(solution)/shard_map/reduce_sum | solution.py:34
  33.9 2.5 %select_reduce_fusion = s32[32]{0:T(128)S(1)} fusion(s32[32,16,256]{2,1,0:T(8,128)S(1)} %constant_dynamic-slice_fusion, s32[32,16,256]{2,1,0:T(8,128)S(1)} %convert_reduce_fusion), kind=kLoop, calls=%fused_computation | loop fusion | flops 12582880 | bytes 1048704 | tf_op jit(solution)/shard_map/reduce_sum | solution.py:224
  36.4 20.9 %all-to-all-done = bf16[128,2,16,256]{3,2,1,0:T(8,128)(2,1)S(1)} async-done(((bf16[128,2,16,256]{3,2,1,0:T(8,128)(2,1)}), bf16[128,2,16,256]{3,2,1,0:T(8,128)(2,1)S(1)}, u32[]{:S(2)}, u32[]{:S(2)}) %all-to-all-start) | async-done | bytes 2097184 | tf_op jit(solution)/shard_map/all_to_all | solution.py:354
  57.3 1.3 %copy-done.3 = bf16[128,2,16,256]{3,2,1,0:T(8,128)(2,1)} copy-done((bf16[128,2,16,256]{3,2,1,0:T(8,128)(2,1)}, bf16[128,2,16,256]{3,2,1,0:T(8,128)(2,1)S(1)}, u32[]{:S(2)}) %copy-start.3) | copy-done | bytes 2097176
  58.6 1.8 %copy.59 = bf16[4,2,32,16,256]{4,3,2,1,0:T(8,128)(2,1)S(1)} copy(bf16[4,2,32,16,256]{4,3,1,0,2:T(8,128)(2,1)} %bitcast.29) | data formatting | bytes 4194304 | tf_op jit(solution)/shard_map/transpose | solution.py:356
  60.4 2.3 %reshape_reshape.3 = bf16[8,131072]{1,0:T(8,128)(2,1)} reshape(bf16[4,2,32,16,256]{4,3,2,1,0:T(8,128)(2,1)S(1)} %copy.59) | data formatting | bytes 4194304 | tf_op jit(solution)/shard_map/reshape;reshape | solution.py:366
  62.7 1.8 %fusion.19 = (bf16[8,512,1]{2,1,0:T(8,128)(2,1)}, bf16[8,512,1]{2,1,0:T(8,128)(2,1)}) fusion(bf16[8,512,256]{2,1,0:T(8,128)(2,1)S(1)} %bitcast.26), kind=kLoop, calls=%fused_computation.54 | loop fusion | bytes 32768 | tf_op jit(solution)/shard_map/slice | solution.py:392
  64.5 1.6 %copy.62 = bf16[8,512,1]{1,0,2:T(8,128)(2,1)S(1)} copy(bf16[8,512,1]{2,1,0:T(8,128)(2,1)} %get-tuple-element.30) | data formatting | bytes 16384 | tf_op jit(solution)/shard_map/slice | solution.py:392
  66.1 1.7 %copy.63 = bf16[8,512,1]{1,0,2:T(8,128)(2,1)S(1)} copy(bf16[8,512,1]{2,1,0:T(8,128)(2,1)} %get-tuple-element.31) | data formatting | bytes 16384 | tf_op jit(solution)/shard_map/slice | solution.py:392
  67.9 0.2 copy.65
  68.1 2.3 %reduce-precision_convert_fusion = (bf16[8,131072]{1,0:T(8,128)(2,1)S(1)}, bf16[8,131072]{1,0:T(8,128)(2,1)S(1)}) fusion(bf16[8,131072]{1,0:T(8,128)(2,1)} %reshape_reshape.3), kind=kLoop, calls=%fused_computation.13 | loop fusion | flops 6291456 | bytes 6291456 | tf_op jit(solution)/shard_map/convert_element_type | solution.py:370
  70.5 3.2 %fusion = f32[24,32]{1,0:T(8,128)S(1)} fusion(s32[131072]{0:T(1024)S(1)} %bitcast.35, bf16[8,131072]{1,0:T(8,128)(2,1)S(1)} %get-tuple-element.33, bf16[8,131072]{1,0:T(8,128)(2,1)S(1)} %get-tuple-element.32, bf16[8,131072]{1,0:T(8,128)(2,1)S(1)} %copy-done.2), kind=kOutput, calls=%fused_computation.3 | convolution fusion | flops 224395264 | bytes 6818816 | tf_op jit(solution)/shard_map/fp,kp->fk/dot_general | solution.py:373
  73.7 0.7 fusion.13.refs_0_
  74.4 12.4 %shard_map.78 = f32[8,128]{1,0:T(8,128)} custom-call(f32[8,128]{1,0:T(8,128)} %fusion.13.refs_0_), custom_call_target="tpu_custom_call" | custom-call | tf_op jit(solution)/shard_map/pallas_call | solution.py:318
  86.8 0.7 slice_bitcast_fusion
  87.6 0.8 add_sqrt_fusion
  88.6 0.2 copy.64
  88.8 0.2 copy.66
  89.1 0.4 fusion.20
  89.6 3.3 %collective-permute-start.1 = (f32[8,512,1]{1,0,2:T(8,128)S(1)}, f32[8,512,1]{1,0,2:T(8,128)S(1)}, u32[]{:S(2)}, u32[]{:S(2)}) collective-permute-start(f32[8,512,1]{1,0,2:T(8,128)S(1)} %copy.68), channel_id=1, source_target_pairs={{1,0},{2,1},{3,2},{5,4},{6,5},{7,6},{9,8},{10,9},{11,10},{13,12},{... | collective-permute-start | bytes 49160 | tf_op jit(solution)/shard_map/ppermute | solution.py:406
  93.0 4.0 %collective-permute-start = (f32[8,512,1]{1,0,2:T(8,128)S(1)}, f32[8,512,1]{1,0,2:T(8,128)S(1)}, u32[]{:S(2)}, u32[]{:S(2)}) collective-permute-start(f32[8,512,1]{1,0,2:T(8,128)S(1)} %copy.67), channel_id=1, source_target_pairs={{0,1},{1,2},{2,3},{4,5},{5,6},{6,7},{8,9},{9,10},{10,11},{12,13},{... | collective-permute-start | bytes 49160 | tf_op jit(solution)/shard_map/ppermute | solution.py:405
  97.0 0.8 reduce_min.9
  97.8 2.0 %copy.70.refs_6_ = f32[8,512,1]{2,1,0:T(8,128)} copy(f32[8,512,1]{1,0,2:T(8,128)S(1)} %collective-permute-done.1) | data formatting | bytes 32768 | tf_op jit(solution)/shard_map/ppermute | solution.py:406
  99.8 2.0 %copy.69.refs_5_ = f32[8,512,1]{2,1,0:T(8,128)} copy(f32[8,512,1]{1,0,2:T(8,128)S(1)} %collective-permute-done) | data formatting | bytes 32768 | tf_op jit(solution)/shard_map/ppermute | solution.py:405
  101.8 12.7 %shard_map.79 = (bf16[8,512,256]{2,1,0:T(8,128)(2,1)}, bf16[8,512,256]{2,1,0:T(8,128)(2,1)}) custom-call(s32[1]{0:T(128)} %bitcast.refs_0_, f32[8,32]{1,0:T(8,128)} %copy-done.6, f32[8,32]{1,0:T(8,128)} %copy-done.5, bf16[8,512,256]{2,1,0:T(8,128)(2,1)} %bitcast.27, s32[512,256]{1,0:T(8,128)} %copy-done.1, f32[8,512,1]{2,1,0:T(8,128)} %copy.69.refs_5_, ...), custom_call_target="tpu_custom_call" | custom-call | tf_op jit(solution)/shard_map/pallas_call | solution.py:192
  (40 shorter events, 1.5 us)
Async XLA Ops:
  15.7 11.5 %copy-start.7 = (s32[32]{0:T(128)S(1)}, s32[32]{0:T(128)}, u32[]{:S(2)}) copy-start(s32[32]{0:T(128)} %refs_0_.1) | copy-start | bytes 388
  15.7 41.6 %all-to-all-start = ((bf16[128,2,16,256]{3,2,1,0:T(8,128)(2,1)}), bf16[128,2,16,256]{3,2,1,0:T(8,128)(2,1)S(1)}, u32[]{:S(2)}, u32[]{:S(2)}) async-start(bf16[128,2,16,256]{3,2,1,0:T(8,128)(2,1)} %bitcast.30), calls=%async_computation | async-start | bytes 4194304 | tf_op jit(solution)/shard_map/all_to_all | solution.py:354
  29.1 67.9 %copy-start.1 = (s32[512,256]{1,0:T(8,128)}, s32[512,256]{1,0:T(8,128)S(1)}, u32[]{:S(2)}) copy-start(s32[512,256]{1,0:T(8,128)S(1)} %convert_reduce_fusion.1.refs_4_) | copy-start | bytes 1572868
  57.3 1.3 %copy-start.3 = (bf16[128,2,16,256]{3,2,1,0:T(8,128)(2,1)}, bf16[128,2,16,256]{3,2,1,0:T(8,128)(2,1)S(1)}, u32[]{:S(2)}) copy-start(bf16[128,2,16,256]{3,2,1,0:T(8,128)(2,1)S(1)} %all-to-all-done) | copy-start | bytes 6291460
  60.4 4.1 %copy-start = (bf16[4,2,32,16,256]{4,3,2,1,0:T(8,128)(2,1)}, bf16[4,2,32,16,256]{4,3,2,1,0:T(8,128)(2,1)S(1)}, u32[]{:S(2)}) copy-start(bf16[4,2,32,16,256]{4,3,2,1,0:T(8,128)(2,1)S(1)} %copy.59) | copy-start | bytes 6291460
  66.1 4.4 %copy-start.2 = (bf16[8,131072]{1,0:T(8,128)(2,1)S(1)}, bf16[8,131072]{1,0:T(8,128)(2,1)}, u32[]{:S(2)}) copy-start(bf16[8,131072]{1,0:T(8,128)(2,1)} %reshape_reshape.3) | copy-start | bytes 6291460
  68.1 2.4 %copy-start.4 = (s32[64,2,8,128]{3,1,2,0:T(2,128)S(1)}, s32[64,2,8,128]{3,1,2,0:T(2,128)}, u32[]{:S(2)}) copy-start(s32[64,2,8,128]{3,1,2,0:T(2,128)} %copy.73) | copy-start | bytes 1572868
  88.4 13.4 %copy-start.5 = (f32[8,32]{1,0:T(8,128)}, f32[8,32]{1,0:T(8,128)S(1)}, u32[]{:S(2)}) copy-start(f32[8,32]{1,0:T(8,128)S(1)} %get-tuple-element.42.refs_2_) | copy-start | bytes 3076
  88.4 13.4 %copy-start.6 = (f32[8,32]{1,0:T(8,128)}, f32[8,32]{1,0:T(8,128)S(1)}, u32[]{:S(2)}) copy-start(f32[8,32]{1,0:T(8,128)S(1)} %get-tuple-element.43.refs_1_) | copy-start | bytes 3076
  89.6 8.2 %collective-permute-start.1 = (f32[8,512,1]{1,0,2:T(8,128)S(1)}, f32[8,512,1]{1,0,2:T(8,128)S(1)}, u32[]{:S(2)}, u32[]{:S(2)}) collective-permute-start(f32[8,512,1]{1,0,2:T(8,128)S(1)} %copy.68), channel_id=1, source_target_pairs={{1,0},{2,1},{3,2},{5,4},{6,5},{7,6},{9,8},{10,9},{11,10},{13,12},{... | collective-permute-start | bytes 49160 | tf_op jit(solution)/shard_map/ppermute | solution.py:406
  93.0 6.8 %collective-permute-start = (f32[8,512,1]{1,0,2:T(8,128)S(1)}, f32[8,512,1]{1,0,2:T(8,128)S(1)}, u32[]{:S(2)}, u32[]{:S(2)}) collective-permute-start(f32[8,512,1]{1,0,2:T(8,128)S(1)} %copy.67), channel_id=1, source_target_pairs={{0,1},{1,2},{2,3},{4,5},{5,6},{6,7},{8,9},{9,10},{10,11},{12,13},{... | collective-permute-start | bytes 49160 | tf_op jit(solution)/shard_map/ppermute | solution.py:405

commit v12 on v11

--- a/solution.py
+++ b/solution.py
@@ -163,8 +163,13 @@
             pixel_mean = jnp.where(hit, mean_ref[frame_pos, level], pixel_mean)
             pixel_rms = jnp.where(hit, rms_ref[frame_pos, level], pixel_rms)
         score = (values - pixel_mean) / pixel_rms
-        left_col = jnp.where(peak_pos == 0, 0.0, left_ref[inner])
-        right_col = jnp.where(peak_pos == n_peak - 1, 0.0, right_ref[inner])
+        pick = lax.broadcasted_iota(jnp.int32, (rows, left_ref.shape[0]), 1) == frame_pos
+        left_all = jnp.transpose(left_ref[...])
+        right_all = jnp.transpose(right_ref[...])
+        left_col = jnp.sum(jnp.where(pick, left_all, 0.0), axis=1, keepdims=True)
+        right_col = jnp.sum(jnp.where(pick, right_all, 0.0), axis=1, keepdims=True)
+        left_col = jnp.where(peak_pos == 0, 0.0, left_col)
+        right_col = jnp.where(peak_pos == n_peak - 1, 0.0, right_col)
         total = 4.0 * score
         for shift, inside in row_shifts:
             total = total - jnp.where(inside, pltpu.roll(score, shift, 0), 0.0)
@@ -182,7 +187,7 @@
     per = 2 if frames % 2 == 0 else 1
     low = jnp.min(cycle).reshape(1)
     block = pl.BlockSpec((per, rows, cols), lambda f, *_: (f, 0, 0))
-    edge = pl.BlockSpec((per, rows, 1), lambda f, *_: (f, 0, 0))
+    edge = pl.BlockSpec((frames, rows), lambda f, *_: (0, 0))
     grid_spec = pltpu.PrefetchScalarGridSpec(
         num_scalar_prefetch=3,
         grid=(frames // per,),
@@ -402,8 +407,8 @@
     edge_score = (edge_values.astype(jnp.float32) - edge_mean) / edge_rms
     fwd = [(i, i + 1) for i in range(n_peak - 1)]
     bwd = [(i + 1, i) for i in range(n_peak - 1)]
-    left = lax.ppermute(edge_score[:, :, :1], "peak", fwd)
-    right = lax.ppermute(edge_score[:, :, 1:], "peak", bwd)
+    left = lax.ppermute(edge_score[:, :, 0], "peak", fwd)
+    right = lax.ppermute(edge_score[:, :, 1], "peak", bwd)
     snr, bent = score_outputs(frame, cycle, cycle_average, cycle_rms, left, right, n_peak)
     return (snr[:, None], bent[:, None])
 

time: 115 us -> 116 us (level)
  local copies, waits for them, and re-layouts: 20.5 us -> 15.7 us
  waiting for transfers between devices: 20.9 us -> 25.3 us
  Pallas kernels: 38.8 us -> 40.1 us
    ppermute x2 -> x0, local copies, waits for them, and re-layouts: 3.95 us -> none  [the longest x1 1.98 us: body(): right = lax.ppermute(edge_score[:, :, 1:], 'peak', bwd)]
    ppermute x2, waiting for transfers between devices: 0.01 us -> 3.57 us  [the longest x1 3.57 us: body(): right = lax.ppermute(edge_score[:, :, 1], 'peak', bwd)]
    unnamed x18 -> x22, local copies, waits for them, and re-layouts: 3.2 us -> 6.17 us
    slice x4 -> x0, local copies, waits for them, and re-layouts: 2.34 us -> none  [the longest x1 1.75 us: body(): frame[:, :, 0]]
    slice x2 -> x1, local copies, waits for them, and re-layouts: 3.42 us -> 1.82 us  [body(): frame[:, :, width_here - 1]]
    pallas_call x1, Pallas kernels: 12.7 us -> 14.1 us  [score_outputs(): pl.pallas_call(lambda *refs: score_kernel(n_peak, levels, per, *refs), gr...]
  transfers between devices with their start and end apart: 3 -> 3, of which waited for: 1 -> 2; matrix products, arithmetic and copies ran while one was open for 10% -> 8% of each run, Pallas kernels for 0% -> 0%
where the time goes in v12:
time: 116 us; the launch traced here: 115 us
  Pallas kernels  40.1 us (35%)
  waiting for transfers between devices  25.3 us (22%)
  starting transfers between devices  18.6 us (16%)
  local copies, waits for them, and re-layouts  15.7 us (14%)
  other arithmetic  11.2 us (10%)
  matrix products  3.41 us (3%)
    all_to_all x1, waiting for transfers between devices, body(): got = lax.all_to_all(send, ('calib', 'peak'), 0, 0, tiled=True)  21.7 us
    pallas_call x1, Pallas kernels, score_outputs(): pl.pallas_call(lambda *refs: score_kernel(n_peak, levels, per, *refs), gr...  14.1 us
    pallas_call x1, Pallas kernels, calibrate_send(): pl.pallas_call(lambda *refs: calibrate_kernel(group, *refs), grid_spec=gr...  13.6 us
    pallas_call x1, Pallas kernels, gather_sum(): pl.pallas_call(lambda *refs: gather_sum_kernel(n_calib, n_peak, *refs), o...  12.4 us
    all_to_all x1, starting transfers between devices, body(): got = lax.all_to_all(send, ('calib', 'peak'), 0, 0, tiled=True)  11.5 us
    unnamed x22, local copies, waits for them, and re-layouts  6.17 us
    ppermute x1, starting transfers between devices, body(): left = lax.ppermute(edge_score[:, :, 0], 'peak', fwd)  5 us
    ppermute x1, waiting for transfers between devices, body(): right = lax.ppermute(edge_score[:, :, 1], 'peak', bwd)  3.57 us
  transfers between devices with their start and end apart: 3, of which 2 were waited for; matrix products, arithmetic and copies ran while one was open for 8% of the time, Pallas kernels for 0%

profile of v12, /device:TPU:1, one launch (start us, length us, event | category | flops | bytes accessed | tf_op | source)
XLA Modules:
  0.0 115.3 jit_solution(15334329712219898842)
XLA Ops:
  0.6 0.8 copy.47
  1.4 0.7 reshape.185.refs_1_
  2.1 13.6 %shard_map.77 = bf16[32,4,2,16,256]{4,3,2,1,0:T(8,128)(2,1)} custom-call(s32[32]{0:T(128)} %refs_0_.1, s32[224]{0:T(256)} %reshape.185.refs_1_, s32[2,32,16,1024]{3,2,1,0:T(8,128)} %refs_2_.1, f32[3,32,16,1024]{3,2,1,0:T(8,128)} %refs_3_.1, bf16[3,32,16,1024]{3,2,1,0:T(8,128)(2,1)} %refs_4_.1, s32[32,16,1024]{2,1,0:T(8,128)} %refs_5_.1), custom_call_target="tpu_custom_call" | custom-call | tf_op jit(solution)/shard_map/pallas_call | solution.py:131
  15.7 11.5 %all-to-all-start = ((bf16[128,2,16,256]{3,2,1,0:T(8,128)(2,1)}), bf16[128,2,16,256]{3,2,1,0:T(8,128)(2,1)S(1)}, u32[]{:S(2)}, u32[]{:S(2)}) async-start(bf16[128,2,16,256]{3,2,1,0:T(8,128)(2,1)} %bitcast.30), calls=%async_computation | async-start | bytes 4194304 | tf_op jit(solution)/shard_map/all_to_all | solution.py:359
  27.5 1.6 %convert_reduce_fusion.1.refs_4_ = s32[512,256]{1,0:T(8,128)S(1)} fusion(s32[512,256]{1,0:T(8,128)S(1)} %broadcast_add_fusion.1, s32[31]{0:T(128)S(1)} %multiply_multiply_fusion), kind=kLoop, calls=%fused_computation.5 | loop fusion | flops 12058624 | bytes 1048700 | tf_op jit(solution)/shard_map/reduce_sum | solution.py:34
  29.3 0.3 copy.61
  30.1 1.1 constant_dynamic-slice_fusion
  31.4 1.7 %convert_reduce_fusion = s32[32,16,256]{2,1,0:T(8,128)S(1)} fusion(s32[32,16,256]{2,1,0:T(8,128)S(1)} %broadcast_add_fusion, s32[31]{0:T(128)S(1)} %multiply_multiply_fusion), kind=kLoop, calls=%fused_computation.4 | loop fusion | flops 12058624 | bytes 1048700 | tf_op jit(solution)/shard_map/reduce_sum | solution.py:34
  33.1 2.5 %select_reduce_fusion = s32[32]{0:T(128)S(1)} fusion(s32[32,16,256]{2,1,0:T(8,128)S(1)} %constant_dynamic-slice_fusion, s32[32,16,256]{2,1,0:T(8,128)S(1)} %convert_reduce_fusion), kind=kLoop, calls=%fused_computation | loop fusion | flops 12582880 | bytes 1048704 | tf_op jit(solution)/shard_map/reduce_sum | solution.py:229
  35.6 21.7 %all-to-all-done = bf16[128,2,16,256]{3,2,1,0:T(8,128)(2,1)S(1)} async-done(((bf16[128,2,16,256]{3,2,1,0:T(8,128)(2,1)}), bf16[128,2,16,256]{3,2,1,0:T(8,128)(2,1)S(1)}, u32[]{:S(2)}, u32[]{:S(2)}) %all-to-all-start) | async-done | bytes 2097184 | tf_op jit(solution)/shard_map/all_to_all | solution.py:359
  57.3 1.3 %copy-done.3 = bf16[128,2,16,256]{3,2,1,0:T(8,128)(2,1)} copy-done((bf16[128,2,16,256]{3,2,1,0:T(8,128)(2,1)}, bf16[128,2,16,256]{3,2,1,0:T(8,128)(2,1)S(1)}, u32[]{:S(2)}) %copy-start.3) | copy-done | bytes 2097176
  58.6 1.8 %copy.48 = bf16[4,2,32,16,256]{4,3,2,1,0:T(8,128)(2,1)S(1)} copy(bf16[4,2,32,16,256]{4,3,1,0,2:T(8,128)(2,1)} %bitcast.29) | data formatting | bytes 4194304 | tf_op jit(solution)/shard_map/transpose | solution.py:361
  60.4 2.3 %reshape_reshape.3 = bf16[8,131072]{1,0:T(8,128)(2,1)} reshape(bf16[4,2,32,16,256]{4,3,2,1,0:T(8,128)(2,1)S(1)} %copy.48) | data formatting | bytes 4194304 | tf_op jit(solution)/shard_map/reshape;reshape | solution.py:371
  62.7 2.4 %reduce-precision_convert_fusion = (bf16[8,131072]{1,0:T(8,128)(2,1)S(1)}, bf16[8,131072]{1,0:T(8,128)(2,1)S(1)}) fusion(bf16[8,131072]{1,0:T(8,128)(2,1)} %reshape_reshape.3), kind=kLoop, calls=%fused_computation.13 | loop fusion | flops 6291456 | bytes 6291456 | tf_op jit(solution)/shard_map/convert_element_type | solution.py:375
  65.1 3.2 %fusion = f32[24,32]{1,0:T(8,128)S(1)} fusion(s32[131072]{0:T(1024)S(1)} %bitcast.33, bf16[8,131072]{1,0:T(8,128)(2,1)S(1)} %get-tuple-element.31, bf16[8,131072]{1,0:T(8,128)(2,1)S(1)} %get-tuple-element.30, bf16[8,131072]{1,0:T(8,128)(2,1)S(1)} %copy-done.2), kind=kOutput, calls=%fused_computation.3 | convolution fusion | flops 224395264 | bytes 6818816 | tf_op jit(solution)/shard_map/fp,kp->fk/dot_general | solution.py:378
  68.4 0.7 fusion.13.refs_0_
  69.1 12.4 %shard_map.78 = f32[8,128]{1,0:T(8,128)} custom-call(f32[8,128]{1,0:T(8,128)} %fusion.13.refs_0_), custom_call_target="tpu_custom_call" | custom-call | tf_op jit(solution)/shard_map/pallas_call | solution.py:323
  81.5 0.8 slice_bitcast_fusion.2
  82.2 0.8 add_sqrt_fusion
  83.2 0.2 copy.55
  83.5 0.2 copy.56
  83.6 0.2 copy.53
  83.8 0.2 copy.54
  84.0 1.8 %fusion.19 = (bf16[8,512,1]{2,1,0:T(8,128)(2,1)}, bf16[8,512,1]{2,1,0:T(8,128)(2,1)}) fusion(bf16[8,512,256]{2,1,0:T(8,128)(2,1)S(1)} %bitcast.26), kind=kLoop, calls=%fused_computation.55 | loop fusion | bytes 32768 | tf_op jit(solution)/shard_map/slice | solution.py:397
  85.8 1.6 %copy.60 = bf16[8,512,1]{1,0,2:T(8,128)(2,1)S(1)} copy(bf16[8,512,1]{2,1,0:T(8,128)(2,1)} %get-tuple-element.29) | data formatting | bytes 16384
  87.4 1.6 %copy.59 = bf16[8,512,1]{1,0,2:T(8,128)(2,1)S(1)} copy(bf16[8,512,1]{2,1,0:T(8,128)(2,1)} %get-tuple-element.28) | data formatting | bytes 16384
  89.1 5.0 %collective-permute-start = (f32[8,512]{1,0:T(8,128)S(1)}, f32[8,512]{1,0:T(8,128)S(1)}, u32[]{:S(2)}, u32[]{:S(2)}) collective-permute-start(f32[8,512]{1,0:T(8,128)S(1)} %get-tuple-element.37), channel_id=1, source_target_pairs={{0,1},{1,2},{2,3},{4,5},{5,6},{6,7},{8,9},{9,10},{10,11},{12,13},{... | collective-permute-start | bytes 49160 | tf_op jit(solution)/shard_map/ppermute | solution.py:410
  94.1 2.1 %collective-permute-start.1 = (f32[8,512]{1,0:T(8,128)S(1)}, f32[8,512]{1,0:T(8,128)S(1)}, u32[]{:S(2)}, u32[]{:S(2)}) collective-permute-start(f32[8,512]{1,0:T(8,128)S(1)} %get-tuple-element.36), channel_id=1, source_target_pairs={{1,0},{2,1},{3,2},{5,4},{6,5},{7,6},{9,8},{10,9},{11,10},{13,12},{... | collective-permute-start | bytes 49160 | tf_op jit(solution)/shard_map/ppermute | solution.py:411
  96.2 0.8 reduce_min.9
  97.1 3.6 %collective-permute-done.1.refs_6_ = f32[8,512]{1,0:T(8,128)S(1)} collective-permute-done((f32[8,512]{1,0:T(8,128)S(1)}, f32[8,512]{1,0:T(8,128)S(1)}, u32[]{:S(2)}, u32[]{:S(2)}) %collective-permute-start.1) | collective-permute-done | bytes 16416 | tf_op jit(solution)/shard_map/ppermute | solution.py:411
  100.7 0.6 copy-done.7
  101.2 14.1 %shard_map.79 = (bf16[8,512,256]{2,1,0:T(8,128)(2,1)}, bf16[8,512,256]{2,1,0:T(8,128)(2,1)}) custom-call(s32[1]{0:T(128)} %bitcast.refs_0_, f32[8,32]{1,0:T(8,128)} %copy-done.5, f32[8,32]{1,0:T(8,128)} %copy-done.4, bf16[8,512,256]{2,1,0:T(8,128)(2,1)} %bitcast.27, s32[512,256]{1,0:T(8,128)} %copy-done.1, f32[8,512]{1,0:T(8,128)} %copy-done.6, ...), custom_call_target="tpu_custom_call" | custom-call | tf_op jit(solution)/shard_map/pallas_call | solution.py:197
  (38 shorter events, 1.3 us)
Async XLA Ops:
  15.7 11.5 %copy-start.8 = (s32[32]{0:T(128)S(1)}, s32[32]{0:T(128)}, u32[]{:S(2)}) copy-start(s32[32]{0:T(128)} %refs_0_.1) | copy-start | bytes 388
  15.7 41.6 %all-to-all-start = ((bf16[128,2,16,256]{3,2,1,0:T(8,128)(2,1)}), bf16[128,2,16,256]{3,2,1,0:T(8,128)(2,1)S(1)}, u32[]{:S(2)}, u32[]{:S(2)}) async-start(bf16[128,2,16,256]{3,2,1,0:T(8,128)(2,1)} %bitcast.30), calls=%async_computation | async-start | bytes 4194304 | tf_op jit(solution)/shard_map/all_to_all | solution.py:359
  29.1 67.1 %copy-start.1 = (s32[512,256]{1,0:T(8,128)}, s32[512,256]{1,0:T(8,128)S(1)}, u32[]{:S(2)}) copy-start(s32[512,256]{1,0:T(8,128)S(1)} %convert_reduce_fusion.1.refs_4_) | copy-start | bytes 1572868
  57.3 1.3 %copy-start.3 = (bf16[128,2,16,256]{3,2,1,0:T(8,128)(2,1)}, bf16[128,2,16,256]{3,2,1,0:T(8,128)(2,1)S(1)}, u32[]{:S(2)}) copy-start(bf16[128,2,16,256]{3,2,1,0:T(8,128)(2,1)S(1)} %all-to-all-done) | copy-start | bytes 6291460
  60.4 23.6 %copy-start = (bf16[4,2,32,16,256]{4,3,2,1,0:T(8,128)(2,1)}, bf16[4,2,32,16,256]{4,3,2,1,0:T(8,128)(2,1)S(1)}, u32[]{:S(2)}) copy-start(bf16[4,2,32,16,256]{4,3,2,1,0:T(8,128)(2,1)S(1)} %copy.48) | copy-start | bytes 6291460
  62.7 2.4 %copy-start.2 = (bf16[8,131072]{1,0:T(8,128)(2,1)S(1)}, bf16[8,131072]{1,0:T(8,128)(2,1)}, u32[]{:S(2)}) copy-start(bf16[8,131072]{1,0:T(8,128)(2,1)} %reshape_reshape.3) | copy-start | bytes 6291460
  83.0 6.0 %copy-start.4 = (f32[8,32]{1,0:T(8,128)}, f32[8,32]{1,0:T(8,128)S(1)}, u32[]{:S(2)}) copy-start(f32[8,32]{1,0:T(8,128)S(1)} %get-tuple-element.40.refs_2_) | copy-start | bytes 3076
  83.1 6.0 %copy-start.5 = (f32[8,32]{1,0:T(8,128)}, f32[8,32]{1,0:T(8,128)S(1)}, u32[]{:S(2)}) copy-start(f32[8,32]{1,0:T(8,128)S(1)} %get-tuple-element.41.refs_1_) | copy-start | bytes 3076
  89.1 8.0 %collective-permute-start = (f32[8,512]{1,0:T(8,128)S(1)}, f32[8,512]{1,0:T(8,128)S(1)}, u32[]{:S(2)}, u32[]{:S(2)}) collective-permute-start(f32[8,512]{1,0:T(8,128)S(1)} %get-tuple-element.37), channel_id=1, source_target_pairs={{0,1},{1,2},{2,3},{4,5},{5,6},{6,7},{8,9},{9,10},{10,11},{12,13},{... | collective-permute-start | bytes 49160 | tf_op jit(solution)/shard_map/ppermute | solution.py:410
  94.1 6.6 %collective-permute-start.1 = (f32[8,512]{1,0:T(8,128)S(1)}, f32[8,512]{1,0:T(8,128)S(1)}, u32[]{:S(2)}, u32[]{:S(2)}) collective-permute-start(f32[8,512]{1,0:T(8,128)S(1)} %get-tuple-element.36), channel_id=1, source_target_pairs={{1,0},{2,1},{3,2},{5,4},{6,5},{7,6},{9,8},{10,9},{11,10},{13,12},{... | collective-permute-start | bytes 49160 | tf_op jit(solution)/shard_map/ppermute | solution.py:411
  97.1 3.6 %copy-start.6 = (f32[8,512]{1,0:T(8,128)}, f32[8,512]{1,0:T(8,128)S(1)}, u32[]{:S(2)}) copy-start(f32[8,512]{1,0:T(8,128)S(1)} %collective-permute-done.refs_5_) | copy-start | bytes 49156
  100.6 0.6 copy-start.7

commit v13 on v12

--- a/solution.py
+++ b/solution.py
@@ -393,22 +393,20 @@
     second = summed[:, CYCLES : 2 * CYCLES]
     present_flag = summed[0, 2 * CYCLES : 3 * CYCLES]
     cycle_average, cycle_rms = cycle_stats(first, second, present_flag)
-    edge_cycle = jnp.stack([cycle[:, width_here - 1], cycle[:, 0]], axis=1)
-    edge_values = jnp.stack([frame[:, :, width_here - 1], frame[:, :, 0]], axis=2)
-    edge_hits = (edge_cycle.reshape(1, -1) == levels[:, None]).astype(jnp.float32)
+    edge_cycle = jnp.concatenate([cycle[:, width_here - 1], cycle[:, 0]])
+    edge_values = jnp.concatenate([frame[:, :, width_here - 1], frame[:, :, 0]], axis=1)
+    edge_hits = (edge_cycle[None, :] == levels[:, None]).astype(jnp.float32)
     edge_table = jnp.einsum(
         "fk,kp->fp",
         jnp.concatenate([cycle_average, cycle_rms], axis=0),
         edge_hits,
         precision=precise_variant,
-    ).reshape(2 * frames_all, mrows, 2)
-    edge_mean = edge_table[:frames_all]
-    edge_rms = edge_table[frames_all:]
-    edge_score = (edge_values.astype(jnp.float32) - edge_mean) / edge_rms
+    )
+    edge_score = (edge_values.astype(jnp.float32) - edge_table[:frames_all]) / edge_table[frames_all:]
     fwd = [(i, i + 1) for i in range(n_peak - 1)]
     bwd = [(i + 1, i) for i in range(n_peak - 1)]
-    left = lax.ppermute(edge_score[:, :, 0], "peak", fwd)
-    right = lax.ppermute(edge_score[:, :, 1], "peak", bwd)
+    left = lax.ppermute(edge_score[:, :mrows], "peak", fwd)
+    right = lax.ppermute(edge_score[:, mrows:], "peak", bwd)
     snr, bent = score_outputs(frame, cycle, cycle_average, cycle_rms, left, right, n_peak)
     return (snr[:, None], bent[:, None])
 

time: 116 us -> 115 us (level)
  no operation moved by 1% of the time
where the time goes in v13:
time: 115 us; the launch traced here: 114 us
  Pallas kernels  40 us (35%)
  waiting for transfers between devices  25.5 us (22%)
  starting transfers between devices  18.6 us (16%)
  local copies, waits for them, and re-layouts  15 us (13%)
  other arithmetic  11 us (10%)
  matrix products  3.42 us (3%)
    all_to_all x1, waiting for transfers between devices, body(): got = lax.all_to_all(send, ('calib', 'peak'), 0, 0, tiled=True)  21.9 us
    pallas_call x1, Pallas kernels, score_outputs(): pl.pallas_call(lambda *refs: score_kernel(n_peak, levels, per, *refs), gr...  14 us
    pallas_call x1, Pallas kernels, calibrate_send(): pl.pallas_call(lambda *refs: calibrate_kernel(group, *refs), grid_spec=gr...  13.6 us
    pallas_call x1, Pallas kernels, gather_sum(): pl.pallas_call(lambda *refs: gather_sum_kernel(n_calib, n_peak, *refs), o...  12.4 us
    all_to_all x1, starting transfers between devices, body(): got = lax.all_to_all(send, ('calib', 'peak'), 0, 0, tiled=True)  11.5 us
    unnamed x22, local copies, waits for them, and re-layouts  6.16 us
    ppermute x1, starting transfers between devices, body(): left = lax.ppermute(edge_score[:, :mrows], 'peak', fwd)  5 us
    ppermute x1, waiting for transfers between devices, body(): right = lax.ppermute(edge_score[:, mrows:], 'peak', bwd)  3.63 us
  transfers between devices with their start and end apart: 3, of which 2 were waited for; matrix products, arithmetic and copies ran while one was open for 8% of the time, Pallas kernels for 0%

profile of v13, /device:TPU:1, one launch (start us, length us, event | category | flops | bytes accessed | tf_op | source)
XLA Modules:
  0.0 114.5 jit_solution(8803480606814721581)
XLA Ops:
  0.6 0.8 copy.25
  1.4 0.7 reshape.181.refs_1_
  2.1 13.6 %shard_map.77 = bf16[32,4,2,16,256]{4,3,2,1,0:T(8,128)(2,1)} custom-call(s32[32]{0:T(128)} %refs_0_.1, s32[224]{0:T(256)} %reshape.181.refs_1_, s32[2,32,16,1024]{3,2,1,0:T(8,128)} %refs_2_.1, f32[3,32,16,1024]{3,2,1,0:T(8,128)} %refs_3_.1, bf16[3,32,16,1024]{3,2,1,0:T(8,128)(2,1)} %refs_4_.1, s32[32,16,1024]{2,1,0:T(8,128)} %refs_5_.1), custom_call_target="tpu_custom_call" | custom-call | tf_op jit(solution)/shard_map/pallas_call | solution.py:131
  15.7 11.5 %all-to-all-start = ((bf16[128,2,16,256]{3,2,1,0:T(8,128)(2,1)}), bf16[128,2,16,256]{3,2,1,0:T(8,128)(2,1)S(1)}, u32[]{:S(2)}, u32[]{:S(2)}) async-start(bf16[128,2,16,256]{3,2,1,0:T(8,128)(2,1)} %bitcast.26), calls=%async_computation | async-start | bytes 4194304 | tf_op jit(solution)/shard_map/all_to_all | solution.py:359
  27.5 0.1 broadcast_add_fusion.1
  27.6 1.6 %convert_reduce_fusion.1.refs_4_ = s32[512,256]{1,0:T(8,128)S(1)} fusion(s32[512,256]{1,0:T(8,128)S(1)} %broadcast_add_fusion.1, s32[31]{0:T(128)S(1)} %multiply_multiply_fusion), kind=kLoop, calls=%fused_computation.5 | loop fusion | flops 12058624 | bytes 1048700 | tf_op jit(solution)/shard_map/reduce_sum | solution.py:34
  29.3 0.3 copy.35
  29.6 0.3 slice_reduce_fusion.1
  30.0 1.1 constant_dynamic-slice_fusion
  31.1 0.1 broadcast_add_fusion
  31.3 1.7 %convert_reduce_fusion = s32[32,16,256]{2,1,0:T(8,128)S(1)} fusion(s32[32,16,256]{2,1,0:T(8,128)S(1)} %broadcast_add_fusion, s32[31]{0:T(128)S(1)} %multiply_multiply_fusion), kind=kLoop, calls=%fused_computation.4 | loop fusion | flops 12058624 | bytes 1048700 | tf_op jit(solution)/shard_map/reduce_sum | solution.py:34
  33.0 2.5 %select_reduce_fusion = s32[32]{0:T(128)S(1)} fusion(s32[32,16,256]{2,1,0:T(8,128)S(1)} %constant_dynamic-slice_fusion, s32[32,16,256]{2,1,0:T(8,128)S(1)} %convert_reduce_fusion), kind=kLoop, calls=%fused_computation | loop fusion | flops 12582880 | bytes 1048704 | tf_op jit(solution)/shard_map/reduce_sum | solution.py:229
  35.4 21.9 %all-to-all-done = bf16[128,2,16,256]{3,2,1,0:T(8,128)(2,1)S(1)} async-done(((bf16[128,2,16,256]{3,2,1,0:T(8,128)(2,1)}), bf16[128,2,16,256]{3,2,1,0:T(8,128)(2,1)S(1)}, u32[]{:S(2)}, u32[]{:S(2)}) %all-to-all-start) | async-done | bytes 2097184 | tf_op jit(solution)/shard_map/all_to_all | solution.py:359
  57.3 1.3 %copy-done.3 = bf16[128,2,16,256]{3,2,1,0:T(8,128)(2,1)} copy-done((bf16[128,2,16,256]{3,2,1,0:T(8,128)(2,1)}, bf16[128,2,16,256]{3,2,1,0:T(8,128)(2,1)S(1)}, u32[]{:S(2)}) %copy-start.3) | copy-done | bytes 2097176
  58.6 1.8 %copy.26 = bf16[4,2,32,16,256]{4,3,2,1,0:T(8,128)(2,1)S(1)} copy(bf16[4,2,32,16,256]{4,3,1,0,2:T(8,128)(2,1)} %bitcast.25) | data formatting | bytes 4194304 | tf_op jit(solution)/shard_map/transpose | solution.py:361
  60.4 2.3 %reshape_reshape.3 = bf16[8,131072]{1,0:T(8,128)(2,1)} reshape(bf16[4,2,32,16,256]{4,3,2,1,0:T(8,128)(2,1)S(1)} %copy.26) | data formatting | bytes 4194304 | tf_op jit(solution)/shard_map/reshape;reshape | solution.py:371
  62.7 2.4 %reduce-precision_convert_fusion = (bf16[8,131072]{1,0:T(8,128)(2,1)S(1)}, bf16[8,131072]{1,0:T(8,128)(2,1)S(1)}) fusion(bf16[8,131072]{1,0:T(8,128)(2,1)} %reshape_reshape.3), kind=kLoop, calls=%fused_computation.13 | loop fusion | flops 6291456 | bytes 6291456 | tf_op jit(solution)/shard_map/convert_element_type | solution.py:375
  65.1 3.2 %fusion = f32[24,32]{1,0:T(8,128)S(1)} fusion(s32[131072]{0:T(1024)S(1)} %bitcast.27, bf16[8,131072]{1,0:T(8,128)(2,1)S(1)} %get-tuple-element.31, bf16[8,131072]{1,0:T(8,128)(2,1)S(1)} %get-tuple-element.30, bf16[8,131072]{1,0:T(8,128)(2,1)S(1)} %copy-done.2), kind=kOutput, calls=%fused_computation.3 | convolution fusion | flops 224395264 | bytes 6818816 | tf_op jit(solution)/shard_map/fp,kp->fk/dot_general | solution.py:378
  68.4 0.7 fusion.13.refs_0_
  69.1 12.4 %shard_map.78 = f32[8,128]{1,0:T(8,128)} custom-call(f32[8,128]{1,0:T(8,128)} %fusion.13.refs_0_), custom_call_target="tpu_custom_call" | custom-call | tf_op jit(solution)/shard_map/pallas_call | solution.py:323
  81.5 0.8 slice_bitcast_fusion
  82.2 0.8 add_sqrt_fusion
  83.1 1.8 %fusion.19 = (bf16[8,512,1]{2,1,0:T(8,128)(2,1)}, bf16[8,512,1]{2,1,0:T(8,128)(2,1)}) fusion(bf16[8,512,256]{2,1,0:T(8,128)(2,1)S(1)} %bitcast.22), kind=kLoop, calls=%fused_computation.56 | loop fusion | bytes 32768 | tf_op jit(solution)/shard_map/slice | solution.py:397
  84.9 1.6 %copy.34 = bf16[8,512,1]{1,0,2:T(8,128)(2,1)S(1)} copy(bf16[8,512,1]{2,1,0:T(8,128)(2,1)} %get-tuple-element.29) | data formatting | bytes 16384
  86.5 1.6 %copy.33 = bf16[8,512,1]{1,0,2:T(8,128)(2,1)S(1)} copy(bf16[8,512,1]{2,1,0:T(8,128)(2,1)} %get-tuple-element.28) | data formatting | bytes 16384
  88.1 0.2 fusion.8
  88.3 5.0 %collective-permute-start = (f32[8,512]{1,0:T(8,128)S(1)}, f32[8,512]{1,0:T(8,128)S(1)}, u32[]{:S(2)}, u32[]{:S(2)}) collective-permute-start(f32[8,512]{1,0:T(8,128)S(1)} %get-tuple-element.33), channel_id=1, source_target_pairs={{0,1},{1,2},{2,3},{4,5},{5,6},{6,7},{8,9},{9,10},{10,11},{12,13},{... | collective-permute-start | bytes 49160 | tf_op jit(solution)/shard_map/ppermute | solution.py:408
  93.3 2.1 %collective-permute-start.1 = (f32[8,512]{1,0:T(8,128)S(1)}, f32[8,512]{1,0:T(8,128)S(1)}, u32[]{:S(2)}, u32[]{:S(2)}) collective-permute-start(f32[8,512]{1,0:T(8,128)S(1)} %get-tuple-element.32), channel_id=1, source_target_pairs={{1,0},{2,1},{3,2},{5,4},{6,5},{7,6},{9,8},{10,9},{11,10},{13,12},{... | collective-permute-start | bytes 49160 | tf_op jit(solution)/shard_map/ppermute | solution.py:409
  95.5 0.8 reduce_min.9
  96.3 3.6 %collective-permute-done.1.refs_6_ = f32[8,512]{1,0:T(8,128)S(1)} collective-permute-done((f32[8,512]{1,0:T(8,128)S(1)}, f32[8,512]{1,0:T(8,128)S(1)}, u32[]{:S(2)}, u32[]{:S(2)}) %collective-permute-start.1) | collective-permute-done | bytes 16416 | tf_op jit(solution)/shard_map/ppermute | solution.py:409
  99.9 0.6 copy-done.7
  100.5 14.0 %shard_map.79 = (bf16[8,512,256]{2,1,0:T(8,128)(2,1)}, bf16[8,512,256]{2,1,0:T(8,128)(2,1)}) custom-call(s32[1]{0:T(128)} %bitcast.refs_0_, f32[8,32]{1,0:T(8,128)} %copy-done.5, f32[8,32]{1,0:T(8,128)} %copy-done.4, bf16[8,512,256]{2,1,0:T(8,128)(2,1)} %bitcast.23, s32[512,256]{1,0:T(8,128)} %copy-done.1, f32[8,512]{1,0:T(8,128)} %copy-done.6, ...), custom_call_target="tpu_custom_call" | custom-call | tf_op jit(solution)/shard_map/pallas_call | solution.py:197
  (32 shorter events, 0.4 us)
Async XLA Ops:
  15.7 11.5 %copy-start.8 = (s32[32]{0:T(128)S(1)}, s32[32]{0:T(128)}, u32[]{:S(2)}) copy-start(s32[32]{0:T(128)} %refs_0_.1) | copy-start | bytes 388
  15.7 41.6 %all-to-all-start = ((bf16[128,2,16,256]{3,2,1,0:T(8,128)(2,1)}), bf16[128,2,16,256]{3,2,1,0:T(8,128)(2,1)S(1)}, u32[]{:S(2)}, u32[]{:S(2)}) async-start(bf16[128,2,16,256]{3,2,1,0:T(8,128)(2,1)} %bitcast.26), calls=%async_computation | async-start | bytes 4194304 | tf_op jit(solution)/shard_map/all_to_all | solution.py:359
  29.3 66.2 %copy-start.1 = (s32[512,256]{1,0:T(8,128)}, s32[512,256]{1,0:T(8,128)S(1)}, u32[]{:S(2)}) copy-start(s32[512,256]{1,0:T(8,128)S(1)} %convert_reduce_fusion.1.refs_4_) | copy-start | bytes 1572868
  57.3 1.3 %copy-start.3 = (bf16[128,2,16,256]{3,2,1,0:T(8,128)(2,1)}, bf16[128,2,16,256]{3,2,1,0:T(8,128)(2,1)S(1)}, u32[]{:S(2)}) copy-start(bf16[128,2,16,256]{3,2,1,0:T(8,128)(2,1)S(1)} %all-to-all-done) | copy-start | bytes 6291460
  60.4 22.7 %copy-start = (bf16[4,2,32,16,256]{4,3,2,1,0:T(8,128)(2,1)}, bf16[4,2,32,16,256]{4,3,2,1,0:T(8,128)(2,1)S(1)}, u32[]{:S(2)}) copy-start(bf16[4,2,32,16,256]{4,3,2,1,0:T(8,128)(2,1)S(1)} %copy.26) | copy-start | bytes 6291460
  62.7 2.4 %copy-start.2 = (bf16[8,131072]{1,0:T(8,128)(2,1)S(1)}, bf16[8,131072]{1,0:T(8,128)(2,1)}, u32[]{:S(2)}) copy-start(bf16[8,131072]{1,0:T(8,128)(2,1)} %reshape_reshape.3) | copy-start | bytes 6291460
  83.1 16.8 %copy-start.4 = (f32[8,32]{1,0:T(8,128)}, f32[8,32]{1,0:T(8,128)S(1)}, u32[]{:S(2)}) copy-start(f32[8,32]{1,0:T(8,128)S(1)} %get-tuple-element.36.refs_2_) | copy-start | bytes 3076
  83.1 16.8 %copy-start.5 = (f32[8,32]{1,0:T(8,128)}, f32[8,32]{1,0:T(8,128)S(1)}, u32[]{:S(2)}) copy-start(f32[8,32]{1,0:T(8,128)S(1)} %get-tuple-element.37.refs_1_) | copy-start | bytes 3076
  88.3 7.9 %collective-permute-start = (f32[8,512]{1,0:T(8,128)S(1)}, f32[8,512]{1,0:T(8,128)S(1)}, u32[]{:S(2)}, u32[]{:S(2)}) collective-permute-start(f32[8,512]{1,0:T(8,128)S(1)} %get-tuple-element.33), channel_id=1, source_target_pairs={{0,1},{1,2},{2,3},{4,5},{5,6},{6,7},{8,9},{9,10},{10,11},{12,13},{... | collective-permute-start | bytes 49160 | tf_op jit(solution)/shard_map/ppermute | solution.py:408
  93.3 6.6 %collective-permute-start.1 = (f32[8,512]{1,0:T(8,128)S(1)}, f32[8,512]{1,0:T(8,128)S(1)}, u32[]{:S(2)}, u32[]{:S(2)}) collective-permute-start(f32[8,512]{1,0:T(8,128)S(1)} %get-tuple-element.32), channel_id=1, source_target_pairs={{1,0},{2,1},{3,2},{5,4},{6,5},{7,6},{9,8},{10,9},{11,10},{13,12},{... | collective-permute-start | bytes 49160 | tf_op jit(solution)/shard_map/ppermute | solution.py:409
  96.3 3.6 %copy-start.6 = (f32[8,512]{1,0:T(8,128)}, f32[8,512]{1,0:T(8,128)S(1)}, u32[]{:S(2)}) copy-start(f32[8,512]{1,0:T(8,128)S(1)} %collective-permute-done.refs_5_) | copy-start | bytes 49156
  99.9 0.6 copy-start.7

commit v14 on v13

--- a/solution.py
+++ b/solution.py
@@ -367,15 +367,15 @@
     dx_two = 2 * xpos + 1 - SLOT_C * COLS
     cycle = cycle_index(dy_two[:, None] * dy_two[:, None] + dx_two[None, :] * dx_two[None, :])
     levels = jnp.arange(CYCLES, dtype=jnp.int32)
-    hits = (cycle.reshape(1, -1) == levels[:, None]).astype(jnp.bfloat16)
-    pixels = frame.reshape(frames_all, -1)
+    hits = (cycle[None] == levels[:, None, None]).astype(jnp.bfloat16)
+    pixels = frame
     values = pixels.astype(jnp.float32)
     square = values * values
     square_top = lax.reduce_precision(square, exponent_bits=8, mantissa_bits=7)
     square_hi = square_top.astype(jnp.bfloat16)
     square_lo = (square - square_top).astype(jnp.bfloat16)
     stacked = jnp.concatenate([pixels, square_hi, square_lo], axis=0)
-    sums = jnp.einsum("fp,kp->fk", stacked, hits, preferred_element_type=jnp.float32)
+    sums = jnp.einsum("frc,krc->fk", stacked, hits, preferred_element_type=jnp.float32)
     first = sums[:frames_all]
     second = sums[frames_all : 2 * frames_all] + sums[2 * frames_all :]
     lanes = 128

time: 115 us -> 111 us (0.965)
  local copies, waits for them, and re-layouts: 15 us -> 10.8 us
    unnamed x22 -> x19, local copies, waits for them, and re-layouts: 6.16 us -> 2.71 us
    reshape x0 -> x1, local copies, waits for them, and re-layouts: none -> 3.15 us  [body(): jnp.transpose(got, (1, 2, 0, 3, 4)).reshape(frames_all, mrows, width_here)]
    another operation x2 -> x1, local copies, waits for them, and re-layouts: 2.27 us -> 0.01 us  [the longest x1 2.27 us: body(): pixels = frame.reshape(frames_all, -1)]
    slice x1 -> x0, local copies, waits for them, and re-layouts: 1.84 us -> none  [body(): frame[:, :, width_here - 1]]
where the time goes in v14:
time: 111 us; the launch traced here: 110 us
  Pallas kernels  40 us (36%)
  waiting for transfers between devices  25.6 us (23%)
  starting transfers between devices  18.6 us (17%)
  other arithmetic  11.1 us (10%)
  local copies, waits for them, and re-layouts  10.8 us (10%)
  matrix products  3.45 us (3%)
    all_to_all x1, waiting for transfers between devices, body(): got = lax.all_to_all(send, ('calib', 'peak'), 0, 0, tiled=True)  21.9 us
    pallas_call x1, Pallas kernels, score_outputs(): pl.pallas_call(lambda *refs: score_kernel(n_peak, levels, per, *refs), gr...  14 us
    pallas_call x1, Pallas kernels, calibrate_send(): pl.pallas_call(lambda *refs: calibrate_kernel(group, *refs), grid_spec=gr...  13.6 us
    pallas_call x1, Pallas kernels, gather_sum(): pl.pallas_call(lambda *refs: gather_sum_kernel(n_calib, n_peak, *refs), o...  12.4 us
    all_to_all x1, starting transfers between devices, body(): got = lax.all_to_all(send, ('calib', 'peak'), 0, 0, tiled=True)  11.5 us
    ppermute x1, starting transfers between devices, body(): left = lax.ppermute(edge_score[:, :mrows], 'peak', fwd)  5 us
    ppermute x1, waiting for transfers between devices, body(): right = lax.ppermute(edge_score[:, mrows:], 'peak', bwd)  3.63 us
    reduce_sum x2, other arithmetic, cycle_index(): return jnp.sum((dist[..., None] >= lows).astype(jnp.int32), axis=-1)  3.34 us
  transfers between devices with their start and end apart: 3, of which 2 were waited for; matrix products, arithmetic and copies ran while one was open for 8% of the time, Pallas kernels for 0%

profile of v14, /device:TPU:1, one launch (start us, length us, event | category | flops | bytes accessed | tf_op | source)
XLA Modules:
  0.0 110.5 jit_solution(16743822612592818773)
XLA Ops:
  0.6 0.8 copy.30
  1.4 0.7 reshape.180.refs_1_
  2.1 13.6 %shard_map.77 = bf16[32,4,2,16,256]{4,3,2,1,0:T(8,128)(2,1)} custom-call(s32[32]{0:T(128)} %refs_0_.1, s32[224]{0:T(256)} %reshape.180.refs_1_, s32[2,32,16,1024]{3,2,1,0:T(8,128)} %refs_2_.1, f32[3,32,16,1024]{3,2,1,0:T(8,128)} %refs_3_.1, bf16[3,32,16,1024]{3,2,1,0:T(8,128)(2,1)} %refs_4_.1, s32[32,16,1024]{2,1,0:T(8,128)} %refs_5_.1), custom_call_target="tpu_custom_call" | custom-call | tf_op jit(solution)/shard_map/pallas_call | solution.py:131
  15.7 11.5 %all-to-all-start = ((bf16[128,2,16,256]{3,2,1,0:T(8,128)(2,1)}), bf16[128,2,16,256]{3,2,1,0:T(8,128)(2,1)S(1)}, u32[]{:S(2)}, u32[]{:S(2)}) async-start(bf16[128,2,16,256]{3,2,1,0:T(8,128)(2,1)} %bitcast.25), calls=%async_computation | async-start | bytes 4194304 | tf_op jit(solution)/shard_map/all_to_all | solution.py:359
  27.3 0.1 add_multiply_fusion.1
  27.4 0.1 copy.35
  27.5 0.1 broadcast_add_fusion.1
  27.6 1.6 %convert_reduce_fusion.1.refs_4_ = s32[512,256]{1,0:T(8,128)S(1)} fusion(s32[512,256]{1,0:T(8,128)S(1)} %broadcast_add_fusion.1, s32[31]{0:T(128)S(1)} %multiply_multiply_fusion), kind=kLoop, calls=%fused_computation.5 | loop fusion | flops 12058624 | bytes 1048700 | tf_op jit(solution)/shard_map/reduce_sum | solution.py:34
  29.3 0.2 copy.34
  29.6 0.3 slice_reduce_fusion.1
  29.9 1.1 constant_dynamic-slice_fusion
  31.0 0.1 add_multiply_fusion
  31.1 0.1 broadcast_add_fusion
  31.2 1.7 %convert_reduce_fusion = s32[32,16,256]{2,1,0:T(8,128)S(1)} fusion(s32[32,16,256]{2,1,0:T(8,128)S(1)} %broadcast_add_fusion, s32[31]{0:T(128)S(1)} %multiply_multiply_fusion), kind=kLoop, calls=%fused_computation.4 | loop fusion | flops 12058624 | bytes 1048700 | tf_op jit(solution)/shard_map/reduce_sum | solution.py:34
  32.9 2.5 %select_reduce_fusion = s32[32]{0:T(128)S(1)} fusion(s32[32,16,256]{2,1,0:T(8,128)S(1)} %constant_dynamic-slice_fusion, s32[32,16,256]{2,1,0:T(8,128)S(1)} %convert_reduce_fusion), kind=kLoop, calls=%fused_computation | loop fusion | flops 12582880 | bytes 1048704 | tf_op jit(solution)/shard_map/reduce_sum | solution.py:229
  35.4 21.9 %all-to-all-done = bf16[128,2,16,256]{3,2,1,0:T(8,128)(2,1)S(1)} async-done(((bf16[128,2,16,256]{3,2,1,0:T(8,128)(2,1)}), bf16[128,2,16,256]{3,2,1,0:T(8,128)(2,1)S(1)}, u32[]{:S(2)}, u32[]{:S(2)}) %all-to-all-start) | async-done | bytes 2097184 | tf_op jit(solution)/shard_map/all_to_all | solution.py:359
  57.3 1.3 %copy-done.3 = bf16[128,2,16,256]{3,2,1,0:T(8,128)(2,1)} copy-done((bf16[128,2,16,256]{3,2,1,0:T(8,128)(2,1)}, bf16[128,2,16,256]{3,2,1,0:T(8,128)(2,1)S(1)}, u32[]{:S(2)}) %copy-start.3) | copy-done | bytes 2097176
  58.6 1.8 %copy.31 = bf16[4,2,32,16,256]{4,3,2,1,0:T(8,128)(2,1)S(1)} copy(bf16[4,2,32,16,256]{4,3,1,0,2:T(8,128)(2,1)} %bitcast.24) | data formatting | bytes 4194304 | tf_op jit(solution)/shard_map/transpose | solution.py:361
  60.4 3.2 %copy.33 = bf16[8,512,256]{1,0,2:T(8,128)(2,1)} copy(bf16[8,512,256]{2,1,0:T(8,128)(2,1)S(1)} %bitcast.22) | data formatting | bytes 4194304 | tf_op jit(solution)/shard_map/reshape | solution.py:361
  63.6 2.5 %reduce-precision_convert_fusion = (bf16[8,512,256]{1,0,2:T(8,128)(2,1)S(1)}, bf16[8,512,256]{1,0,2:T(8,128)(2,1)S(1)}) fusion(bf16[8,512,256]{1,0,2:T(8,128)(2,1)} %copy.33), kind=kLoop, calls=%fused_computation.13 | loop fusion | flops 6291456 | bytes 6291456 | tf_op jit(solution)/shard_map/convert_element_type | solution.py:375
  66.1 3.3 %fusion.8 = f32[24,32]{1,0:T(8,128)S(1)} fusion(s32[512,256]{0,1:T(8,128)S(1)} %copy.34, bf16[8,512,256]{1,0,2:T(8,128)(2,1)S(1)} %get-tuple-element.31, bf16[8,512,256]{1,0,2:T(8,128)(2,1)S(1)} %get-tuple-element.30, bf16[8,512,256]{1,0,2:T(8,128)(2,1)S(1)} %copy-done.2), kind=kOutput, calls=%fused_computation.16 | convolution fusion | flops 224395264 | bytes 6818816 | tf_op jit(solution)/shard_map/frc,krc->fk/dot_general | solution.py:378
  69.4 0.7 fusion.16.refs_0_
  70.1 12.4 %shard_map.78 = f32[8,128]{1,0:T(8,128)} custom-call(f32[8,128]{1,0:T(8,128)} %fusion.16.refs_0_), custom_call_target="tpu_custom_call" | custom-call | tf_op jit(solution)/shard_map/pallas_call | solution.py:323
  82.5 0.8 slice_bitcast_fusion.2
  83.2 0.8 add_sqrt_fusion
  84.1 0.2 fusion.11
  84.3 5.0 %collective-permute-start = (f32[8,512]{1,0:T(8,128)S(1)}, f32[8,512]{1,0:T(8,128)S(1)}, u32[]{:S(2)}, u32[]{:S(2)}) collective-permute-start(f32[8,512]{1,0:T(8,128)S(1)} %get-tuple-element.33), channel_id=1, source_target_pairs={{0,1},{1,2},{2,3},{4,5},{5,6},{6,7},{8,9},{9,10},{10,11},{12,13},{... | collective-permute-start | bytes 49160 | tf_op jit(solution)/shard_map/ppermute | solution.py:408
  89.3 2.1 %collective-permute-start.1 = (f32[8,512]{1,0:T(8,128)S(1)}, f32[8,512]{1,0:T(8,128)S(1)}, u32[]{:S(2)}, u32[]{:S(2)}) collective-permute-start(f32[8,512]{1,0:T(8,128)S(1)} %get-tuple-element.32), channel_id=1, source_target_pairs={{1,0},{2,1},{3,2},{5,4},{6,5},{7,6},{9,8},{10,9},{11,10},{13,12},{... | collective-permute-start | bytes 49160 | tf_op jit(solution)/shard_map/ppermute | solution.py:409
  91.5 0.8 reduce_min.9
  92.2 3.6 %collective-permute-done.1.refs_6_ = f32[8,512]{1,0:T(8,128)S(1)} collective-permute-done((f32[8,512]{1,0:T(8,128)S(1)}, f32[8,512]{1,0:T(8,128)S(1)}, u32[]{:S(2)}, u32[]{:S(2)}) %collective-permute-start.1) | collective-permute-done | bytes 16416 | tf_op jit(solution)/shard_map/ppermute | solution.py:409
  95.9 0.6 copy-done.7
  96.5 14.0 %shard_map.79 = (bf16[8,512,256]{2,1,0:T(8,128)(2,1)}, bf16[8,512,256]{2,1,0:T(8,128)(2,1)}) custom-call(s32[1]{0:T(128)} %bitcast.refs_0_, f32[8,32]{1,0:T(8,128)} %copy-done.5, f32[8,32]{1,0:T(8,128)} %copy-done.4, bf16[8,512,256]{2,1,0:T(8,128)(2,1)} %bitcast.23, s32[512,256]{1,0:T(8,128)} %copy-done.1, f32[8,512]{1,0:T(8,128)} %copy-done.6, ...), custom_call_target="tpu_custom_call" | custom-call | tf_op jit(solution)/shard_map/pallas_call | solution.py:197
  (30 shorter events, 0.2 us)
Async XLA Ops:
  15.7 11.5 %copy-start.8 = (s32[32]{0:T(128)S(1)}, s32[32]{0:T(128)}, u32[]{:S(2)}) copy-start(s32[32]{0:T(128)} %refs_0_.1) | copy-start | bytes 388
  15.7 41.6 %all-to-all-start = ((bf16[128,2,16,256]{3,2,1,0:T(8,128)(2,1)}), bf16[128,2,16,256]{3,2,1,0:T(8,128)(2,1)S(1)}, u32[]{:S(2)}, u32[]{:S(2)}) async-start(bf16[128,2,16,256]{3,2,1,0:T(8,128)(2,1)} %bitcast.25), calls=%async_computation | async-start | bytes 4194304 | tf_op jit(solution)/shard_map/all_to_all | solution.py:359
  29.3 62.2 %copy-start.1 = (s32[512,256]{1,0:T(8,128)}, s32[512,256]{1,0:T(8,128)S(1)}, u32[]{:S(2)}) copy-start(s32[512,256]{1,0:T(8,128)S(1)} %convert_reduce_fusion.1.refs_4_) | copy-start | bytes 1572868
  57.3 1.3 %copy-start.3 = (bf16[128,2,16,256]{3,2,1,0:T(8,128)(2,1)}, bf16[128,2,16,256]{3,2,1,0:T(8,128)(2,1)S(1)}, u32[]{:S(2)}) copy-start(bf16[128,2,16,256]{3,2,1,0:T(8,128)(2,1)S(1)} %all-to-all-done) | copy-start | bytes 6291460
  60.4 5.6 %copy-start = (bf16[4,2,32,16,256]{4,3,2,1,0:T(8,128)(2,1)}, bf16[4,2,32,16,256]{4,3,2,1,0:T(8,128)(2,1)S(1)}, u32[]{:S(2)}) copy-start(bf16[4,2,32,16,256]{4,3,2,1,0:T(8,128)(2,1)S(1)} %copy.31) | copy-start | bytes 6291460
  63.6 2.5 %copy-start.2 = (bf16[8,512,256]{1,0,2:T(8,128)(2,1)S(1)}, bf16[8,512,256]{1,0,2:T(8,128)(2,1)}, u32[]{:S(2)}) copy-start(bf16[8,512,256]{1,0,2:T(8,128)(2,1)} %copy.33) | copy-start | bytes 6291460
  84.1 11.8 %copy-start.4 = (f32[8,32]{1,0:T(8,128)}, f32[8,32]{1,0:T(8,128)S(1)}, u32[]{:S(2)}) copy-start(f32[8,32]{1,0:T(8,128)S(1)} %get-tuple-element.36.refs_2_) | copy-start | bytes 3076
  84.1 11.8 %copy-start.5 = (f32[8,32]{1,0:T(8,128)}, f32[8,32]{1,0:T(8,128)S(1)}, u32[]{:S(2)}) copy-start(f32[8,32]{1,0:T(8,128)S(1)} %get-tuple-element.37.refs_1_) | copy-start | bytes 3076
  84.3 7.9 %collective-permute-start = (f32[8,512]{1,0:T(8,128)S(1)}, f32[8,512]{1,0:T(8,128)S(1)}, u32[]{:S(2)}, u32[]{:S(2)}) collective-permute-start(f32[8,512]{1,0:T(8,128)S(1)} %get-tuple-element.33), channel_id=1, source_target_pairs={{0,1},{1,2},{2,3},{4,5},{5,6},{6,7},{8,9},{9,10},{10,11},{12,13},{... | collective-permute-start | bytes 49160 | tf_op jit(solution)/shard_map/ppermute | solution.py:408
  89.3 6.6 %collective-permute-start.1 = (f32[8,512]{1,0:T(8,128)S(1)}, f32[8,512]{1,0:T(8,128)S(1)}, u32[]{:S(2)}, u32[]{:S(2)}) collective-permute-start(f32[8,512]{1,0:T(8,128)S(1)} %get-tuple-element.32), channel_id=1, source_target_pairs={{1,0},{2,1},{3,2},{5,4},{6,5},{7,6},{9,8},{10,9},{11,10},{13,12},{... | collective-permute-start | bytes 49160 | tf_op jit(solution)/shard_map/ppermute | solution.py:409
  92.2 3.6 %copy-start.6 = (f32[8,512]{1,0:T(8,128)}, f32[8,512]{1,0:T(8,128)S(1)}, u32[]{:S(2)}) copy-start(f32[8,512]{1,0:T(8,128)S(1)} %collective-permute-done.refs_5_) | copy-start | bytes 49156
  95.9 0.6 copy-start.7

commit v15 on v14

--- a/solution.py
+++ b/solution.py
@@ -180,12 +180,11 @@
         bent_ref[inner] = total.astype(bent_ref.dtype)
 
 
-def score_outputs(frame, cycle, cycle_average, cycle_rms, left, right, n_peak):
+def score_outputs(frame, cycle, low, cycle_average, cycle_rms, left, right, n_peak):
     frames, rows, cols = frame.shape
     span = (rows * rows + cols * cols) ** 0.5
     levels = min(CYCLES, int(span // CYCLE_W) + 2)
     per = 2 if frames % 2 == 0 else 1
-    low = jnp.min(cycle).reshape(1)
     block = pl.BlockSpec((per, rows, cols), lambda f, *_: (f, 0, 0))
     edge = pl.BlockSpec((frames, rows), lambda f, *_: (0, 0))
     grid_spec = pltpu.PrefetchScalarGridSpec(
@@ -317,13 +316,15 @@
     o_ref[...] = lax.fori_loop(0, n_calib, add_far, jnp.zeros(x_ref.shape, x_ref.dtype))
 
 
-def gather_sum(x):
+def gather_sum(x, *after):
     n_calib = lax.axis_size("calib")
     n_peak = lax.axis_size("peak")
+    held = len(after)
     return pl.pallas_call(
-        lambda *refs: gather_sum_kernel(n_calib, n_peak, *refs),
+        lambda x_ref, *refs: gather_sum_kernel(n_calib, n_peak, x_ref, *refs[held:]),
         out_shape=jax.ShapeDtypeStruct(x.shape, x.dtype),
-        in_specs=[pl.BlockSpec(memory_space=pltpu.VMEM)],
+        in_specs=[pl.BlockSpec(memory_space=pltpu.VMEM)]
+        + [pl.BlockSpec(memory_space=pl.ANY)] * held,
         out_specs=pl.BlockSpec(memory_space=pltpu.VMEM),
         scratch_shapes=[
             pltpu.VMEM((n_peak,) + x.shape, x.dtype),
@@ -335,7 +336,7 @@
             pltpu.SemaphoreType.DMA,
         ],
         compiler_params=pltpu.CompilerParams(collective_id=0, has_side_effects=True),
-    )(x)
+    )(x, *after)
 
 
 def cycle_stats(first, second, present_flag):
@@ -388,7 +389,8 @@
         ],
         axis=1,
     )
-    summed = gather_sum(packed)
+    low = jnp.min(cycle).reshape(1)
+    summed = gather_sum(packed, low)
     first = summed[:, :CYCLES]
     second = summed[:, CYCLES : 2 * CYCLES]
     present_flag = summed[0, 2 * CYCLES : 3 * CYCLES]
@@ -407,7 +409,7 @@
     bwd = [(i + 1, i) for i in range(n_peak - 1)]
     left = lax.ppermute(edge_score[:, :mrows], "peak", fwd)
     right = lax.ppermute(edge_score[:, mrows:], "peak", bwd)
-    snr, bent = score_outputs(frame, cycle, cycle_average, cycle_rms, left, right, n_peak)
+    snr, bent = score_outputs(frame, cycle, low, cycle_average, cycle_rms, left, right, n_peak)
     return (snr[:, None], bent[:, None])
 
 

time: 111 us -> 112 us (level)
  no operation moved by 1% of the time
where the time goes in v15:
time: 112 us; the launch traced here: 111 us
  Pallas kernels  40.7 us (36%)
  waiting for transfers between devices  25.6 us (23%)
  starting transfers between devices  18.6 us (17%)
  other arithmetic  11.1 us (10%)
  local copies, waits for them, and re-layouts  10.8 us (10%)
  matrix products  3.45 us (3%)
    all_to_all x1, waiting for transfers between devices, body(): got = lax.all_to_all(send, ('calib', 'peak'), 0, 0, tiled=True)  21.2 us
    pallas_call x1, Pallas kernels, score_outputs(): pl.pallas_call(lambda *refs: score_kernel(n_peak, levels, per, *refs), gr...  14 us
    pallas_call x1, Pallas kernels, calibrate_send(): pl.pallas_call(lambda *refs: calibrate_kernel(group, *refs), grid_spec=gr...  13.6 us
    pallas_call x1, Pallas kernels, gather_sum(): pl.pallas_call(lambda x_ref, *refs: gather_sum_kernel(n_calib, n_peak, x_...  13 us
    all_to_all x1, starting transfers between devices, body(): got = lax.all_to_all(send, ('calib', 'peak'), 0, 0, tiled=True)  11.5 us
    ppermute x1, starting transfers between devices, body(): left = lax.ppermute(edge_score[:, :mrows], 'peak', fwd)  5 us
    ppermute x1, waiting for transfers between devices, body(): right = lax.ppermute(edge_score[:, mrows:], 'peak', bwd)  4.39 us
    reduce_sum x2, other arithmetic, cycle_index(): return jnp.sum((dist[..., None] >= lows).astype(jnp.int32), axis=-1)  3.34 us
  transfers between devices with their start and end apart: 3, of which 2 were waited for; matrix products, arithmetic and copies ran while one was open for 8% of the time, Pallas kernels for 0%

profile of v15, /device:TPU:1, one launch (start us, length us, event | category | flops | bytes accessed | tf_op | source)
XLA Modules:
  0.0 111.1 jit_solution(14718678021296452695)
XLA Ops:
  0.6 0.8 copy.30
  1.4 0.7 reshape.180.refs_1_
  2.1 13.6 %shard_map.77 = bf16[32,4,2,16,256]{4,3,2,1,0:T(8,128)(2,1)} custom-call(s32[32]{0:T(128)} %refs_0_.1, s32[224]{0:T(256)} %reshape.180.refs_1_, s32[2,32,16,1024]{3,2,1,0:T(8,128)} %refs_2_.1, f32[3,32,16,1024]{3,2,1,0:T(8,128)} %refs_3_.1, bf16[3,32,16,1024]{3,2,1,0:T(8,128)(2,1)} %refs_4_.1, s32[32,16,1024]{2,1,0:T(8,128)} %refs_5_.1), custom_call_target="tpu_custom_call" | custom-call | tf_op jit(solution)/shard_map/pallas_call | solution.py:131
  15.7 11.5 %all-to-all-start = ((bf16[128,2,16,256]{3,2,1,0:T(8,128)(2,1)}), bf16[128,2,16,256]{3,2,1,0:T(8,128)(2,1)S(1)}, u32[]{:S(2)}, u32[]{:S(2)}) async-start(bf16[128,2,16,256]{3,2,1,0:T(8,128)(2,1)} %bitcast.25), calls=%async_computation | async-start | bytes 4194304 | tf_op jit(solution)/shard_map/all_to_all | solution.py:360
  27.3 0.1 broadcast_add_fusion.1
  27.5 1.6 %convert_reduce_fusion.1.refs_4_ = s32[512,256]{1,0:T(8,128)S(1)} fusion(s32[512,256]{1,0:T(8,128)S(1)} %broadcast_add_fusion.1, s32[31]{0:T(128)S(1)} %multiply_multiply_fusion), kind=kLoop, calls=%fused_computation.5 | loop fusion | flops 12058624 | bytes 1048700 | tf_op jit(solution)/shard_map/reduce_sum | solution.py:34
  29.1 0.2 copy.34
  29.3 0.8 reduce_min.9
  30.1 0.1 add_multiply_fusion.1
  30.2 0.1 copy.35
  30.2 0.1 pad.12.clone
  30.3 0.3 slice_reduce_fusion.1
  30.6 1.1 constant_dynamic-slice_fusion
  31.8 0.1 broadcast_add_fusion
  31.9 1.7 %convert_reduce_fusion = s32[32,16,256]{2,1,0:T(8,128)S(1)} fusion(s32[32,16,256]{2,1,0:T(8,128)S(1)} %broadcast_add_fusion, s32[31]{0:T(128)S(1)} %multiply_multiply_fusion), kind=kLoop, calls=%fused_computation.4 | loop fusion | flops 12058624 | bytes 1048700 | tf_op jit(solution)/shard_map/reduce_sum | solution.py:34
  33.7 2.5 %select_reduce_fusion = s32[32]{0:T(128)S(1)} fusion(s32[32,16,256]{2,1,0:T(8,128)S(1)} %constant_dynamic-slice_fusion, s32[32,16,256]{2,1,0:T(8,128)S(1)} %convert_reduce_fusion), kind=kLoop, calls=%fused_computation | loop fusion | flops 12582880 | bytes 1048704 | tf_op jit(solution)/shard_map/reduce_sum | solution.py:228
  36.1 21.2 %all-to-all-done = bf16[128,2,16,256]{3,2,1,0:T(8,128)(2,1)S(1)} async-done(((bf16[128,2,16,256]{3,2,1,0:T(8,128)(2,1)}), bf16[128,2,16,256]{3,2,1,0:T(8,128)(2,1)S(1)}, u32[]{:S(2)}, u32[]{:S(2)}) %all-to-all-start) | async-done | bytes 2097184 | tf_op jit(solution)/shard_map/all_to_all | solution.py:360
  57.3 1.3 %copy-done.3 = bf16[128,2,16,256]{3,2,1,0:T(8,128)(2,1)} copy-done((bf16[128,2,16,256]{3,2,1,0:T(8,128)(2,1)}, bf16[128,2,16,256]{3,2,1,0:T(8,128)(2,1)S(1)}, u32[]{:S(2)}) %copy-start.3) | copy-done | bytes 2097176
  58.6 1.8 %copy.31 = bf16[4,2,32,16,256]{4,3,2,1,0:T(8,128)(2,1)S(1)} copy(bf16[4,2,32,16,256]{4,3,1,0,2:T(8,128)(2,1)} %bitcast.24) | data formatting | bytes 4194304 | tf_op jit(solution)/shard_map/transpose | solution.py:362
  60.4 3.1 %copy.33 = bf16[8,512,256]{1,0,2:T(8,128)(2,1)} copy(bf16[8,512,256]{2,1,0:T(8,128)(2,1)S(1)} %bitcast.22) | data formatting | bytes 4194304 | tf_op jit(solution)/shard_map/reshape | solution.py:362
  63.6 2.5 %reduce-precision_convert_fusion = (bf16[8,512,256]{1,0,2:T(8,128)(2,1)S(1)}, bf16[8,512,256]{1,0,2:T(8,128)(2,1)S(1)}) fusion(bf16[8,512,256]{1,0,2:T(8,128)(2,1)} %copy.33), kind=kLoop, calls=%fused_computation.13 | loop fusion | flops 6291456 | bytes 6291456 | tf_op jit(solution)/shard_map/convert_element_type | solution.py:376
  66.1 3.3 %fusion.8 = f32[24,32]{1,0:T(8,128)S(1)} fusion(s32[512,256]{0,1:T(8,128)S(1)} %copy.34, bf16[8,512,256]{1,0,2:T(8,128)(2,1)S(1)} %get-tuple-element.31, bf16[8,512,256]{1,0,2:T(8,128)(2,1)S(1)} %get-tuple-element.30, bf16[8,512,256]{1,0,2:T(8,128)(2,1)S(1)} %copy-done.2), kind=kOutput, calls=%fused_computation.16 | convolution fusion | flops 224395264 | bytes 6818816 | tf_op jit(solution)/shard_map/frc,krc->fk/dot_general | solution.py:379
  69.4 0.7 fusion.16.x_ref
  70.1 13.0 %shard_map.78 = f32[8,128]{1,0:T(8,128)} custom-call(f32[8,128]{1,0:T(8,128)} %fusion.16.x_ref, s32[1]{0:T(128)} %bitcast.refs_0_), custom_call_target="tpu_custom_call" | custom-call | tf_op jit(solution)/shard_map/pallas_call | solution.py:323
  83.1 0.8 slice_bitcast_fusion.2
  83.9 0.8 add_sqrt_fusion
  84.7 0.2 fusion.11
  84.9 5.0 %collective-permute-start = (f32[8,512]{1,0:T(8,128)S(1)}, f32[8,512]{1,0:T(8,128)S(1)}, u32[]{:S(2)}, u32[]{:S(2)}) collective-permute-start(f32[8,512]{1,0:T(8,128)S(1)} %get-tuple-element.33), channel_id=1, source_target_pairs={{0,1},{1,2},{2,3},{4,5},{5,6},{6,7},{8,9},{9,10},{10,11},{12,13},{... | collective-permute-start | bytes 49160 | tf_op jit(solution)/shard_map/ppermute | solution.py:410
  89.9 2.1 %collective-permute-start.1 = (f32[8,512]{1,0:T(8,128)S(1)}, f32[8,512]{1,0:T(8,128)S(1)}, u32[]{:S(2)}, u32[]{:S(2)}) collective-permute-start(f32[8,512]{1,0:T(8,128)S(1)} %get-tuple-element.32), channel_id=1, source_target_pairs={{1,0},{2,1},{3,2},{5,4},{6,5},{7,6},{9,8},{10,9},{11,10},{13,12},{... | collective-permute-start | bytes 49160 | tf_op jit(solution)/shard_map/ppermute | solution.py:411
  92.1 4.4 %collective-permute-done.1.refs_6_ = f32[8,512]{1,0:T(8,128)S(1)} collective-permute-done((f32[8,512]{1,0:T(8,128)S(1)}, f32[8,512]{1,0:T(8,128)S(1)}, u32[]{:S(2)}, u32[]{:S(2)}) %collective-permute-start.1) | collective-permute-done | bytes 16416 | tf_op jit(solution)/shard_map/ppermute | solution.py:411
  96.5 0.6 copy-done.7
  97.1 14.0 %shard_map.79 = (bf16[8,512,256]{2,1,0:T(8,128)(2,1)}, bf16[8,512,256]{2,1,0:T(8,128)(2,1)}) custom-call(s32[1]{0:T(128)} %bitcast.refs_0_, f32[8,32]{1,0:T(8,128)} %copy-done.5, f32[8,32]{1,0:T(8,128)} %copy-done.4, bf16[8,512,256]{2,1,0:T(8,128)(2,1)} %bitcast.23, s32[512,256]{1,0:T(8,128)} %copy-done.1, f32[8,512]{1,0:T(8,128)} %copy-done.6, ...), custom_call_target="tpu_custom_call" | custom-call | tf_op jit(solution)/shard_map/pallas_call | solution.py:196
  (30 shorter events, 0.2 us)
Async XLA Ops:
  15.7 11.5 %copy-start.8 = (s32[32]{0:T(128)S(1)}, s32[32]{0:T(128)}, u32[]{:S(2)}) copy-start(s32[32]{0:T(128)} %refs_0_.1) | copy-start | bytes 388
  15.7 41.6 %all-to-all-start = ((bf16[128,2,16,256]{3,2,1,0:T(8,128)(2,1)}), bf16[128,2,16,256]{3,2,1,0:T(8,128)(2,1)S(1)}, u32[]{:S(2)}, u32[]{:S(2)}) async-start(bf16[128,2,16,256]{3,2,1,0:T(8,128)(2,1)} %bitcast.25), calls=%async_computation | async-start | bytes 4194304 | tf_op jit(solution)/shard_map/all_to_all | solution.py:360
  29.1 31.3 %copy-start.1 = (s32[512,256]{1,0:T(8,128)}, s32[512,256]{1,0:T(8,128)S(1)}, u32[]{:S(2)}) copy-start(s32[512,256]{1,0:T(8,128)S(1)} %convert_reduce_fusion.1.refs_4_) | copy-start | bytes 1572868
  57.3 1.3 %copy-start.3 = (bf16[128,2,16,256]{3,2,1,0:T(8,128)(2,1)}, bf16[128,2,16,256]{3,2,1,0:T(8,128)(2,1)S(1)}, u32[]{:S(2)}) copy-start(bf16[128,2,16,256]{3,2,1,0:T(8,128)(2,1)S(1)} %all-to-all-done) | copy-start | bytes 6291460
  60.4 5.6 %copy-start = (bf16[4,2,32,16,256]{4,3,2,1,0:T(8,128)(2,1)}, bf16[4,2,32,16,256]{4,3,2,1,0:T(8,128)(2,1)S(1)}, u32[]{:S(2)}) copy-start(bf16[4,2,32,16,256]{4,3,2,1,0:T(8,128)(2,1)S(1)} %copy.31) | copy-start | bytes 6291460
  63.6 2.5 %copy-start.2 = (bf16[8,512,256]{1,0,2:T(8,128)(2,1)S(1)}, bf16[8,512,256]{1,0,2:T(8,128)(2,1)}, u32[]{:S(2)}) copy-start(bf16[8,512,256]{1,0,2:T(8,128)(2,1)} %copy.33) | copy-start | bytes 6291460
  84.7 11.8 %copy-start.4 = (f32[8,32]{1,0:T(8,128)}, f32[8,32]{1,0:T(8,128)S(1)}, u32[]{:S(2)}) copy-start(f32[8,32]{1,0:T(8,128)S(1)} %get-tuple-element.36.refs_2_) | copy-start | bytes 3076
  84.7 11.8 %copy-start.5 = (f32[8,32]{1,0:T(8,128)}, f32[8,32]{1,0:T(8,128)S(1)}, u32[]{:S(2)}) copy-start(f32[8,32]{1,0:T(8,128)S(1)} %get-tuple-element.37.refs_1_) | copy-start | bytes 3076
  84.9 7.2 %collective-permute-start = (f32[8,512]{1,0:T(8,128)S(1)}, f32[8,512]{1,0:T(8,128)S(1)}, u32[]{:S(2)}, u32[]{:S(2)}) collective-permute-start(f32[8,512]{1,0:T(8,128)S(1)} %get-tuple-element.33), channel_id=1, source_target_pairs={{0,1},{1,2},{2,3},{4,5},{5,6},{6,7},{8,9},{9,10},{10,11},{12,13},{... | collective-permute-start | bytes 49160 | tf_op jit(solution)/shard_map/ppermute | solution.py:410
  89.9 6.6 %collective-permute-start.1 = (f32[8,512]{1,0:T(8,128)S(1)}, f32[8,512]{1,0:T(8,128)S(1)}, u32[]{:S(2)}, u32[]{:S(2)}) collective-permute-start(f32[8,512]{1,0:T(8,128)S(1)} %get-tuple-element.32), channel_id=1, source_target_pairs={{1,0},{2,1},{3,2},{5,4},{6,5},{7,6},{9,8},{10,9},{11,10},{13,12},{... | collective-permute-start | bytes 49160 | tf_op jit(solution)/shard_map/ppermute | solution.py:411
  92.1 4.4 %copy-start.6 = (f32[8,512]{1,0:T(8,128)}, f32[8,512]{1,0:T(8,128)S(1)}, u32[]{:S(2)}) copy-start(f32[8,512]{1,0:T(8,128)S(1)} %collective-permute-done.refs_5_) | copy-start | bytes 49156
  96.5 0.6 copy-start.7

commit v16 on v14

--- a/solution.py
+++ b/solution.py
@@ -154,6 +154,8 @@
     for j in range(levels):
         level = jnp.minimum(low_ref[0] + j, tops)
         hits.append((level, cycle == level))
+    left_all = jnp.transpose(left_ref[...])
+    right_all = jnp.transpose(right_ref[...])
     for inner in range(per):
         frame_pos = pl.program_id(0) * per + inner
         values = frame_ref[inner].astype(jnp.float32)
@@ -164,8 +166,6 @@
             pixel_rms = jnp.where(hit, rms_ref[frame_pos, level], pixel_rms)
         score = (values - pixel_mean) / pixel_rms
         pick = lax.broadcasted_iota(jnp.int32, (rows, left_ref.shape[0]), 1) == frame_pos
-        left_all = jnp.transpose(left_ref[...])
-        right_all = jnp.transpose(right_ref[...])
         left_col = jnp.sum(jnp.where(pick, left_all, 0.0), axis=1, keepdims=True)
         right_col = jnp.sum(jnp.where(pick, right_all, 0.0), axis=1, keepdims=True)
         left_col = jnp.where(peak_pos == 0, 0.0, left_col)

time: 111 us -> 111 us (level)
  no operation moved by 1% of the time
where the time goes in v16:
time: 111 us; the launch traced here: 110 us
  Pallas kernels  39.6 us (36%)
  waiting for transfers between devices  25.6 us (23%)
  starting transfers between devices  18.6 us (17%)
  other arithmetic  11.1 us (10%)
  local copies, waits for them, and re-layouts  10.8 us (10%)
  matrix products  3.45 us (3%)
    all_to_all x1, waiting for transfers between devices, body(): got = lax.all_to_all(send, ('calib', 'peak'), 0, 0, tiled=True)  21.9 us
    pallas_call x1, Pallas kernels, calibrate_send(): pl.pallas_call(lambda *refs: calibrate_kernel(group, *refs), grid_spec=gr...  13.6 us
    pallas_call x1, Pallas kernels, score_outputs(): pl.pallas_call(lambda *refs: score_kernel(n_peak, levels, per, *refs), gr...  13.6 us
    pallas_call x1, Pallas kernels, gather_sum(): pl.pallas_call(lambda *refs: gather_sum_kernel(n_calib, n_peak, *refs), o...  12.4 us
    all_to_all x1, starting transfers between devices, body(): got = lax.all_to_all(send, ('calib', 'peak'), 0, 0, tiled=True)  11.5 us
    ppermute x1, starting transfers between devices, body(): left = lax.ppermute(edge_score[:, :mrows], 'peak', fwd)  5 us
    ppermute x1, waiting for transfers between devices, body(): right = lax.ppermute(edge_score[:, mrows:], 'peak', bwd)  3.63 us
    reduce_sum x2, other arithmetic, cycle_index(): return jnp.sum((dist[..., None] >= lows).astype(jnp.int32), axis=-1)  3.34 us
  transfers between devices with their start and end apart: 3, of which 2 were waited for; matrix products, arithmetic and copies ran while one was open for 8% of the time, Pallas kernels for 0%

profile of v16, /device:TPU:1, one launch (start us, length us, event | category | flops | bytes accessed | tf_op | source)
XLA Modules:
  0.0 110.0 jit_solution(1020656681355314930)
XLA Ops:
  0.6 0.8 copy.30
  1.4 0.7 reshape.180.refs_1_
  2.1 13.6 %shard_map.77 = bf16[32,4,2,16,256]{4,3,2,1,0:T(8,128)(2,1)} custom-call(s32[32]{0:T(128)} %refs_0_.1, s32[224]{0:T(256)} %reshape.180.refs_1_, s32[2,32,16,1024]{3,2,1,0:T(8,128)} %refs_2_.1, f32[3,32,16,1024]{3,2,1,0:T(8,128)} %refs_3_.1, bf16[3,32,16,1024]{3,2,1,0:T(8,128)(2,1)} %refs_4_.1, s32[32,16,1024]{2,1,0:T(8,128)} %refs_5_.1), custom_call_target="tpu_custom_call" | custom-call | tf_op jit(solution)/shard_map/pallas_call | solution.py:131
  15.7 11.5 %all-to-all-start = ((bf16[128,2,16,256]{3,2,1,0:T(8,128)(2,1)}), bf16[128,2,16,256]{3,2,1,0:T(8,128)(2,1)S(1)}, u32[]{:S(2)}, u32[]{:S(2)}) async-start(bf16[128,2,16,256]{3,2,1,0:T(8,128)(2,1)} %bitcast.25), calls=%async_computation | async-start | bytes 4194304 | tf_op jit(solution)/shard_map/all_to_all | solution.py:359
  27.3 0.1 add_multiply_fusion.1
  27.4 0.1 copy.35
  27.5 0.1 broadcast_add_fusion.1
  27.6 1.6 %convert_reduce_fusion.1.refs_4_ = s32[512,256]{1,0:T(8,128)S(1)} fusion(s32[512,256]{1,0:T(8,128)S(1)} %broadcast_add_fusion.1, s32[31]{0:T(128)S(1)} %multiply_multiply_fusion), kind=kLoop, calls=%fused_computation.5 | loop fusion | flops 12058624 | bytes 1048700 | tf_op jit(solution)/shard_map/reduce_sum | solution.py:34
  29.3 0.2 copy.34
  29.6 0.3 slice_reduce_fusion.1
  29.9 1.1 constant_dynamic-slice_fusion
  31.0 0.1 add_multiply_fusion
  31.1 0.1 broadcast_add_fusion
  31.2 1.7 %convert_reduce_fusion = s32[32,16,256]{2,1,0:T(8,128)S(1)} fusion(s32[32,16,256]{2,1,0:T(8,128)S(1)} %broadcast_add_fusion, s32[31]{0:T(128)S(1)} %multiply_multiply_fusion), kind=kLoop, calls=%fused_computation.4 | loop fusion | flops 12058624 | bytes 1048700 | tf_op jit(solution)/shard_map/reduce_sum | solution.py:34
  32.9 2.5 %select_reduce_fusion = s32[32]{0:T(128)S(1)} fusion(s32[32,16,256]{2,1,0:T(8,128)S(1)} %constant_dynamic-slice_fusion, s32[32,16,256]{2,1,0:T(8,128)S(1)} %convert_reduce_fusion), kind=kLoop, calls=%fused_computation | loop fusion | flops 12582880 | bytes 1048704 | tf_op jit(solution)/shard_map/reduce_sum | solution.py:229
  35.4 21.9 %all-to-all-done = bf16[128,2,16,256]{3,2,1,0:T(8,128)(2,1)S(1)} async-done(((bf16[128,2,16,256]{3,2,1,0:T(8,128)(2,1)}), bf16[128,2,16,256]{3,2,1,0:T(8,128)(2,1)S(1)}, u32[]{:S(2)}, u32[]{:S(2)}) %all-to-all-start) | async-done | bytes 2097184 | tf_op jit(solution)/shard_map/all_to_all | solution.py:359
  57.3 1.3 %copy-done.3 = bf16[128,2,16,256]{3,2,1,0:T(8,128)(2,1)} copy-done((bf16[128,2,16,256]{3,2,1,0:T(8,128)(2,1)}, bf16[128,2,16,256]{3,2,1,0:T(8,128)(2,1)S(1)}, u32[]{:S(2)}) %copy-start.3) | copy-done | bytes 2097176
  58.6 1.8 %copy.31 = bf16[4,2,32,16,256]{4,3,2,1,0:T(8,128)(2,1)S(1)} copy(bf16[4,2,32,16,256]{4,3,1,0,2:T(8,128)(2,1)} %bitcast.24) | data formatting | bytes 4194304 | tf_op jit(solution)/shard_map/transpose | solution.py:361
  60.4 3.2 %copy.33 = bf16[8,512,256]{1,0,2:T(8,128)(2,1)} copy(bf16[8,512,256]{2,1,0:T(8,128)(2,1)S(1)} %bitcast.22) | data formatting | bytes 4194304 | tf_op jit(solution)/shard_map/reshape | solution.py:361
  63.6 2.5 %reduce-precision_convert_fusion = (bf16[8,512,256]{1,0,2:T(8,128)(2,1)S(1)}, bf16[8,512,256]{1,0,2:T(8,128)(2,1)S(1)}) fusion(bf16[8,512,256]{1,0,2:T(8,128)(2,1)} %copy.33), kind=kLoop, calls=%fused_computation.13 | loop fusion | flops 6291456 | bytes 6291456 | tf_op jit(solution)/shard_map/convert_element_type | solution.py:375
  66.1 3.3 %fusion.8 = f32[24,32]{1,0:T(8,128)S(1)} fusion(s32[512,256]{0,1:T(8,128)S(1)} %copy.34, bf16[8,512,256]{1,0,2:T(8,128)(2,1)S(1)} %get-tuple-element.31, bf16[8,512,256]{1,0,2:T(8,128)(2,1)S(1)} %get-tuple-element.30, bf16[8,512,256]{1,0,2:T(8,128)(2,1)S(1)} %copy-done.2), kind=kOutput, calls=%fused_computation.16 | convolution fusion | flops 224395264 | bytes 6818816 | tf_op jit(solution)/shard_map/frc,krc->fk/dot_general | solution.py:378
  69.4 0.7 fusion.16.refs_0_
  70.1 12.4 %shard_map.78 = f32[8,128]{1,0:T(8,128)} custom-call(f32[8,128]{1,0:T(8,128)} %fusion.16.refs_0_), custom_call_target="tpu_custom_call" | custom-call | tf_op jit(solution)/shard_map/pallas_call | solution.py:323
  82.5 0.8 slice_bitcast_fusion.2
  83.2 0.8 add_sqrt_fusion
  84.1 0.2 fusion.11
  84.3 5.0 %collective-permute-start = (f32[8,512]{1,0:T(8,128)S(1)}, f32[8,512]{1,0:T(8,128)S(1)}, u32[]{:S(2)}, u32[]{:S(2)}) collective-permute-start(f32[8,512]{1,0:T(8,128)S(1)} %get-tuple-element.33), channel_id=1, source_target_pairs={{0,1},{1,2},{2,3},{4,5},{5,6},{6,7},{8,9},{9,10},{10,11},{12,13},{... | collective-permute-start | bytes 49160 | tf_op jit(solution)/shard_map/ppermute | solution.py:408
  89.3 2.1 %collective-permute-start.1 = (f32[8,512]{1,0:T(8,128)S(1)}, f32[8,512]{1,0:T(8,128)S(1)}, u32[]{:S(2)}, u32[]{:S(2)}) collective-permute-start(f32[8,512]{1,0:T(8,128)S(1)} %get-tuple-element.32), channel_id=1, source_target_pairs={{1,0},{2,1},{3,2},{5,4},{6,5},{7,6},{9,8},{10,9},{11,10},{13,12},{... | collective-permute-start | bytes 49160 | tf_op jit(solution)/shard_map/ppermute | solution.py:409
  91.5 0.8 reduce_min.9
  92.2 3.6 %collective-permute-done.1.refs_6_ = f32[8,512]{1,0:T(8,128)S(1)} collective-permute-done((f32[8,512]{1,0:T(8,128)S(1)}, f32[8,512]{1,0:T(8,128)S(1)}, u32[]{:S(2)}, u32[]{:S(2)}) %collective-permute-start.1) | collective-permute-done | bytes 16416 | tf_op jit(solution)/shard_map/ppermute | solution.py:409
  95.9 0.6 copy-done.7
  96.5 13.6 %shard_map.79 = (bf16[8,512,256]{2,1,0:T(8,128)(2,1)}, bf16[8,512,256]{2,1,0:T(8,128)(2,1)}) custom-call(s32[1]{0:T(128)} %bitcast.refs_0_, f32[8,32]{1,0:T(8,128)} %copy-done.5, f32[8,32]{1,0:T(8,128)} %copy-done.4, bf16[8,512,256]{2,1,0:T(8,128)(2,1)} %bitcast.23, s32[512,256]{1,0:T(8,128)} %copy-done.1, f32[8,512]{1,0:T(8,128)} %copy-done.6, ...), custom_call_target="tpu_custom_call" | custom-call | tf_op jit(solution)/shard_map/pallas_call | solution.py:197
  (30 shorter events, 0.2 us)
Async XLA Ops:
  15.7 11.5 %copy-start.8 = (s32[32]{0:T(128)S(1)}, s32[32]{0:T(128)}, u32[]{:S(2)}) copy-start(s32[32]{0:T(128)} %refs_0_.1) | copy-start | bytes 388
  15.7 41.6 %all-to-all-start = ((bf16[128,2,16,256]{3,2,1,0:T(8,128)(2,1)}), bf16[128,2,16,256]{3,2,1,0:T(8,128)(2,1)S(1)}, u32[]{:S(2)}, u32[]{:S(2)}) async-start(bf16[128,2,16,256]{3,2,1,0:T(8,128)(2,1)} %bitcast.25), calls=%async_computation | async-start | bytes 4194304 | tf_op jit(solution)/shard_map/all_to_all | solution.py:359
  29.3 62.2 %copy-start.1 = (s32[512,256]{1,0:T(8,128)}, s32[512,256]{1,0:T(8,128)S(1)}, u32[]{:S(2)}) copy-start(s32[512,256]{1,0:T(8,128)S(1)} %convert_reduce_fusion.1.refs_4_) | copy-start | bytes 1572868
  57.3 1.3 %copy-start.3 = (bf16[128,2,16,256]{3,2,1,0:T(8,128)(2,1)}, bf16[128,2,16,256]{3,2,1,0:T(8,128)(2,1)S(1)}, u32[]{:S(2)}) copy-start(bf16[128,2,16,256]{3,2,1,0:T(8,128)(2,1)S(1)} %all-to-all-done) | copy-start | bytes 6291460
  60.4 5.6 %copy-start = (bf16[4,2,32,16,256]{4,3,2,1,0:T(8,128)(2,1)}, bf16[4,2,32,16,256]{4,3,2,1,0:T(8,128)(2,1)S(1)}, u32[]{:S(2)}) copy-start(bf16[4,2,32,16,256]{4,3,2,1,0:T(8,128)(2,1)S(1)} %copy.31) | copy-start | bytes 6291460
  63.6 2.5 %copy-start.2 = (bf16[8,512,256]{1,0,2:T(8,128)(2,1)S(1)}, bf16[8,512,256]{1,0,2:T(8,128)(2,1)}, u32[]{:S(2)}) copy-start(bf16[8,512,256]{1,0,2:T(8,128)(2,1)} %copy.33) | copy-start | bytes 6291460
  84.1 11.8 %copy-start.4 = (f32[8,32]{1,0:T(8,128)}, f32[8,32]{1,0:T(8,128)S(1)}, u32[]{:S(2)}) copy-start(f32[8,32]{1,0:T(8,128)S(1)} %get-tuple-element.36.refs_2_) | copy-start | bytes 3076
  84.1 11.8 %copy-start.5 = (f32[8,32]{1,0:T(8,128)}, f32[8,32]{1,0:T(8,128)S(1)}, u32[]{:S(2)}) copy-start(f32[8,32]{1,0:T(8,128)S(1)} %get-tuple-element.37.refs_1_) | copy-start | bytes 3076
  84.3 7.9 %collective-permute-start = (f32[8,512]{1,0:T(8,128)S(1)}, f32[8,512]{1,0:T(8,128)S(1)}, u32[]{:S(2)}, u32[]{:S(2)}) collective-permute-start(f32[8,512]{1,0:T(8,128)S(1)} %get-tuple-element.33), channel_id=1, source_target_pairs={{0,1},{1,2},{2,3},{4,5},{5,6},{6,7},{8,9},{9,10},{10,11},{12,13},{... | collective-permute-start | bytes 49160 | tf_op jit(solution)/shard_map/ppermute | solution.py:408
  89.3 6.6 %collective-permute-start.1 = (f32[8,512]{1,0:T(8,128)S(1)}, f32[8,512]{1,0:T(8,128)S(1)}, u32[]{:S(2)}, u32[]{:S(2)}) collective-permute-start(f32[8,512]{1,0:T(8,128)S(1)} %get-tuple-element.32), channel_id=1, source_target_pairs={{1,0},{2,1},{3,2},{5,4},{6,5},{7,6},{9,8},{10,9},{11,10},{13,12},{... | collective-permute-start | bytes 49160 | tf_op jit(solution)/shard_map/ppermute | solution.py:409
  92.2 3.6 %copy-start.6 = (f32[8,512]{1,0:T(8,128)}, f32[8,512]{1,0:T(8,128)S(1)}, u32[]{:S(2)}) copy-start(f32[8,512]{1,0:T(8,128)S(1)} %collective-permute-done.refs_5_) | copy-start | bytes 49156
  95.9 0.6 copy-start.7

commit v17 on v14

--- a/solution.py
+++ b/solution.py
@@ -184,7 +184,7 @@
     frames, rows, cols = frame.shape
     span = (rows * rows + cols * cols) ** 0.5
     levels = min(CYCLES, int(span // CYCLE_W) + 2)
-    per = 2 if frames % 2 == 0 else 1
+    per = 4 if frames % 4 == 0 else 1
     low = jnp.min(cycle).reshape(1)
     block = pl.BlockSpec((per, rows, cols), lambda f, *_: (f, 0, 0))
     edge = pl.BlockSpec((frames, rows), lambda f, *_: (0, 0))

time: 111 us -> 112 us (level)
  no operation moved by 1% of the time
where the time goes in v17:
time: 112 us; the launch traced here: 111 us
  Pallas kernels  40.6 us (36%)
  waiting for transfers between devices  25.6 us (23%)
  starting transfers between devices  18.6 us (17%)
  other arithmetic  11.1 us (10%)
  local copies, waits for them, and re-layouts  10.8 us (10%)
  matrix products  3.45 us (3%)
    all_to_all x1, waiting for transfers between devices, body(): got = lax.all_to_all(send, ('calib', 'peak'), 0, 0, tiled=True)  21.9 us
    pallas_call x1, Pallas kernels, score_outputs(): pl.pallas_call(lambda *refs: score_kernel(n_peak, levels, per, *refs), gr...  14.6 us
    pallas_call x1, Pallas kernels, calibrate_send(): pl.pallas_call(lambda *refs: calibrate_kernel(group, *refs), grid_spec=gr...  13.6 us
    pallas_call x1, Pallas kernels, gather_sum(): pl.pallas_call(lambda *refs: gather_sum_kernel(n_calib, n_peak, *refs), o...  12.4 us
    all_to_all x1, starting transfers between devices, body(): got = lax.all_to_all(send, ('calib', 'peak'), 0, 0, tiled=True)  11.5 us
    ppermute x1, starting transfers between devices, body(): left = lax.ppermute(edge_score[:, :mrows], 'peak', fwd)  5 us
    ppermute x1, waiting for transfers between devices, body(): right = lax.ppermute(edge_score[:, mrows:], 'peak', bwd)  3.63 us
    reduce_sum x2, other arithmetic, cycle_index(): return jnp.sum((dist[..., None] >= lows).astype(jnp.int32), axis=-1)  3.34 us
  transfers between devices with their start and end apart: 3, of which 2 were waited for; matrix products, arithmetic and copies ran while one was open for 8% of the time, Pallas kernels for 0%

profile of v17, /device:TPU:1, one launch (start us, length us, event | category | flops | bytes accessed | tf_op | source)
XLA Modules:
  0.0 111.1 jit_solution(1034996985382988505)
XLA Ops:
  0.6 0.8 copy.30
  1.4 0.7 reshape.180.refs_1_
  2.1 13.6 %shard_map.77 = bf16[32,4,2,16,256]{4,3,2,1,0:T(8,128)(2,1)} custom-call(s32[32]{0:T(128)} %refs_0_.1, s32[224]{0:T(256)} %reshape.180.refs_1_, s32[2,32,16,1024]{3,2,1,0:T(8,128)} %refs_2_.1, f32[3,32,16,1024]{3,2,1,0:T(8,128)} %refs_3_.1, bf16[3,32,16,1024]{3,2,1,0:T(8,128)(2,1)} %refs_4_.1, s32[32,16,1024]{2,1,0:T(8,128)} %refs_5_.1), custom_call_target="tpu_custom_call" | custom-call | tf_op jit(solution)/shard_map/pallas_call | solution.py:131
  15.7 11.5 %all-to-all-start = ((bf16[128,2,16,256]{3,2,1,0:T(8,128)(2,1)}), bf16[128,2,16,256]{3,2,1,0:T(8,128)(2,1)S(1)}, u32[]{:S(2)}, u32[]{:S(2)}) async-start(bf16[128,2,16,256]{3,2,1,0:T(8,128)(2,1)} %bitcast.25), calls=%async_computation | async-start | bytes 4194304 | tf_op jit(solution)/shard_map/all_to_all | solution.py:359
  27.3 0.1 add_multiply_fusion.1
  27.4 0.1 copy.35
  27.5 0.1 broadcast_add_fusion.1
  27.6 1.6 %convert_reduce_fusion.1.refs_4_ = s32[512,256]{1,0:T(8,128)S(1)} fusion(s32[512,256]{1,0:T(8,128)S(1)} %broadcast_add_fusion.1, s32[31]{0:T(128)S(1)} %multiply_multiply_fusion), kind=kLoop, calls=%fused_computation.5 | loop fusion | flops 12058624 | bytes 1048700 | tf_op jit(solution)/shard_map/reduce_sum | solution.py:34
  29.3 0.2 copy.34
  29.6 0.3 slice_reduce_fusion.1
  29.9 1.1 constant_dynamic-slice_fusion
  31.0 0.1 add_multiply_fusion
  31.1 0.1 broadcast_add_fusion
  31.2 1.7 %convert_reduce_fusion = s32[32,16,256]{2,1,0:T(8,128)S(1)} fusion(s32[32,16,256]{2,1,0:T(8,128)S(1)} %broadcast_add_fusion, s32[31]{0:T(128)S(1)} %multiply_multiply_fusion), kind=kLoop, calls=%fused_computation.4 | loop fusion | flops 12058624 | bytes 1048700 | tf_op jit(solution)/shard_map/reduce_sum | solution.py:34
  32.9 2.5 %select_reduce_fusion = s32[32]{0:T(128)S(1)} fusion(s32[32,16,256]{2,1,0:T(8,128)S(1)} %constant_dynamic-slice_fusion, s32[32,16,256]{2,1,0:T(8,128)S(1)} %convert_reduce_fusion), kind=kLoop, calls=%fused_computation | loop fusion | flops 12582880 | bytes 1048704 | tf_op jit(solution)/shard_map/reduce_sum | solution.py:229
  35.4 21.9 %all-to-all-done = bf16[128,2,16,256]{3,2,1,0:T(8,128)(2,1)S(1)} async-done(((bf16[128,2,16,256]{3,2,1,0:T(8,128)(2,1)}), bf16[128,2,16,256]{3,2,1,0:T(8,128)(2,1)S(1)}, u32[]{:S(2)}, u32[]{:S(2)}) %all-to-all-start) | async-done | bytes 2097184 | tf_op jit(solution)/shard_map/all_to_all | solution.py:359
  57.3 1.3 %copy-done.3 = bf16[128,2,16,256]{3,2,1,0:T(8,128)(2,1)} copy-done((bf16[128,2,16,256]{3,2,1,0:T(8,128)(2,1)}, bf16[128,2,16,256]{3,2,1,0:T(8,128)(2,1)S(1)}, u32[]{:S(2)}) %copy-start.3) | copy-done | bytes 2097176
  58.6 1.8 %copy.31 = bf16[4,2,32,16,256]{4,3,2,1,0:T(8,128)(2,1)S(1)} copy(bf16[4,2,32,16,256]{4,3,1,0,2:T(8,128)(2,1)} %bitcast.24) | data formatting | bytes 4194304 | tf_op jit(solution)/shard_map/transpose | solution.py:361
  60.4 3.2 %copy.33 = bf16[8,512,256]{1,0,2:T(8,128)(2,1)} copy(bf16[8,512,256]{2,1,0:T(8,128)(2,1)S(1)} %bitcast.22) | data formatting | bytes 4194304 | tf_op jit(solution)/shard_map/reshape | solution.py:361
  63.6 2.5 %reduce-precision_convert_fusion = (bf16[8,512,256]{1,0,2:T(8,128)(2,1)S(1)}, bf16[8,512,256]{1,0,2:T(8,128)(2,1)S(1)}) fusion(bf16[8,512,256]{1,0,2:T(8,128)(2,1)} %copy.33), kind=kLoop, calls=%fused_computation.13 | loop fusion | flops 6291456 | bytes 6291456 | tf_op jit(solution)/shard_map/convert_element_type | solution.py:375
  66.1 3.3 %fusion.8 = f32[24,32]{1,0:T(8,128)S(1)} fusion(s32[512,256]{0,1:T(8,128)S(1)} %copy.34, bf16[8,512,256]{1,0,2:T(8,128)(2,1)S(1)} %get-tuple-element.31, bf16[8,512,256]{1,0,2:T(8,128)(2,1)S(1)} %get-tuple-element.30, bf16[8,512,256]{1,0,2:T(8,128)(2,1)S(1)} %copy-done.2), kind=kOutput, calls=%fused_computation.16 | convolution fusion | flops 224395264 | bytes 6818816 | tf_op jit(solution)/shard_map/frc,krc->fk/dot_general | solution.py:378
  69.4 0.7 fusion.16.refs_0_
  70.1 12.4 %shard_map.78 = f32[8,128]{1,0:T(8,128)} custom-call(f32[8,128]{1,0:T(8,128)} %fusion.16.refs_0_), custom_call_target="tpu_custom_call" | custom-call | tf_op jit(solution)/shard_map/pallas_call | solution.py:323
  82.5 0.8 slice_bitcast_fusion.2
  83.2 0.8 add_sqrt_fusion
  84.1 0.2 fusion.11
  84.3 5.0 %collective-permute-start = (f32[8,512]{1,0:T(8,128)S(1)}, f32[8,512]{1,0:T(8,128)S(1)}, u32[]{:S(2)}, u32[]{:S(2)}) collective-permute-start(f32[8,512]{1,0:T(8,128)S(1)} %get-tuple-element.33), channel_id=1, source_target_pairs={{0,1},{1,2},{2,3},{4,5},{5,6},{6,7},{8,9},{9,10},{10,11},{12,13},{... | collective-permute-start | bytes 49160 | tf_op jit(solution)/shard_map/ppermute | solution.py:408
  89.3 2.1 %collective-permute-start.1 = (f32[8,512]{1,0:T(8,128)S(1)}, f32[8,512]{1,0:T(8,128)S(1)}, u32[]{:S(2)}, u32[]{:S(2)}) collective-permute-start(f32[8,512]{1,0:T(8,128)S(1)} %get-tuple-element.32), channel_id=1, source_target_pairs={{1,0},{2,1},{3,2},{5,4},{6,5},{7,6},{9,8},{10,9},{11,10},{13,12},{... | collective-permute-start | bytes 49160 | tf_op jit(solution)/shard_map/ppermute | solution.py:409
  91.5 0.8 reduce_min.9
  92.2 3.6 %collective-permute-done.1.refs_6_ = f32[8,512]{1,0:T(8,128)S(1)} collective-permute-done((f32[8,512]{1,0:T(8,128)S(1)}, f32[8,512]{1,0:T(8,128)S(1)}, u32[]{:S(2)}, u32[]{:S(2)}) %collective-permute-start.1) | collective-permute-done | bytes 16416 | tf_op jit(solution)/shard_map/ppermute | solution.py:409
  95.9 0.6 copy-done.7
  96.5 14.6 %shard_map.79 = (bf16[8,512,256]{2,1,0:T(8,128)(2,1)}, bf16[8,512,256]{2,1,0:T(8,128)(2,1)}) custom-call(s32[1]{0:T(128)} %bitcast.refs_0_, f32[8,32]{1,0:T(8,128)} %copy-done.5, f32[8,32]{1,0:T(8,128)} %copy-done.4, bf16[8,512,256]{2,1,0:T(8,128)(2,1)} %bitcast.23, s32[512,256]{1,0:T(8,128)} %copy-done.1, f32[8,512]{1,0:T(8,128)} %copy-done.6, ...), custom_call_target="tpu_custom_call" | custom-call | tf_op jit(solution)/shard_map/pallas_call | solution.py:197
  (30 shorter events, 0.2 us)
Async XLA Ops:
  15.7 11.5 %copy-start.8 = (s32[32]{0:T(128)S(1)}, s32[32]{0:T(128)}, u32[]{:S(2)}) copy-start(s32[32]{0:T(128)} %refs_0_.1) | copy-start | bytes 388
  15.7 41.6 %all-to-all-start = ((bf16[128,2,16,256]{3,2,1,0:T(8,128)(2,1)}), bf16[128,2,16,256]{3,2,1,0:T(8,128)(2,1)S(1)}, u32[]{:S(2)}, u32[]{:S(2)}) async-start(bf16[128,2,16,256]{3,2,1,0:T(8,128)(2,1)} %bitcast.25), calls=%async_computation | async-start | bytes 4194304 | tf_op jit(solution)/shard_map/all_to_all | solution.py:359
  29.3 62.2 %copy-start.1 = (s32[512,256]{1,0:T(8,128)}, s32[512,256]{1,0:T(8,128)S(1)}, u32[]{:S(2)}) copy-start(s32[512,256]{1,0:T(8,128)S(1)} %convert_reduce_fusion.1.refs_4_) | copy-start | bytes 1572868
  57.3 1.3 %copy-start.3 = (bf16[128,2,16,256]{3,2,1,0:T(8,128)(2,1)}, bf16[128,2,16,256]{3,2,1,0:T(8,128)(2,1)S(1)}, u32[]{:S(2)}) copy-start(bf16[128,2,16,256]{3,2,1,0:T(8,128)(2,1)S(1)} %all-to-all-done) | copy-start | bytes 6291460
  60.4 5.6 %copy-start = (bf16[4,2,32,16,256]{4,3,2,1,0:T(8,128)(2,1)}, bf16[4,2,32,16,256]{4,3,2,1,0:T(8,128)(2,1)S(1)}, u32[]{:S(2)}) copy-start(bf16[4,2,32,16,256]{4,3,2,1,0:T(8,128)(2,1)S(1)} %copy.31) | copy-start | bytes 6291460
  63.6 2.5 %copy-start.2 = (bf16[8,512,256]{1,0,2:T(8,128)(2,1)S(1)}, bf16[8,512,256]{1,0,2:T(8,128)(2,1)}, u32[]{:S(2)}) copy-start(bf16[8,512,256]{1,0,2:T(8,128)(2,1)} %copy.33) | copy-start | bytes 6291460
  84.1 11.8 %copy-start.4 = (f32[8,32]{1,0:T(8,128)}, f32[8,32]{1,0:T(8,128)S(1)}, u32[]{:S(2)}) copy-start(f32[8,32]{1,0:T(8,128)S(1)} %get-tuple-element.36.refs_2_) | copy-start | bytes 3076
  84.1 11.8 %copy-start.5 = (f32[8,32]{1,0:T(8,128)}, f32[8,32]{1,0:T(8,128)S(1)}, u32[]{:S(2)}) copy-start(f32[8,32]{1,0:T(8,128)S(1)} %get-tuple-element.37.refs_1_) | copy-start | bytes 3076
  84.3 7.9 %collective-permute-start = (f32[8,512]{1,0:T(8,128)S(1)}, f32[8,512]{1,0:T(8,128)S(1)}, u32[]{:S(2)}, u32[]{:S(2)}) collective-permute-start(f32[8,512]{1,0:T(8,128)S(1)} %get-tuple-element.33), channel_id=1, source_target_pairs={{0,1},{1,2},{2,3},{4,5},{5,6},{6,7},{8,9},{9,10},{10,11},{12,13},{... | collective-permute-start | bytes 49160 | tf_op jit(solution)/shard_map/ppermute | solution.py:408
  89.3 6.6 %collective-permute-start.1 = (f32[8,512]{1,0:T(8,128)S(1)}, f32[8,512]{1,0:T(8,128)S(1)}, u32[]{:S(2)}, u32[]{:S(2)}) collective-permute-start(f32[8,512]{1,0:T(8,128)S(1)} %get-tuple-element.32), channel_id=1, source_target_pairs={{1,0},{2,1},{3,2},{5,4},{6,5},{7,6},{9,8},{10,9},{11,10},{13,12},{... | collective-permute-start | bytes 49160 | tf_op jit(solution)/shard_map/ppermute | solution.py:409
  92.2 3.6 %copy-start.6 = (f32[8,512]{1,0:T(8,128)}, f32[8,512]{1,0:T(8,128)S(1)}, u32[]{:S(2)}) copy-start(f32[8,512]{1,0:T(8,128)S(1)} %collective-permute-done.refs_5_) | copy-start | bytes 49156
  95.9 0.6 copy-start.7

commit v18 on v14

--- a/solution.py
+++ b/solution.py
@@ -114,7 +114,7 @@
 def calibrate_send(raw, pedestal, gain, good, bounds, table, n_peak):
     frame_dev, mods, row_dev, cols = raw.shape
     width = cols // n_peak
-    group = 8
+    group = 4
     grid_spec = pltpu.PrefetchScalarGridSpec(
         num_scalar_prefetch=2,
         grid=(mods // group,),

time: 111 us -> 111 us (level)
  no operation moved by 1% of the time
where the time goes in v18:
time: 111 us
  Pallas kernels  40.4 us (36%)
  waiting for transfers between devices  25.6 us (23%)
  starting transfers between devices  18.6 us (17%)
  other arithmetic  11.1 us (10%)
  local copies, waits for them, and re-layouts  10.8 us (10%)
  matrix products  3.45 us (3%)
    all_to_all x1, waiting for transfers between devices, body(): got = lax.all_to_all(send, ('calib', 'peak'), 0, 0, tiled=True)  21.9 us
    pallas_call x1, Pallas kernels, calibrate_send(): pl.pallas_call(lambda *refs: calibrate_kernel(group, *refs), grid_spec=gr...  14 us
    pallas_call x1, Pallas kernels, score_outputs(): pl.pallas_call(lambda *refs: score_kernel(n_peak, levels, per, *refs), gr...  14 us
    pallas_call x1, Pallas kernels, gather_sum(): pl.pallas_call(lambda *refs: gather_sum_kernel(n_calib, n_peak, *refs), o...  12.4 us
    all_to_all x1, starting transfers between devices, body(): got = lax.all_to_all(send, ('calib', 'peak'), 0, 0, tiled=True)  11.5 us
    ppermute x1, starting transfers between devices, body(): left = lax.ppermute(edge_score[:, :mrows], 'peak', fwd)  5 us
    ppermute x1, waiting for transfers between devices, body(): right = lax.ppermute(edge_score[:, mrows:], 'peak', bwd)  3.67 us
    reduce_sum x2, other arithmetic, cycle_index(): return jnp.sum((dist[..., None] >= lows).astype(jnp.int32), axis=-1)  3.34 us
  transfers between devices with their start and end apart: 3, of which 2 were waited for; matrix products, arithmetic and copies ran while one was open for 8% of the time, Pallas kernels for 0%

profile of v18, /device:TPU:1, one launch (start us, length us, event | category | flops | bytes accessed | tf_op | source)
XLA Modules:
  0.0 110.8 jit_solution(10512471423734737766)
XLA Ops:
  0.6 0.8 copy.30
  1.4 0.7 reshape.180.refs_1_
  2.1 14.0 %shard_map.77 = bf16[32,4,2,16,256]{4,3,2,1,0:T(8,128)(2,1)} custom-call(s32[32]{0:T(128)} %refs_0_.1, s32[224]{0:T(256)} %reshape.180.refs_1_, s32[2,32,16,1024]{3,2,1,0:T(8,128)} %refs_2_.1, f32[3,32,16,1024]{3,2,1,0:T(8,128)} %refs_3_.1, bf16[3,32,16,1024]{3,2,1,0:T(8,128)(2,1)} %refs_4_.1, s32[32,16,1024]{2,1,0:T(8,128)} %refs_5_.1), custom_call_target="tpu_custom_call" | custom-call | tf_op jit(solution)/shard_map/pallas_call | solution.py:131
  16.1 11.5 %all-to-all-start = ((bf16[128,2,16,256]{3,2,1,0:T(8,128)(2,1)}), bf16[128,2,16,256]{3,2,1,0:T(8,128)(2,1)S(1)}, u32[]{:S(2)}, u32[]{:S(2)}) async-start(bf16[128,2,16,256]{3,2,1,0:T(8,128)(2,1)} %bitcast.25), calls=%async_computation | async-start | bytes 4194304 | tf_op jit(solution)/shard_map/all_to_all | solution.py:359
  27.7 0.1 add_multiply_fusion.1
  27.8 0.1 copy.35
  27.9 0.1 broadcast_add_fusion.1
  28.0 1.6 %convert_reduce_fusion.1.refs_4_ = s32[512,256]{1,0:T(8,128)S(1)} fusion(s32[512,256]{1,0:T(8,128)S(1)} %broadcast_add_fusion.1, s32[31]{0:T(128)S(1)} %multiply_multiply_fusion), kind=kLoop, calls=%fused_computation.5 | loop fusion | flops 12058624 | bytes 1048700 | tf_op jit(solution)/shard_map/reduce_sum | solution.py:34
  29.7 0.2 copy.34
  30.0 0.3 slice_reduce_fusion.1
  30.3 1.1 constant_dynamic-slice_fusion
  31.4 0.1 add_multiply_fusion
  31.4 0.1 broadcast_add_fusion
  31.6 1.7 %convert_reduce_fusion = s32[32,16,256]{2,1,0:T(8,128)S(1)} fusion(s32[32,16,256]{2,1,0:T(8,128)S(1)} %broadcast_add_fusion, s32[31]{0:T(128)S(1)} %multiply_multiply_fusion), kind=kLoop, calls=%fused_computation.4 | loop fusion | flops 12058624 | bytes 1048700 | tf_op jit(solution)/shard_map/reduce_sum | solution.py:34
  33.3 2.5 %select_reduce_fusion = s32[32]{0:T(128)S(1)} fusion(s32[32,16,256]{2,1,0:T(8,128)S(1)} %constant_dynamic-slice_fusion, s32[32,16,256]{2,1,0:T(8,128)S(1)} %convert_reduce_fusion), kind=kLoop, calls=%fused_computation | loop fusion | flops 12582880 | bytes 1048704 | tf_op jit(solution)/shard_map/reduce_sum | solution.py:229
  35.7 21.9 %all-to-all-done = bf16[128,2,16,256]{3,2,1,0:T(8,128)(2,1)S(1)} async-done(((bf16[128,2,16,256]{3,2,1,0:T(8,128)(2,1)}), bf16[128,2,16,256]{3,2,1,0:T(8,128)(2,1)S(1)}, u32[]{:S(2)}, u32[]{:S(2)}) %all-to-all-start) | async-done | bytes 2097184 | tf_op jit(solution)/shard_map/all_to_all | solution.py:359
  57.7 1.3 %copy-done.3 = bf16[128,2,16,256]{3,2,1,0:T(8,128)(2,1)} copy-done((bf16[128,2,16,256]{3,2,1,0:T(8,128)(2,1)}, bf16[128,2,16,256]{3,2,1,0:T(8,128)(2,1)S(1)}, u32[]{:S(2)}) %copy-start.3) | copy-done | bytes 2097176
  59.0 1.8 %copy.31 = bf16[4,2,32,16,256]{4,3,2,1,0:T(8,128)(2,1)S(1)} copy(bf16[4,2,32,16,256]{4,3,1,0,2:T(8,128)(2,1)} %bitcast.24) | data formatting | bytes 4194304 | tf_op jit(solution)/shard_map/transpose | solution.py:361
  60.8 3.2 %copy.33 = bf16[8,512,256]{1,0,2:T(8,128)(2,1)} copy(bf16[8,512,256]{2,1,0:T(8,128)(2,1)S(1)} %bitcast.22) | data formatting | bytes 4194304 | tf_op jit(solution)/shard_map/reshape | solution.py:361
  64.0 2.5 %reduce-precision_convert_fusion = (bf16[8,512,256]{1,0,2:T(8,128)(2,1)S(1)}, bf16[8,512,256]{1,0,2:T(8,128)(2,1)S(1)}) fusion(bf16[8,512,256]{1,0,2:T(8,128)(2,1)} %copy.33), kind=kLoop, calls=%fused_computation.13 | loop fusion | flops 6291456 | bytes 6291456 | tf_op jit(solution)/shard_map/convert_element_type | solution.py:375
  66.5 3.3 %fusion.8 = f32[24,32]{1,0:T(8,128)S(1)} fusion(s32[512,256]{0,1:T(8,128)S(1)} %copy.34, bf16[8,512,256]{1,0,2:T(8,128)(2,1)S(1)} %get-tuple-element.31, bf16[8,512,256]{1,0,2:T(8,128)(2,1)S(1)} %get-tuple-element.30, bf16[8,512,256]{1,0,2:T(8,128)(2,1)S(1)} %copy-done.2), kind=kOutput, calls=%fused_computation.16 | convolution fusion | flops 224395264 | bytes 6818816 | tf_op jit(solution)/shard_map/frc,krc->fk/dot_general | solution.py:378
  69.8 0.7 fusion.16.refs_0_
  70.4 12.4 %shard_map.78 = f32[8,128]{1,0:T(8,128)} custom-call(f32[8,128]{1,0:T(8,128)} %fusion.16.refs_0_), custom_call_target="tpu_custom_call" | custom-call | tf_op jit(solution)/shard_map/pallas_call | solution.py:323
  82.9 0.8 slice_bitcast_fusion.2
  83.6 0.8 add_sqrt_fusion
  84.5 0.2 fusion.11
  84.7 5.0 %collective-permute-start = (f32[8,512]{1,0:T(8,128)S(1)}, f32[8,512]{1,0:T(8,128)S(1)}, u32[]{:S(2)}, u32[]{:S(2)}) collective-permute-start(f32[8,512]{1,0:T(8,128)S(1)} %get-tuple-element.33), channel_id=1, source_target_pairs={{0,1},{1,2},{2,3},{4,5},{5,6},{6,7},{8,9},{9,10},{10,11},{12,13},{... | collective-permute-start | bytes 49160 | tf_op jit(solution)/shard_map/ppermute | solution.py:408
  89.7 2.1 %collective-permute-start.1 = (f32[8,512]{1,0:T(8,128)S(1)}, f32[8,512]{1,0:T(8,128)S(1)}, u32[]{:S(2)}, u32[]{:S(2)}) collective-permute-start(f32[8,512]{1,0:T(8,128)S(1)} %get-tuple-element.32), channel_id=1, source_target_pairs={{1,0},{2,1},{3,2},{5,4},{6,5},{7,6},{9,8},{10,9},{11,10},{13,12},{... | collective-permute-start | bytes 49160 | tf_op jit(solution)/shard_map/ppermute | solution.py:409
  91.8 0.8 reduce_min.9
  92.6 3.7 %collective-permute-done.1.refs_6_ = f32[8,512]{1,0:T(8,128)S(1)} collective-permute-done((f32[8,512]{1,0:T(8,128)S(1)}, f32[8,512]{1,0:T(8,128)S(1)}, u32[]{:S(2)}, u32[]{:S(2)}) %collective-permute-start.1) | collective-permute-done | bytes 16416 | tf_op jit(solution)/shard_map/ppermute | solution.py:409
  96.3 0.6 copy-done.7
  96.9 14.0 %shard_map.79 = (bf16[8,512,256]{2,1,0:T(8,128)(2,1)}, bf16[8,512,256]{2,1,0:T(8,128)(2,1)}) custom-call(s32[1]{0:T(128)} %bitcast.refs_0_, f32[8,32]{1,0:T(8,128)} %copy-done.5, f32[8,32]{1,0:T(8,128)} %copy-done.4, bf16[8,512,256]{2,1,0:T(8,128)(2,1)} %bitcast.23, s32[512,256]{1,0:T(8,128)} %copy-done.1, f32[8,512]{1,0:T(8,128)} %copy-done.6, ...), custom_call_target="tpu_custom_call" | custom-call | tf_op jit(solution)/shard_map/pallas_call | solution.py:197
  (30 shorter events, 0.2 us)
Async XLA Ops:
  16.1 11.5 %copy-start.8 = (s32[32]{0:T(128)S(1)}, s32[32]{0:T(128)}, u32[]{:S(2)}) copy-start(s32[32]{0:T(128)} %refs_0_.1) | copy-start | bytes 388
  16.1 41.6 %all-to-all-start = ((bf16[128,2,16,256]{3,2,1,0:T(8,128)(2,1)}), bf16[128,2,16,256]{3,2,1,0:T(8,128)(2,1)S(1)}, u32[]{:S(2)}, u32[]{:S(2)}) async-start(bf16[128,2,16,256]{3,2,1,0:T(8,128)(2,1)} %bitcast.25), calls=%async_computation | async-start | bytes 4194304 | tf_op jit(solution)/shard_map/all_to_all | solution.py:359
  29.7 62.1 %copy-start.1 = (s32[512,256]{1,0:T(8,128)}, s32[512,256]{1,0:T(8,128)S(1)}, u32[]{:S(2)}) copy-start(s32[512,256]{1,0:T(8,128)S(1)} %convert_reduce_fusion.1.refs_4_) | copy-start | bytes 1572868
  57.7 1.3 %copy-start.3 = (bf16[128,2,16,256]{3,2,1,0:T(8,128)(2,1)}, bf16[128,2,16,256]{3,2,1,0:T(8,128)(2,1)S(1)}, u32[]{:S(2)}) copy-start(bf16[128,2,16,256]{3,2,1,0:T(8,128)(2,1)S(1)} %all-to-all-done) | copy-start | bytes 6291460
  60.8 5.6 %copy-start = (bf16[4,2,32,16,256]{4,3,2,1,0:T(8,128)(2,1)}, bf16[4,2,32,16,256]{4,3,2,1,0:T(8,128)(2,1)S(1)}, u32[]{:S(2)}) copy-start(bf16[4,2,32,16,256]{4,3,2,1,0:T(8,128)(2,1)S(1)} %copy.31) | copy-start | bytes 6291460
  64.0 2.5 %copy-start.2 = (bf16[8,512,256]{1,0,2:T(8,128)(2,1)S(1)}, bf16[8,512,256]{1,0,2:T(8,128)(2,1)}, u32[]{:S(2)}) copy-start(bf16[8,512,256]{1,0,2:T(8,128)(2,1)} %copy.33) | copy-start | bytes 6291460
  84.5 11.8 %copy-start.4 = (f32[8,32]{1,0:T(8,128)}, f32[8,32]{1,0:T(8,128)S(1)}, u32[]{:S(2)}) copy-start(f32[8,32]{1,0:T(8,128)S(1)} %get-tuple-element.36.refs_2_) | copy-start | bytes 3076
  84.5 11.8 %copy-start.5 = (f32[8,32]{1,0:T(8,128)}, f32[8,32]{1,0:T(8,128)S(1)}, u32[]{:S(2)}) copy-start(f32[8,32]{1,0:T(8,128)S(1)} %get-tuple-element.37.refs_1_) | copy-start | bytes 3076
  84.7 7.9 %collective-permute-start = (f32[8,512]{1,0:T(8,128)S(1)}, f32[8,512]{1,0:T(8,128)S(1)}, u32[]{:S(2)}, u32[]{:S(2)}) collective-permute-start(f32[8,512]{1,0:T(8,128)S(1)} %get-tuple-element.33), channel_id=1, source_target_pairs={{0,1},{1,2},{2,3},{4,5},{5,6},{6,7},{8,9},{9,10},{10,11},{12,13},{... | collective-permute-start | bytes 49160 | tf_op jit(solution)/shard_map/ppermute | solution.py:408
  89.7 6.6 %collective-permute-start.1 = (f32[8,512]{1,0:T(8,128)S(1)}, f32[8,512]{1,0:T(8,128)S(1)}, u32[]{:S(2)}, u32[]{:S(2)}) collective-permute-start(f32[8,512]{1,0:T(8,128)S(1)} %get-tuple-element.32), channel_id=1, source_target_pairs={{1,0},{2,1},{3,2},{5,4},{6,5},{7,6},{9,8},{10,9},{11,10},{13,12},{... | collective-permute-start | bytes 49160 | tf_op jit(solution)/shard_map/ppermute | solution.py:409
  92.6 3.7 %copy-start.6 = (f32[8,512]{1,0:T(8,128)}, f32[8,512]{1,0:T(8,128)S(1)}, u32[]{:S(2)}) copy-start(f32[8,512]{1,0:T(8,128)S(1)} %collective-permute-done.refs_5_) | copy-start | bytes 49156
  96.2 0.6 copy-start.7
